TPU v7x, 32 devices: a whole 2x2x4 slice. The times are simulated.
32 devices in a mesh: ep: 16 (over z, x, core), es: 2 (over y).
Axes of the slice: x: 2, y: 2, z: 4, core: 2. Of those that a mesh axis runs over, the one named last changes fastest.
Arguments:
- inputs: bfloat16 [16384, 1024], P(('ep', 'es')), may hold values from -6 to 6
- grad_output: bfloat16 [16384, 1024], P(('ep', 'es')), may hold values from -6 to 6
- expert_choice: int32 [16384, 1], P(('ep', 'es')), may hold values from 0 to 15; in each aligned block of 512 rows (0 to 511, 512 to 1023, ...) at most 45 rows name the same one
- pre_gain: float32 [1024], replicated, may hold values from 0.25 to 1.75
- pre_shift: float32 [1024], replicated, may hold values from -4 to 4
- w_query: bfloat16 [1024, 1024], P('es'), may hold values from -0.1875 to 0.1875
- w_key: bfloat16 [1024, 1024], P('es'), may hold values from -0.1875 to 0.1875
- w_value: bfloat16 [1024, 1024], P('es'), may hold values from -0.1875 to 0.1875
- w_output: bfloat16 [1024, 1024], P('es'), may hold values from -3 to 3
- mid_gain: float32 [1024], replicated, may hold values from 0.25 to 1.75
- mid_shift: float32 [1024], replicated, may hold values from -4 to 4
- w_up: bfloat16 [1024, 4096], P('es'), may hold values from -0.1875 to 0.1875
- w_down: bfloat16 [4096, 1024], P('es'), may hold values from -0.09375 to 0.09375
- w_router: bfloat16 [1024, 16], replicated, may hold values from -0.3125 to 0.3125
- w_mix: bfloat16 [1024, 2], replicated, may hold values from -0.3125 to 0.3125
- expert_up: bfloat16 [16, 1024, 4096], P('ep', None, 'es'), may hold values from -0.1875 to 0.1875
- expert_down: bfloat16 [16, 4096, 1024], P('ep', 'es'), may hold values from -6 to 6
Outputs:
- output: bfloat16 [16384, 1024], P(('ep', 'es'))
- grad_inputs: float32 [16384, 1024], P(('ep', 'es'))
- grad_pre_gain: float32 [1024], P(('ep', 'es'))
- grad_pre_shift: float32 [1024], P(('ep', 'es'))
- grad_w_query: float32 [1024, 1024], P(('ep', 'es'))
- grad_w_key: float32 [1024, 1024], P(('ep', 'es'))
- grad_w_value: float32 [1024, 1024], P(('ep', 'es'))
- grad_w_output: float32 [1024, 1024], P(('ep', 'es'))
- grad_mid_gain: float32 [1024], P(('ep', 'es'))
- grad_mid_shift: float32 [1024], P(('ep', 'es'))
- grad_w_up: float32 [1024, 4096], P(('ep', 'es'))
- grad_w_down: float32 [4096, 1024], P(('ep', 'es'))
- grad_w_router: float32 [1024, 16], P(('ep', 'es'))
- grad_w_mix: float32 [1024, 2], P(('ep', 'es'))
- grad_expert_up: float32 [16, 1024, 4096], P('ep', None, 'es')
- grad_expert_down: float32 [16, 4096, 1024], P('ep', 'es')
Inputs may be any that keep to these rules, and one draw needn't show every extreme that they name: `expert_choice`: in each aligned block of 512 rows (the rows of one device) no expert is named more than 45 times; in some of these blocks an expert is named exactly 45 times.
All inputs are finite; a program needn't handle non-finite values.
Results may differ from a plain program's by a relative error of at most 0.019.
The roundings to bfloat16 on the way count: a program that leaves them out, or rounds other values in their place, can miss the bound.
Values may be sent and summed in bfloat16 or wider, within the bound.
No kernel may reach another device: no remote copies, remote signals or barrier semaphores. Data moves between devices by JAX's collectives and lax.ppermute only.
A program may use at most 320 MiB of HBM per device.

v0:
```python
import jax
import jax.numpy as jnp
from jax import lax
from jax.sharding import PartitionSpec as P

HEAD_DIM = 64


def shifted(value, axis, by):
    size = lax.axis_size(axis)
    pairs = [(i, i + by) for i in range(size) if 0 <= i + by < size]
    return lax.ppermute(value, axis, pairs)


def layer_norm(values, gain, shift):
    center = jnp.mean(values, axis=-1, keepdims=True)
    centred = values - center
    spread = jnp.mean(centred * centred, axis=-1, keepdims=True)
    return centred * lax.rsqrt(spread + 1e-05) * gain + shift


def gelu_tanh(values):
    return jax.nn.gelu(values, approximate=True)


def matmul(left, right):
    return jnp.dot(left, right, preferred_element_type=jnp.float32)


def matmul_nt(left, right):
    return lax.dot_general(
        left, right, (((1,), (1,)), ((), ())), preferred_element_type=jnp.float32
    )


def matmul_tn(left, right):
    return lax.dot_general(
        left, right, (((0,), (0,)), ((), ())), preferred_element_type=jnp.float32
    )


def body(
    inputs,
    grad_output,
    expert_choice,
    pre_gain,
    pre_shift,
    w_query,
    w_key,
    w_value,
    w_output,
    mid_gain,
    mid_shift,
    w_up,
    w_down,
    w_router,
    w_mix,
    expert_up,
    expert_down,
):
    tokens, width = inputs.shape
    heads = width // HEAD_DIM
    owners = lax.axis_size("ep")
    experts = w_router.shape[1]
    capacity = max(2, 10 * tokens // (7 * owners))
    slots_all = owners * capacity
    side = lax.axis_index("es")
    query_w, key_w, value_w, output_w, up_w, down_w = (
        lax.all_gather(w_query, "es", axis=0, tiled=True),
        lax.all_gather(w_key, "es", axis=0, tiled=True),
        lax.all_gather(w_value, "es", axis=0, tiled=True),
        lax.all_gather(w_output, "es", axis=0, tiled=True),
        lax.all_gather(w_up, "es", axis=0, tiled=True),
        lax.all_gather(w_down, "es", axis=0, tiled=True),
    )
    source = inputs.astype(jnp.float32)
    first = layer_norm(source, pre_gain, pre_shift).astype(jnp.bfloat16)
    query = matmul(first, query_w).astype(jnp.bfloat16)
    keys = matmul(first, key_w).astype(jnp.bfloat16)
    values = matmul(first, value_w).astype(jnp.bfloat16)
    earlier = shifted(jnp.stack([keys, values]), "es", 1)
    all_keys = jnp.concatenate([earlier[0], keys], 0).reshape(2 * tokens, heads, HEAD_DIM)
    all_values = jnp.concatenate([earlier[1], values], 0).reshape(2 * tokens, heads, HEAD_DIM)
    query_heads = query.reshape(tokens, heads, HEAD_DIM)
    block = min(512, tokens)
    blocks = tokens // block
    scale = HEAD_DIM ** (-0.5)
    key_pos = (side - 1) * tokens + jnp.arange(2 * tokens, dtype=jnp.int32)

    def block_scores(index):
        start = index * block
        scores = (
            jnp.einsum("qhd,khd->hqk", query_heads, all_keys, preferred_element_type=jnp.float32)
            * scale
        )
        query_pos = side * tokens + start + jnp.arange(block, dtype=jnp.int32)
        allowed = (key_pos[None, :] <= query_pos[:, None]) & (key_pos[None, :] >= 0)
        return (query_heads, jnp.where(allowed[None], scores, -1e30))

    def forward_block(index):
        query_block, scores = block_scores(index)
        peak = jnp.max(scores, axis=-1, keepdims=True)
        expo = jnp.exp(scores - peak)
        total = jnp.sum(expo, axis=-1, keepdims=True)
        probs = (expo / total).astype(jnp.bfloat16)
        result = jnp.einsum("hqk,khd->qhd", probs, all_values, preferred_element_type=jnp.float32)
        return (result.astype(jnp.bfloat16), (peak + jnp.log(total))[..., 0])

    attended, log_sums = lax.map(forward_block, jnp.arange(blocks))
    attended = attended.reshape(tokens, width)
    resid = source + matmul(attended, output_w)
    second = layer_norm(resid, mid_gain, mid_shift).astype(jnp.bfloat16)
    up_pre = matmul(second, up_w)
    hidden = gelu_tanh(up_pre).astype(jnp.bfloat16)
    dense = matmul(hidden, down_w)
    route_logits = matmul(second, w_router)
    mix_logits = matmul(second, w_mix)
    chosen = expert_choice[:, 0]
    onehot = (chosen[:, None] == jnp.arange(experts, dtype=jnp.int32)[None, :]).astype(jnp.int32)
    ranks = jnp.sum(onehot * jnp.cumsum(onehot, axis=0), axis=1) - 1
    place = chosen * capacity + ranks
    placing = (jnp.arange(slots_all, dtype=jnp.int32)[:, None] == place[None, :]).astype(
        jnp.bfloat16
    )
    sent = matmul(placing, second).astype(jnp.bfloat16).reshape(owners, capacity, width)
    arrived = lax.all_to_all(sent, "ep", split_axis=0, concat_axis=0, tiled=True).reshape(
        slots_all, width
    )
    gathered = lax.all_gather(arrived, "es", axis=0, tiled=True)
    expert_pre = matmul(gathered, expert_up[0])
    expert_hidden = gelu_tanh(expert_pre).astype(jnp.bfloat16)
    expert_out = lax.psum_scatter(
        matmul(expert_hidden, expert_down[0]), "es", scatter_dimension=0, tiled=True
    ).astype(jnp.bfloat16)
    returned = lax.all_to_all(
        expert_out.reshape(owners, capacity, width), "ep", split_axis=0, concat_axis=0, tiled=True
    )
    routed = jnp.take(returned.reshape(slots_all, width), place, axis=0).astype(jnp.float32)
    choice_mask = onehot.astype(jnp.float32)

    def combine(dense_part, routed_part, route_part, mix_part):
        route_probs = jax.nn.softmax(route_part, axis=-1)
        gate = jnp.sum(route_probs * choice_mask, axis=-1, keepdims=True)
        mix = jax.nn.softmax(mix_part, axis=-1)
        return mix[:, 0:1] * dense_part + mix[:, 1:2] * gate * routed_part

    mixed, mix_pull = jax.vjp(combine, dense, routed, route_logits, mix_logits)
    output = (resid + mixed).astype(jnp.bfloat16)
    upstream = grad_output.astype(jnp.float32)
    d_dense, d_routed, d_route, d_mix = mix_pull(upstream)
    d_dense = d_dense.astype(jnp.bfloat16)
    d_routed = d_routed.astype(jnp.bfloat16)
    d_route = d_route.astype(jnp.bfloat16)
    d_mix = d_mix.astype(jnp.bfloat16)
    d_hidden = matmul_nt(d_dense, down_w)
    d_up = jax.vjp(gelu_tanh, up_pre)[1](d_hidden)[0].astype(jnp.bfloat16)
    grad_down = matmul_tn(hidden, d_dense)
    grad_up = matmul_tn(second, d_up)
    grad_router = matmul_tn(second, d_route)
    grad_mixer = matmul_tn(second, d_mix)
    d_second = matmul_nt(d_up, up_w) + matmul_nt(d_route, w_router) + matmul_nt(d_mix, w_mix)
    grad_sent = matmul(placing, d_routed).astype(jnp.bfloat16).reshape(owners, capacity, width)
    grad_arrived = lax.all_to_all(grad_sent, "ep", split_axis=0, concat_axis=0, tiled=True).reshape(
        slots_all, width
    )
    grad_gathered = lax.all_gather(grad_arrived, "es", axis=0, tiled=True)
    d_expert_hidden = matmul_nt(grad_gathered, expert_down[0])
    d_expert_pre = jax.vjp(gelu_tanh, expert_pre)[1](d_expert_hidden)[0].astype(jnp.bfloat16)
    grad_expert_down = matmul_tn(expert_hidden, grad_gathered)[None]
    grad_expert_up = matmul_tn(gathered, d_expert_pre)[None]
    d_slots = lax.psum_scatter(
        matmul_nt(d_expert_pre, expert_up[0]), "es", scatter_dimension=0, tiled=True
    )
    d_returned = lax.all_to_all(
        d_slots.reshape(owners, capacity, width), "ep", split_axis=0, concat_axis=0, tiled=True
    )
    d_second = d_second + jnp.take(d_returned.reshape(slots_all, width), place, axis=0)
    d_resid_mid, grad_mid_gain, grad_mid_shift = jax.vjp(layer_norm, resid, mid_gain, mid_shift)[1](
        d_second
    )
    d_resid = upstream + d_resid_mid
    d_attn = d_resid.astype(jnp.bfloat16)
    grad_out_w = matmul_tn(attended, d_attn)
    d_attended = matmul_nt(d_attn, output_w).astype(jnp.bfloat16).reshape(tokens, heads, HEAD_DIM)

    def backward_block(carry, index):
        d_keys, d_values = carry
        query_block, scores = block_scores(index)
        probs = jnp.exp(scores - log_sums[index][..., None])
        d_values = d_values + jnp.einsum(
            "hqk,qhd->khd",
            probs.astype(jnp.bfloat16),
            d_attended,
            preferred_element_type=jnp.float32,
        )
        d_probs = jnp.einsum(
            "qhd,khd->hqk", d_attended, all_values, preferred_element_type=jnp.float32
        )
        d_scores = probs * (d_probs - jnp.sum(probs * d_probs, axis=-1, keepdims=True))
        d_scores = d_scores.astype(jnp.bfloat16)
        d_query = (
            jnp.einsum("hqk,khd->qhd", d_scores, all_keys, preferred_element_type=jnp.float32)
            * scale
        )
        d_keys = (
            d_keys
            + jnp.einsum("hqk,qhd->khd", d_scores, query_block, preferred_element_type=jnp.float32)
            * scale
        )
        return ((d_keys, d_values), d_query)

    zeros = jnp.zeros((2 * tokens, heads, HEAD_DIM), jnp.float32)
    (d_keys, d_values), d_query = lax.scan(backward_block, (zeros, zeros), jnp.arange(blocks))
    d_query = d_query.reshape(tokens, width).astype(jnp.bfloat16)
    d_keys = d_keys.reshape(2 * tokens, width)
    d_values = d_values.reshape(2 * tokens, width)
    later = shifted(jnp.stack([d_keys[:tokens], d_values[:tokens]]), "es", -1)
    d_key_low = (d_keys[tokens:] + later[0]).astype(jnp.bfloat16)
    d_value_low = (d_values[tokens:] + later[1]).astype(jnp.bfloat16)
    grad_query = matmul_tn(first, d_query)
    grad_key = matmul_tn(first, d_key_low)
    grad_value = matmul_tn(first, d_value_low)
    d_first = (
        matmul_nt(d_query, query_w) + matmul_nt(d_key_low, key_w) + matmul_nt(d_value_low, value_w)
    )
    d_source, grad_pre_gain, grad_pre_shift = jax.vjp(layer_norm, source, pre_gain, pre_shift)[1](
        d_first
    )
    grad_inputs = d_resid + d_source
    summed = (
        lax.psum_scatter(grad_pre_gain, ("ep", "es"), scatter_dimension=0, tiled=True),
        lax.psum_scatter(grad_pre_shift, ("ep", "es"), scatter_dimension=0, tiled=True),
        lax.psum_scatter(grad_query, ("ep", "es"), scatter_dimension=0, tiled=True),
        lax.psum_scatter(grad_key, ("ep", "es"), scatter_dimension=0, tiled=True),
        lax.psum_scatter(grad_value, ("ep", "es"), scatter_dimension=0, tiled=True),
        lax.psum_scatter(grad_out_w, ("ep", "es"), scatter_dimension=0, tiled=True),
        lax.psum_scatter(grad_mid_gain, ("ep", "es"), scatter_dimension=0, tiled=True),
        lax.psum_scatter(grad_mid_shift, ("ep", "es"), scatter_dimension=0, tiled=True),
        lax.psum_scatter(grad_up, ("ep", "es"), scatter_dimension=0, tiled=True),
        lax.psum_scatter(grad_down, ("ep", "es"), scatter_dimension=0, tiled=True),
        lax.psum_scatter(grad_router, ("ep", "es"), scatter_dimension=0, tiled=True),
        lax.psum_scatter(grad_mixer, ("ep", "es"), scatter_dimension=0, tiled=True),
    )
    return (
        output,
        grad_inputs,
        summed[0],
        summed[1],
        summed[2],
        summed[3],
        summed[4],
        summed[5],
        summed[6],
        summed[7],
        summed[8],
        summed[9],
        summed[10],
        summed[11],
        grad_expert_up,
        grad_expert_down,
    )


def solution(mesh):
    placed = (
        P(("ep", "es"), None),
        P(("ep", "es"), None),
        P(("ep", "es"), None),
        P(),
        P(),
        P("es", None),
        P("es", None),
        P("es", None),
        P("es", None),
        P(),
        P(),
        P("es", None),
        P("es", None),
        P(),
        P(),
        P("ep", None, "es"),
        P("ep", "es", None),
    )
    return jax.shard_map(
        body,
        mesh=mesh,
        in_specs=placed,
        out_specs=(
            P(("ep", "es"), None),
            P(("ep", "es"), None),
            P(("ep", "es")),
            P(("ep", "es")),
            P(("ep", "es"), None),
            P(("ep", "es"), None),
            P(("ep", "es"), None),
            P(("ep", "es"), None),
            P(("ep", "es")),
            P(("ep", "es")),
            P(("ep", "es"), None),
            P(("ep", "es"), None),
            P(("ep", "es"), None),
            P(("ep", "es"), None),
            P("ep", None, "es"),
            P("ep", "es", None),
        ),
        check_vma=False,
    )
```

profile of v0, /device:TPU:18, one launch (start us, length us, event | category | flops | bytes accessed | tf_op | source)
XLA Modules:
  0.0 2406.4 jit_solution(14598408635629982050)
XLA Ops:
  10.7 33.0 %all-gather.11.cloned.1.call-done = bf16[1024,1024]{1,0:T(8,128)(2,1)} async-done(((bf16[512,1024]{1,0:T(8,128)(2,1)}), bf16[1024,1024]{1,0:T(8,128)(2,1)}) %all-gather.11.cloned.1.call-update) | async-done | bytes 2097168 | tf_op jit(solution)/shard_map/all_gather | solution.py:71
  43.8 2.9 convolution_convert_fusion.4
  46.7 31.8 %all-gather.9.cloned.1.call-done = bf16[1024,1024]{1,0:T(8,128)(2,1)} async-done(((bf16[512,1024]{1,0:T(8,128)(2,1)}), bf16[1024,1024]{1,0:T(8,128)(2,1)}) %all-gather.9.cloned.1.call-update) | async-done | bytes 2097168 | tf_op jit(solution)/shard_map/all_gather | solution.py:70
  78.4 2.9 convolution_convert_fusion.5
  83.8 3.8 collective-permute-start
  93.5 40.2 %all-gather.13.cloned.1.call-done = bf16[1024,1024]{1,0:T(8,128)(2,1)} async-done(((bf16[512,1024]{1,0:T(8,128)(2,1)}), bf16[1024,1024]{1,0:T(8,128)(2,1)}) %all-gather.13.cloned.1.call-update) | async-done | bytes 2097168 | tf_op jit(solution)/shard_map/all_gather | solution.py:69
  133.6 3.9 convolution_convert_fusion.3
  139.0 24.1 %collective-permute-done = bf16[2,512,1024]{2,1,0:T(8,128)(2,1)} collective-permute-done((bf16[2,512,1024]{2,1,0:T(8,128)(2,1)}, bf16[2,512,1024]{2,1,0:T(8,128)(2,1)}, u32[]{:S(2)}, u32[]{:S(2)}) %collective-permute-start) | collective-permute-done | bytes 2097184 | tf_op jit(solution)/shard_map/ppermute | solution.py:12
  163.1 3.0 fusion.97
  170.7 15.0 fusion.100
  185.8 14.4 fusion
  200.3 13.7 fusion.55
  214.0 3.3 fusion.101
  221.4 40.6 %all_to_all.20 = bf16[16,45,1024]{2,1,0:T(8,128)(2,1)} all-to-all(bf16[16,45,1024]{2,1,0:T(8,128)(2,1)} %reshape.303), channel_id=1, replica_groups=mesh['ep'=16,'es'=2] {'ep'}, dimensions={0} | all-to-all | bytes 2949120 | tf_op jit(solution)/shard_map/all_to_all | solution.py:126
  261.9 2.5 reshape.304
  264.7 45.0 %all-gather.21.cloned.1.call-done = bf16[1440,1024]{1,0:T(8,128)(2,1)} async-done(((bf16[720,1024]{1,0:T(8,128)(2,1)}), bf16[1440,1024]{1,0:T(8,128)(2,1)}) %all-gather.21.cloned.1.call-update) | async-done | bytes 2949136 | tf_op jit(solution)/shard_map/all_gather | solution.py:129
  309.8 9.2 fusion.28
  319.0 4.3 copy-done.57
  323.3 9.0 fusion.22
  333.8 71.5 %reduce-scatter.15.cloned.1.call-done = f32[720,1024]{1,0:T(8,128)} async-done(((f32[1440,1024]{1,0:T(8,128)}), f32[720,1024]{1,0:T(8,128)}) %reduce-scatter.15.cloned.1.call-update) | async-done | bytes 2949136 | tf_op jit(solution)/shard_map/reduce_scatter | solution.py:132
  408.8 6.0 all-to-all-start.1
  416.3 94.6 %all-gather.17.cloned.1.call-done = bf16[1024,4096]{1,0:T(8,128)(2,1)} async-done(((bf16[512,4096]{1,0:T(8,128)(2,1)}), bf16[1024,4096]{1,0:T(8,128)(2,1)}) %all-gather.17.cloned.1.call-update) | async-done | bytes 8388624 | tf_op jit(solution)/shard_map/all_gather | solution.py:73
  510.9 10.2 fusion.104
  523.0 2.8 gather_fusion
  525.8 90.7 %all-gather.19.cloned.1.call-done = bf16[4096,1024]{1,0:T(8,128)(2,1)} async-done(((bf16[2048,1024]{1,0:T(8,128)(2,1)}), bf16[4096,1024]{1,0:T(8,128)(2,1)}) %all-gather.19.cloned.1.call-update) | async-done | bytes 8388624 | tf_op jit(solution)/shard_map/all_gather | solution.py:74
  616.4 13.1 fusion.49
  631.8 2.5 reshape.309
  634.3 40.6 %all_to_all.21 = bf16[16,45,1024]{2,1,0:T(8,128)(2,1)} all-to-all(bf16[16,45,1024]{2,1,0:T(8,128)(2,1)} %reshape.309), channel_id=1, replica_groups=mesh['ep'=16,'es'=2] {'ep'}, dimensions={0} | all-to-all | bytes 2949120 | tf_op jit(solution)/shard_map/all_to_all | solution.py:163
  674.8 2.5 reshape.310
  677.6 43.2 %all-gather.23.cloned.1.call-done = bf16[1440,1024]{1,0:T(8,128)(2,1)} async-done(((bf16[720,1024]{1,0:T(8,128)(2,1)}), bf16[1440,1024]{1,0:T(8,128)(2,1)}) %all-gather.23.cloned.1.call-update) | async-done | bytes 2949136 | tf_op jit(solution)/shard_map/all_gather | solution.py:166
  720.8 17.3 fusion.12
  738.0 2.5 copy-done.56
  740.6 8.3 fusion.26
  749.0 73.0 %reduce-scatter.17.cloned.1.call-done = f32[720,1024]{1,0:T(8,128)} async-done(((f32[1440,1024]{1,0:T(8,128)}), f32[720,1024]{1,0:T(8,128)}) %reduce-scatter.17.cloned.1.call-update) | async-done | bytes 2949136 | tf_op jit(solution)/shard_map/reduce_scatter | solution.py:171
  822.0 3.2 reshape.311
  825.2 6.0 all-to-all-start.3
  836.1 12.5 fusion.19
  850.6 8.3 fusion.105
  858.9 40.7 %all-to-all-done.3 = f32[16,45,1024]{2,1,0:T(8,128)} async-done(((f32[16,45,1024]{2,1,0:T(8,128)}), f32[16,45,1024]{2,1,0:T(8,128)}, u32[]{:S(2)}, u32[]{:S(2)}) %all-to-all-start.3) | async-done | bytes 2949152 | tf_op jit(solution)/shard_map/all_to_all | solution.py:174
  901.7 2.7 gather_fusion.1
  904.4 5.1 multiply_reduce_fusion.1
  913.8 3.2 fusion.108
  917.8 4.1 convolution_convert_fusion.2
  923.4 22.3 multiply_reduce_fusion
  945.7 27.9 %multiply_convert_fusion = bf16[16,512,1024]{2,1,0:T(8,128)(2,1)} fusion(f32[16,512,1024]{2,1,0:T(8,128)} %get-tuple-element.118, f32[16,512,1024]{2,1,0:T(8,128)} %get-tuple-element.108, f32[16,512]{1,0:T(8,128)S(1)} %get-tuple-element.117, f32[16,512]{1,0:T(8,128)S(1)} %log_add_fusion), kind=kLoop, calls=%fused_computation.2 | loop fusion | flops 33554432 | bytes 83951616 | tf_op jit(solution)/shard_map/while/body/eval_jaxpr/convert_element_type | solution.py:200
  973.7 12.4 multiply_convert_fusion.3
  986.1 4.8 fusion.88
  992.1 15.1 fusion.62
  1008.4 10.4 fusion.109
  1019.0 15.5 fusion.36
  1034.5 2.8 fusion.95
  1037.3 8.9 multiply_bitcast_fusion
  1048.5 128.7 %collective-permute-done.1 = f32[2,512,1024]{1,2,0:T(8,128)S(1)} collective-permute-done((f32[2,512,1024]{1,2,0:T(8,128)S(1)}, f32[2,512,1024]{1,2,0:T(8,128)S(1)}, u32[]{:S(2)}, u32[]{:S(2)}) %collective-permute-start.1) | collective-permute-done | bytes 4194336 | tf_op jit(solution)/shard_map/ppermute | solution.py:12
  1179.3 3.5 fusion.84
  1183.1 3.5 fusion.86
  1189.5 11.9 convolution_bitcast_fusion.1
  1201.4 13.2 convolution_bitcast_fusion
  1220.9 46.2 %all-reduce.6 = (f32[1024]{0:T(1024)S(1)}, f32[1024]{0:T(1024)S(1)}, f32[1024]{0:T(1024)S(1)}, f32[1024]{0:T(1024)S(1)}) all-reduce(f32[1024]{0:T(1024)S(1)} %get-tuple-element.64, f32[1024]{0:T(1024)S(1)} %get-tuple-element.78, f32[1024]{0:T(1024)S(1)} %copy-done.46, ...), channel_id=4, replica_groups=mesh['ep'=16,'es'=2] {'ep','es'}, use_global_device_ids=true, to_apply=%region_26.27.clone | all-reduce | flops 4096 | bytes 32768
  1269.5 4.1 add_add_fusion.2
  1273.6 117.9 %reduce-scatter.19.cloned.1.call-done = f32[32,1024]{1,0:T(8,128)} async-done(((f32[1024,1024]{1,0:T(8,128)}), f32[32,1024]{1,0:T(8,128)}) %reduce-scatter.19.cloned.1.call-update) | async-done | bytes 131088 | tf_op jit(solution)/shard_map/reduce_scatter | solution.py:233
  1391.5 374.0 %reduce-scatter.29.cloned.1.call-done = f32[128,1024]{1,0:T(8,128)} async-done(((f32[4096,1024]{1,0:T(8,128)}), f32[128,1024]{1,0:T(8,128)}) %reduce-scatter.29.cloned.1.call-update) | async-done | bytes 524304 | tf_op jit(solution)/shard_map/reduce_scatter | solution.py:240
  1765.5 361.3 %reduce-scatter.27.cloned.1.call-done = f32[32,4096]{1,0:T(8,128)} async-done(((f32[1024,4096]{1,0:T(8,128)}), f32[32,4096]{1,0:T(8,128)}) %reduce-scatter.27.cloned.1.call-update) | async-done | bytes 524304 | tf_op jit(solution)/shard_map/reduce_scatter | solution.py:239
  2126.8 129.8 %reduce-scatter.23.cloned.1.call-done = f32[32,1024]{1,0:T(8,128)} async-done(((f32[1024,1024]{1,0:T(8,128)}), f32[32,1024]{1,0:T(8,128)}) %reduce-scatter.23.cloned.1.call-update) | async-done | bytes 131088 | tf_op jit(solution)/shard_map/reduce_scatter | solution.py:235
  2256.6 142.5 %reduce-scatter.21.cloned.1.call-done = f32[32,1024]{1,0:T(8,128)} async-done(((f32[1024,1024]{1,0:T(8,128)}), f32[32,1024]{1,0:T(8,128)}) %reduce-scatter.21.cloned.1.call-update) | async-done | bytes 131088 | tf_op jit(solution)/shard_map/reduce_scatter | solution.py:234
  (227 shorter events, 67.2 us)
Async XLA Ops:
  7.2 408.6 %copy-start = (bf16[1024,16]{0,1:T(8,128)(2,1)S(1)}, bf16[1024,16]{0,1:T(8,128)(2,1)}, u32[]{:S(2)}) copy-start(bf16[1024,16]{0,1:T(8,128)(2,1)} %param.30) | copy-start | bytes 98308
  7.2 2.3 copy-start.4
  7.2 36.6 %copy-start.37 = (f32[1024]{0:T(1024)S(1)}, f32[1024]{0:T(1024)}, u32[]{:S(2)}) copy-start(f32[1024]{0:T(1024)} %param.20) | copy-start | bytes 12292
  7.2 36.5 %copy-start.54 = (f32[1024]{0:T(1024)S(1)}, f32[1024]{0:T(1024)}, u32[]{:S(2)}) copy-start(f32[1024]{0:T(1024)} %param.21) | copy-start | bytes 12292
  7.2 36.5 %all-gather.11.cloned.1.call-start = ((), (), s32[]{:S(2)}) async-start(), calls=%async_computation.15 | async-start | bytes 3145728 | tf_op jit(solution)/shard_map/all_gather | solution.py:71
  8.0 70.5 %all-gather.9.cloned.1.call-start = ((), (), s32[]{:S(2)}) async-start(), calls=%async_computation.14 | async-start | bytes 3145728 | tf_op jit(solution)/shard_map/all_gather | solution.py:70
  8.7 124.9 %all-gather.13.cloned.1.call-start = ((), (), s32[]{:S(2)}) async-start(), calls=%async_computation.16 | async-start | bytes 3145728 | tf_op jit(solution)/shard_map/all_gather | solution.py:69
  9.5 204.5 %all-gather.15.cloned.1.call-start = ((), (), s32[]{:S(2)}) async-start(), calls=%async_computation.17 | async-start | bytes 3145728 | tf_op jit(solution)/shard_map/all_gather | solution.py:72
  9.7 123.9 %copy-start.34 = (f32[512]{0:T(512)}, f32[512]{0:T(512)S(1)}, u32[]{:S(2)}) copy-start(f32[512]{0:T(512)S(1)} %broadcast_multiply_fusion.1) | copy-start | bytes 6148
  10.7 122.9 %copy-start.39 = (f32[512]{0:T(512)}, f32[512]{0:T(512)S(1)}, u32[]{:S(2)}) copy-start(f32[512]{0:T(512)S(1)} %fusion.72) | copy-start | bytes 6148
  81.3 6.5 copy-start.33
  83.8 79.3 %collective-permute-start = (bf16[2,512,1024]{2,1,0:T(8,128)(2,1)}, bf16[2,512,1024]{2,1,0:T(8,128)(2,1)}, u32[]{:S(2)}, u32[]{:S(2)}) collective-permute-start(bf16[2,512,1024]{2,1,0:T(8,128)(2,1)} %pad_maximum_fusion.1), channel_id=1, source_target_pairs={{0,1},{2,3},{4,5},{6,7},{8,9},{10,11},{12,13},{14,15},{16,17},{18,... | collective-permute-start | bytes 6291464 | tf_op jit(solution)/shard_map/ppermute | solution.py:12
  87.6 222.2 %all-gather.21.cloned.1.call-start = ((), (), s32[]{:S(2)}) async-start(), calls=%async_computation.20 | async-start | bytes 4423680 | tf_op jit(solution)/shard_map/all_gather | solution.py:129
  92.1 78.6 %copy-start.11 = (bf16[512,1024]{0,1:T(8,128)(2,1)}, bf16[512,1024]{0,1:T(8,128)(2,1)S(1)}, u32[]{:S(2)}) copy-start(bf16[512,1024]{0,1:T(8,128)(2,1)S(1)} %copy.53) | copy-start | bytes 3145732
  139.0 31.8 %copy-start.9 = (bf16[512,1024]{0,1:T(8,128)(2,1)}, bf16[512,1024]{0,1:T(8,128)(2,1)S(1)}, u32[]{:S(2)}) copy-start(bf16[512,1024]{0,1:T(8,128)(2,1)S(1)} %copy.51) | copy-start | bytes 3145732
  185.8 14.5 copy-start.29
  185.8 14.5 copy-start.13
  185.8 14.5 copy-start.15
  200.2 13.8 copy-start.31
  214.0 4.6 copy-start.36
  214.0 4.6 copy-start.48
  219.0 613.6 %copy-start.6 = (bf16[512,1024]{1,0:T(8,128)(2,1)}, bf16[512,1024]{1,0:T(8,128)(2,1)S(1)}, u32[]{:S(2)}) copy-start(bf16[512,1024]{1,0:T(8,128)(2,1)S(1)} %add_convert_fusion) | copy-start | bytes 3145732
  264.4 140.9 %reduce-scatter.15.cloned.1.call-start = ((), (), s32[]{:S(2)}) async-start(), calls=%async_computation.21 | async-start | bytes 8847360 | tf_op jit(solution)/shard_map/reduce_scatter | solution.py:132
  309.8 13.5 copy-start.49
  319.0 4.3 copy-start.57
  332.3 178.6 %all-gather.17.cloned.1.call-start = ((), (), s32[]{:S(2)}) async-start(), calls=%async_computation.18 | async-start | bytes 12582912 | tf_op jit(solution)/shard_map/all_gather | solution.py:73
  333.0 283.4 %all-gather.19.cloned.1.call-start = ((), (), s32[]{:S(2)}) async-start(), calls=%async_computation.19 | async-start | bytes 12582912 | tf_op jit(solution)/shard_map/all_gather | solution.py:74
  407.4 8.0 copy-start.45
  408.8 112.3 %all-to-all-start.1 = ((bf16[16,45,1024]{2,1,0:T(8,128)(2,1)}), bf16[16,45,1024]{2,1,0:T(8,128)(2,1)}, u32[]{:S(2)}, u32[]{:S(2)}) async-start(bf16[16,45,1024]{2,1,0:T(8,128)(2,1)} %reshape.305), calls=%async_computation.2 | async-start | bytes 3145728 | tf_op jit(solution)/shard_map/all_to_all | solution.py:135
  414.8 306.0 %all-gather.23.cloned.1.call-start = ((), (), s32[]{:S(2)}) async-start(), calls=%async_computation.22 | async-start | bytes 4423680 | tf_op jit(solution)/shard_map/all_gather | solution.py:166
  616.4 13.2 copy-start.17
  677.3 144.6 %reduce-scatter.17.cloned.1.call-start = ((), (), s32[]{:S(2)}) async-start(), calls=%async_computation.23 | async-start | bytes 8847360 | tf_op jit(solution)/shard_map/reduce_scatter | solution.py:171
  720.8 19.8 copy-start.50
  738.0 2.6 copy-start.56
  825.2 74.5 %all-to-all-start.3 = ((f32[16,45,1024]{2,1,0:T(8,128)}), f32[16,45,1024]{2,1,0:T(8,128)}, u32[]{:S(2)}, u32[]{:S(2)}) async-start(f32[16,45,1024]{2,1,0:T(8,128)} %reshape.311), calls=%async_computation.5 | async-start | bytes 6291456 | tf_op jit(solution)/shard_map/all_to_all | solution.py:174
  831.2 355.5 %reduce-scatter.33.cloned.1.call-start = ((), (), s32[]{:S(2)}) async-start(), calls=%async_computation.31 | async-start | bytes 540672
  832.6 355.5 %reduce-scatter.31.cloned.1.call-start = ((), (), s32[]{:S(2)}) async-start(), calls=%async_computation.30 | async-start | bytes 540672
  834.1 439.5 %reduce-scatter.25.cloned.1.call-start = ((), (), s32[]{:S(2)}) async-start(), calls=%async_computation.27 | async-start | bytes 4325376 | tf_op jit(solution)/shard_map/reduce_scatter | solution.py:236
  848.6 2.0 copy-start.21
  904.4 5.1 copy-start.3
  904.4 5.1 copy-start.22
  904.4 5.1 copy-start.26
  909.5 3.6 copy-start.18
  911.8 5.2 copy-start.41
  917.0 474.4 %reduce-scatter.19.cloned.1.call-start = ((), (), s32[]{:S(2)}) async-start(), calls=%async_computation.24 | async-start | bytes 4325376 | tf_op jit(solution)/shard_map/reduce_scatter | solution.py:233
  917.8 5.6 copy-start.14
  917.8 5.6 copy-start.16
  945.7 27.9 %copy-start.12 = (bf16[512,1024]{0,1:T(8,128)(2,1)S(1)}, bf16[512,1024]{0,1:T(8,128)(2,1)}, u32[]{:S(2)}) copy-start(bf16[512,1024]{0,1:T(8,128)(2,1)} %copy-done.11) | copy-start | bytes 3145732
  973.6 12.4 copy-start.5
  973.6 12.4 copy-start.35
  973.6 12.4 copy-start.38
  973.7 12.4 copy-start.40
  973.7 12.4 copy-start.55
  990.9 774.6 %reduce-scatter.29.cloned.1.call-start = ((), (), s32[]{:S(2)}) async-start(), calls=%async_computation.29 | async-start | bytes 17301504 | tf_op jit(solution)/shard_map/reduce_scatter | solution.py:240
  1007.2 1119.6 %reduce-scatter.27.cloned.1.call-start = ((), (), s32[]{:S(2)}) async-start(), calls=%async_computation.28 | async-start | bytes 17301504 | tf_op jit(solution)/shard_map/reduce_scatter | solution.py:239
  1018.8 1237.8 %reduce-scatter.23.cloned.1.call-start = ((), (), s32[]{:S(2)}) async-start(), calls=%async_computation.26 | async-start | bytes 4325376 | tf_op jit(solution)/shard_map/reduce_scatter | solution.py:235
  1034.5 2.8 copy-start.10
  1047.2 130.0 %collective-permute-start.1 = (f32[2,512,1024]{1,2,0:T(8,128)S(1)}, f32[2,512,1024]{1,2,0:T(8,128)S(1)}, u32[]{:S(2)}, u32[]{:S(2)}) collective-permute-start(f32[2,512,1024]{1,2,0:T(8,128)S(1)} %pad_maximum_fusion), channel_id=1, source_target_pairs={{1,0},{3,2},{5,4},{7,6},{9,8},{11,10},{13,12},{15,14},{17,16},{19,... | collective-permute-start | bytes 12582920 | tf_op jit(solution)/shard_map/ppermute | solution.py:12
  1182.8 1216.2 %reduce-scatter.21.cloned.1.call-start = ((), (), s32[]{:S(2)}) async-start(), calls=%async_computation.25 | async-start | bytes 4325376 | tf_op jit(solution)/shard_map/reduce_scatter | solution.py:234
  1189.5 11.9 copy-start.51
  1201.4 13.2 copy-start.27
  1201.4 13.2 copy-start.53
  1219.9 49.6 %copy-start.42 = (f32[512]{0:T(512)S(1)}, f32[512]{0:T(512)}, u32[]{:S(2)}) copy-start(f32[512]{0:T(512)} %copy-done.41) | copy-start | bytes 6148
  1269.5 1129.6 %copy-start.1 = (bf16[1024,16]{0,1:T(8,128)(2,1)S(1)}, bf16[1024,16]{0,1:T(8,128)(2,1)}, u32[]{:S(2)}) copy-start(bf16[1024,16]{0,1:T(8,128)(2,1)} %param.30) | copy-start | bytes 98308
  (16 other events, 19.9 us)
Sparse Core Ops, SparseCore 0:
  9.6 34.1 all-gather.10
  45.3 33.0 all-gather.8
  80.0 53.6 all-gather.12
  135.0 41.1 all-gather.14
  264.5 45.1 all-gather.20
  332.4 72.8 reduce-scatter.14
  406.9 103.9 all-gather.16
  512.4 103.9 all-gather.18
  677.5 43.2 all-gather.22
  749.1 72.8 reduce-scatter.16
  834.2 123.0 reduce-scatter.32
  959.4 127.2 reduce-scatter.30
  1089.6 156.0 reduce-scatter.24
  1248.4 143.0 reduce-scatter.18
  1394.2 371.2 reduce-scatter.28
  1768.2 358.5 reduce-scatter.26
  2129.5 127.0 reduce-scatter.22
  2259.3 139.7 reduce-scatter.20
where the time goes:
time: 2430 us; the launch traced here: 2410 us
  waiting for transfers between devices  1850 us (76%)
  matrix products  276 us (11%)
  blocking collectives  127 us (5%)
  local copies, waits for them, and re-layouts  62.2 us (3%)
  other arithmetic  59.3 us (2%)
    reduce_scatter x1, waiting for transfers between devices, body(): lax.psum_scatter(grad_down, ('ep', 'es'), scatter_dimension=0, tiled=True)  374 us
    reduce_scatter x1, waiting for transfers between devices, body(): lax.psum_scatter(grad_up, ('ep', 'es'), scatter_dimension=0, tiled=True)  361 us
    ppermute x2, waiting for transfers between devices, shifted(): return lax.ppermute(value, axis, pairs)  153 us
    reduce_scatter x1, waiting for transfers between devices, body(): lax.psum_scatter(grad_key, ('ep', 'es'), scatter_dimension=0, tiled=True)  142 us
    reduce_scatter x1, waiting for transfers between devices, body(): lax.psum_scatter(grad_value, ('ep', 'es'), scatter_dimension=0, tiled=True)  130 us
    reduce_scatter x1, waiting for transfers between devices, body(): lax.psum_scatter(grad_query, ('ep', 'es'), scatter_dimension=0, tiled=True)  118 us
    all_gather x1, waiting for transfers between devices, body(): lax.all_gather(w_up, 'es', axis=0, tiled=True)  94.6 us
    all_gather x1, waiting for transfers between devices, body(): lax.all_gather(w_down, 'es', axis=0, tiled=True)  90.7 us
  transfers between devices with their start and end apart: 22, of which 17 were waited for; matrix products, arithmetic and copies ran while one was open for 13% of the time, Pallas kernels for 0%

commit v1 on v0

v1 whole, which is shorter than its diff:
```python
import jax
import jax.numpy as jnp
from jax import lax
from jax.experimental import pallas as pl
from jax.experimental.pallas import tpu as pltpu
from jax.sharding import PartitionSpec as P

HEAD_DIM = 64
SCALE = HEAD_DIM ** (-0.5)
LANES = 128
QB = 256
BF = jnp.bfloat16
F32 = jnp.float32


def layer_norm(values, gain, shift):
    center = jnp.mean(values, axis=-1, keepdims=True)
    centred = values - center
    spread = jnp.mean(centred * centred, axis=-1, keepdims=True)
    return centred * lax.rsqrt(spread + 1e-05) * gain + shift


def gelu_tanh(values):
    return jax.nn.gelu(values, approximate=True)


def matmul(left, right):
    return jnp.dot(left, right, preferred_element_type=F32)


def matmul_nt(left, right):
    return lax.dot_general(left, right, (((1,), (1,)), ((), ())), preferred_element_type=F32)


def matmul_tn(left, right):
    return lax.dot_general(left, right, (((0,), (0,)), ((), ())), preferred_element_type=F32)


def swap(value):
    return lax.ppermute(value, "es", [(0, 1), (1, 0)])


def core_swap(value):
    size = lax.axis_size("ep")
    return lax.ppermute(value, "ep", [(i, i ^ 1) for i in range(size)])


def rows_of(value, start, count, axis=0):
    return lax.dynamic_slice_in_dim(value, start, count, axis)


def fetch(payload, core):
    half = payload.shape[0] // 2
    got = swap(rows_of(payload, core * half, half))
    other = core_swap(got)
    first = core == 0
    return jnp.concatenate([jnp.where(first, got, other), jnp.where(first, other, got)], 0)


def ordered(own, other, side, axis=0):
    early = side == 0
    return jnp.concatenate(
        [jnp.where(early, own, other), jnp.where(early, other, own)], axis
    )


def head_masks():
    lane = lax.broadcasted_iota(jnp.int32, (1, LANES), 1)
    return (lane < HEAD_DIM, lane >= HEAD_DIM)


def attend_kernel(qkv_ref, out_ref, lse_ref):
    length = qkv_ref.shape[0]
    masks = head_masks()
    for start in range(0, length, QB):
        reach = start + QB
        query = qkv_ref[start:reach, 0:LANES] * SCALE
        keys = qkv_ref[0:reach, LANES : 2 * LANES]
        values = qkv_ref[0:reach, 2 * LANES :]
        row = lax.broadcasted_iota(jnp.int32, (QB, reach), 0) + start
        col = lax.broadcasted_iota(jnp.int32, (QB, reach), 1)
        outs, logs = [], []
        for mask in masks:
            scores = matmul_nt(jnp.where(mask, query, 0.0).astype(BF), keys)
            scores = jnp.where(col <= row, scores, -1e30)
            peak = jnp.max(scores, axis=-1, keepdims=True)
            expo = jnp.exp(scores - peak)
            total = jnp.sum(expo, axis=-1, keepdims=True)
            probs = (expo * (1.0 / total)).astype(BF)
            outs.append(matmul(probs, values))
            logs.append(peak + jnp.log(total))
        out_ref[start:reach, :] = jnp.where(masks[0], outs[0], outs[1]).astype(BF)
        lse_ref[start:reach, :] = jnp.where(masks[0], logs[0], logs[1])


def attend_back_kernel(qkv_ref, out_ref, lse_ref, grad_ref, dqkv_ref, dk_ref, dv_ref):
    length = qkv_ref.shape[0]
    masks = head_masks()
    for start in reversed(range(0, length, QB)):
        reach = start + QB
        query = qkv_ref[start:reach, 0:LANES] * SCALE
        keys = qkv_ref[0:reach, LANES : 2 * LANES]
        values = qkv_ref[0:reach, 2 * LANES :]
        grad = grad_ref[start:reach, :]
        weighed = grad.astype(F32) * out_ref[start:reach, :].astype(F32)
        row = lax.broadcasted_iota(jnp.int32, (QB, reach), 0) + start
        col = lax.broadcasted_iota(jnp.int32, (QB, reach), 1)
        dq, dk, dv = [], None, None
        for h, mask in enumerate(masks):
            q_h = jnp.where(mask, query, 0.0).astype(BF)
            g_h = jnp.where(mask, grad, 0.0).astype(BF)
            scores = matmul_nt(q_h, keys)
            lse = lse_ref[start:reach, h * HEAD_DIM : h * HEAD_DIM + 1]
            probs = jnp.where(col <= row, jnp.exp(scores - lse), 0.0)
            delta = jnp.sum(jnp.where(mask, weighed, 0.0), axis=-1, keepdims=True)
            d_scores = (probs * (matmul_nt(g_h, values) - delta)).astype(BF)
            dq.append(matmul(d_scores, keys))
            dk_h = matmul_tn(d_scores, q_h)
            dv_h = matmul_tn(probs.astype(BF), g_h)
            dk = dk_h if dk is None else dk + dk_h
            dv = dv_h if dv is None else dv + dv_h
        dqkv_ref[start:reach, 0:LANES] = (
            jnp.where(masks[0], dq[0], dq[1]) * SCALE
        ).astype(BF)
        if reach == length:
            dk_ref[...] = dk
            dv_ref[...] = dv
        else:
            dk_ref[0:reach, :] += dk
            dv_ref[0:reach, :] += dv
    dqkv_ref[:, LANES : 2 * LANES] = dk_ref[...].astype(BF)
    dqkv_ref[:, 2 * LANES :] = dv_ref[...].astype(BF)


def attend(qkv):
    length, columns = qkv.shape
    pairs = columns // (3 * LANES)
    wide = pl.BlockSpec((length, 3 * LANES), lambda h: (0, h))
    slim = pl.BlockSpec((length, LANES), lambda h: (0, h))
    return pl.pallas_call(
        attend_kernel,
        grid=(pairs,),
        in_specs=[wide],
        out_specs=[slim, slim],
        out_shape=[
            jax.ShapeDtypeStruct((length, pairs * LANES), BF),
            jax.ShapeDtypeStruct((length, pairs * LANES), F32),
        ],
        name="attend",
    )(qkv)


def attend_back(qkv, out, lse, grad):
    length, columns = qkv.shape
    pairs = columns // (3 * LANES)
    wide = pl.BlockSpec((length, 3 * LANES), lambda h: (0, h))
    slim = pl.BlockSpec((length, LANES), lambda h: (0, h))
    return pl.pallas_call(
        attend_back_kernel,
        grid=(pairs,),
        in_specs=[wide, slim, slim, slim],
        out_specs=wide,
        out_shape=jax.ShapeDtypeStruct((length, columns), BF),
        scratch_shapes=[pltpu.VMEM((length, LANES), F32), pltpu.VMEM((length, LANES), F32)],
        name="attend_back",
    )(qkv, out, lse, grad)


def pieces(value):
    high = lax.reduce_precision(value, 8, 7)
    rest = value - high
    mid = lax.reduce_precision(rest, 8, 7)
    return [high, mid, rest - mid]


def body(
    inputs,
    grad_output,
    expert_choice,
    pre_gain,
    pre_shift,
    w_query,
    w_key,
    w_value,
    w_output,
    mid_gain,
    mid_shift,
    w_up,
    w_down,
    w_router,
    w_mix,
    expert_up,
    expert_down,
):
    tokens, width = inputs.shape
    owners = lax.axis_size("ep")
    experts = w_router.shape[1]
    capacity = max(2, 10 * tokens // (7 * owners))
    room = -(-(capacity + 3) // 16) * 16
    side = lax.axis_index("es")
    rank = lax.axis_index("ep")
    core = rank % 2
    half = w_query.shape[0]
    pairs = half // LANES
    hidden_half = w_down.shape[0]

    def pair_columns(at):
        parts = [
            rows_of(w, at * half, half, 1).reshape(half, pairs, 1, LANES)
            for w in (w_query, w_key, w_value)
        ]
        return jnp.concatenate(parts, 2).reshape(half, 3 * half)

    inputs_other = swap(inputs)
    qkv_other = fetch(pair_columns(1 - side), core)
    grad_other = swap(grad_output)
    choice_other = swap(expert_choice)
    output_other = fetch(w_output, core)
    up_other = fetch(rows_of(w_up, (1 - side) * hidden_half, hidden_half, 1), core)

    source = ordered(inputs, inputs_other, side).astype(F32)
    qkv_w = ordered(pair_columns(side), qkv_other, side)
    up_w = ordered(rows_of(w_up, side * hidden_half, hidden_half, 1), up_other, side)
    upstream = ordered(grad_output, grad_other, side)
    chosen = ordered(expert_choice, choice_other, side)[:, 0]

    onehot = (chosen[:, None] == jnp.arange(experts, dtype=jnp.int32)[None, :]).astype(jnp.int32)
    running = jnp.cumsum(onehot.reshape(2, tokens, experts), axis=1).reshape(2 * tokens, experts)
    place = chosen * room + jnp.sum(onehot * running, axis=1) - 1
    slots = experts * room
    hit = jnp.arange(slots, dtype=jnp.int32)[None, :, None] == place.reshape(2, 1, tokens)
    placing = hit.astype(BF)

    def dispatch(rows):
        return jnp.einsum(
            "bst,btd->bsd", placing, rows.reshape(2, tokens, width), preferred_element_type=F32
        )

    def collect(arrived):
        rows = arrived.reshape(experts, 2, room, width)
        return jnp.einsum(
            "bst,sbd->btd",
            placing,
            rows.transpose(0, 2, 1, 3).reshape(slots, 2, width),
            preferred_element_type=F32,
        ).reshape(2 * tokens, width)

    def exchange(rows):
        return lax.all_to_all(
            rows.reshape(owners, 2 * room, width), "ep", split_axis=0, concat_axis=0, tiled=True
        )

    pad_row = jnp.arange(room, dtype=jnp.int32)[None, None, :, None] - capacity

    def with_scalars(rows, scalars):
        wide = [
            jnp.pad(piece, ((0, 0), (0, 0), (0, width - room)))[:, :, None, :]
            for piece in pieces(scalars)
        ]
        for at, piece in enumerate(wide):
            rows = jnp.where(pad_row == at, piece, rows)
        return rows.astype(BF)

    def scalars_of(rows):
        spare = rows[:, :, capacity : capacity + 3, :room].astype(F32)
        return spare[:, :, 0] + spare[:, :, 1] + spare[:, :, 2]

    def to_owner(rows):
        return rows.reshape(2, owners, room, -1).transpose(1, 0, 2, 3)

    grad_slots = exchange(to_owner(dispatch(upstream)).astype(BF))

    first = layer_norm(source, pre_gain, pre_shift).astype(BF)
    qkv = matmul(first, qkv_w).astype(BF)
    attended, lse = attend(qkv)
    attended_other = swap(attended)
    resid = source + matmul(attended, w_output) + matmul(attended_other, output_other)
    second = layer_norm(resid, mid_gain, mid_shift).astype(BF)
    small_w = jnp.concatenate([w_router, w_mix], 1)
    logits = matmul(second, small_w)
    route_probs = jax.nn.softmax(logits[:, :experts], axis=-1)
    mask = onehot.astype(F32)
    gate = jnp.sum(route_probs * mask, axis=-1, keepdims=True)
    mix = jax.nn.softmax(logits[:, experts:], axis=-1)
    coef = mix[:, 1:2] * gate

    coef_slots = jnp.sum(
        jnp.where(hit, coef.reshape(2, 1, tokens), 0.0), axis=-1
    )
    sent = with_scalars(
        to_owner(dispatch(second)), coef_slots.reshape(2, owners, room).transpose(1, 0, 2)
    )
    arrived = exchange(sent)

    up_pre = matmul(second, up_w)
    hidden = gelu_tanh(up_pre).astype(BF)
    dense = matmul(hidden, w_down)
    up32 = upstream.astype(F32)
    d_dense = (mix[:, 0:1] * up32).astype(BF)
    d_up = jax.vjp(gelu_tanh, up_pre)[1](matmul_nt(d_dense, w_down))[0].astype(BF)
    grad_down = matmul_tn(hidden, d_dense)
    grad_up = matmul_tn(second, d_up)

    count = owners * 2 * room
    coef_there = scalars_of(arrived.reshape(owners, 2, room, width)).reshape(count, 1)
    gathered = arrived.reshape(count, width)
    grad_there = grad_slots.reshape(count, width)
    expert_pre = matmul(gathered, expert_up[0])
    expert_hidden = gelu_tanh(expert_pre).astype(BF)
    expert_out = matmul(expert_hidden, expert_down[0])
    d_routed = (coef_there * grad_there.astype(F32)).astype(BF)
    d_expert_pre = jax.vjp(gelu_tanh, expert_pre)[1](matmul_nt(d_routed, expert_down[0]))[0]
    d_expert_pre = d_expert_pre.astype(BF)
    along = jnp.sum(grad_there.astype(F32) * expert_out, axis=-1)
    d_slots = matmul_nt(d_expert_pre, expert_up[0])
    back = exchange(
        with_scalars(d_slots.reshape(owners, 2, room, width), along.reshape(owners, 2, room))
    )
    out_back = exchange(expert_out.astype(BF))
    grad_expert_down = matmul_tn(expert_hidden, d_routed)[None]
    grad_expert_up = matmul_tn(gathered, d_expert_pre)[None]

    back_rows = back.reshape(owners, 2, room, width)
    along_here = jnp.sum(
        jnp.where(
            hit, scalars_of(back_rows).transpose(1, 0, 2).reshape(2, slots, 1), 0.0
        ),
        axis=1,
    ).reshape(2 * tokens, 1)
    along_dense = jnp.sum(up32 * dense, axis=-1, keepdims=True)
    d_gate = mix[:, 1:2] * along_here
    d_both = jnp.concatenate([along_dense, gate * along_here], 1)
    d_route = route_probs * (mask * d_gate - gate * d_gate)
    d_mix = mix * (d_both - jnp.sum(mix * d_both, axis=-1, keepdims=True))
    d_small = jnp.concatenate([d_route, d_mix], 1).astype(BF)
    grad_small = matmul_tn(second, d_small)

    d_second = matmul_nt(d_up, up_w) + matmul_nt(d_small, small_w) + collect(back)
    theirs = swap(rows_of(d_second, (1 - side) * tokens, tokens).astype(BF))
    d_second = rows_of(d_second, side * tokens, tokens) + theirs.astype(F32)
    d_resid_mid, grad_mid_gain, grad_mid_shift = jax.vjp(
        layer_norm, rows_of(resid, side * tokens, tokens), mid_gain, mid_shift
    )[1](d_second)
    d_resid = grad_output.astype(F32) + d_resid_mid
    d_attn_own = d_resid.astype(BF)
    d_attn = ordered(d_attn_own, swap(d_attn_own), side)
    grad_out_w = matmul_tn(attended, d_attn)
    d_attended = matmul_nt(d_attn, w_output).astype(BF)
    d_qkv = attend_back(qkv, attended, lse, d_attended)
    grad_qkv = matmul_tn(first, d_qkv)
    d_first = matmul_nt(d_qkv, qkv_w)
    theirs = swap(rows_of(d_first, (1 - side) * tokens, tokens).astype(BF))
    d_first = rows_of(d_first, side * tokens, tokens) + theirs.astype(F32)
    d_source, grad_pre_gain, grad_pre_shift = jax.vjp(
        layer_norm, inputs.astype(F32), pre_gain, pre_shift
    )[1](d_first)
    grad_inputs = d_resid + d_source

    mixed = mix[:, 0:1] * dense + coef * collect(out_back)
    theirs = swap(rows_of(mixed, (1 - side) * tokens, tokens).astype(BF))
    output = (
        rows_of(resid, side * tokens, tokens)
        + rows_of(mixed, side * tokens, tokens)
        + theirs.astype(F32)
    ).astype(BF)

    def reduce_rows(value):
        return lax.psum_scatter(value, "ep", scatter_dimension=0, tiled=True)

    up_rows = reduce_rows(grad_up.astype(BF))
    down_rows = reduce_rows(
        jnp.concatenate(
            [
                grad_down.astype(BF).reshape(owners, -1, width),
                grad_out_w.astype(BF).reshape(owners, -1, width),
            ],
            1,
        ).reshape(-1, width)
    )
    vectors = jnp.stack([grad_pre_gain, grad_pre_shift, grad_mid_gain, grad_mid_shift], 1)
    extra = jnp.concatenate([vectors, grad_small], 1)
    last_rows = reduce_rows(jnp.concatenate([grad_qkv, extra], 1).astype(BF))
    small_rows = last_rows[:, 3 * half :]
    mine = last_rows.shape[0] // 2

    def trade(rows):
        return rows_of(rows, side * mine, mine), swap(rows_of(rows, (1 - side) * mine, mine))

    up_own, up_theirs = trade(up_rows)
    grad_up_out = ordered(up_own, up_theirs, side, 1).astype(F32)
    last_own, last_theirs = trade(last_rows)

    def split_qkv(rows):
        rows = rows[:, : 3 * half].reshape(mine, pairs, 3, LANES)
        return [rows[:, :, at].reshape(mine, half) for at in range(3)]

    qkv_outs = [
        ordered(a, b, side, 1).astype(F32)
        for a, b in zip(split_qkv(last_own), split_qkv(last_theirs))
    ]
    extra_out = last_own[:, 3 * half :].astype(F32) + last_theirs[:, 3 * half :].astype(F32)
    route = [(2 * j + s, owners * s + j) for j in range(owners) for s in range(2)]
    down_rows = lax.ppermute(down_rows, ("ep", "es"), route).astype(F32)
    per_down = hidden_half // owners
    return (
        output,
        grad_inputs,
        extra_out[:, 0],
        extra_out[:, 1],
        qkv_outs[0],
        qkv_outs[1],
        qkv_outs[2],
        down_rows[per_down:],
        extra_out[:, 2],
        extra_out[:, 3],
        grad_up_out,
        down_rows[:per_down],
        extra_out[:, 4 : 4 + experts],
        extra_out[:, 4 + experts :],
        grad_expert_up,
        grad_expert_down,
    )


def solution(mesh):
    placed = (
        P(("ep", "es"), None),
        P(("ep", "es"), None),
        P(("ep", "es"), None),
        P(),
        P(),
        P("es", None),
        P("es", None),
        P("es", None),
        P("es", None),
        P(),
        P(),
        P("es", None),
        P("es", None),
        P(),
        P(),
        P("ep", None, "es"),
        P("ep", "es", None),
    )
    return jax.shard_map(
        body,
        mesh=mesh,
        in_specs=placed,
        out_specs=(
            P(("ep", "es"), None),
            P(("ep", "es"), None),
            P(("ep", "es")),
            P(("ep", "es")),
            P(("ep", "es"), None),
            P(("ep", "es"), None),
            P(("ep", "es"), None),
            P(("ep", "es"), None),
            P(("ep", "es")),
            P(("ep", "es")),
            P(("ep", "es"), None),
            P(("ep", "es"), None),
            P(("ep", "es"), None),
            P(("ep", "es"), None),
            P("ep", None, "es"),
            P("ep", "es", None),
        ),
        check_vma=False,
    )
```

time: 2430 us -> 854 us (0.35)
  waiting for transfers between devices: 1850 us -> 394 us
  matrix products: 276 us -> 176 us
  blocking collectives: 127 us -> 74.3 us
  Pallas kernels: 0 us -> 38.4 us
    reduce_scatter x8 -> x3, waiting for transfers between devices: 1270 us -> 90.7 us  [reduce_rows(): return lax.psum_scatter(value, 'ep', scatter_dimension=0, tiled=True)]
    all_gather x8 -> x0, waiting for transfers between devices: 378 us -> none  [the longest x1 94.6 us: body(): lax.all_gather(w_up, 'es', axis=0, tiled=True)]
    dot_general x18 -> x12, matrix products: 146 us -> 64.2 us  [the longest x8 54.6 us: matmul(): return jnp.dot(left, right, preferred_element_type=F32)]
    all_to_all x2 -> x3, waiting for transfers between devices: 40.7 us -> 118 us  [exchange(): lax.all_to_all(rows.reshape(owners, 2 * room, width), 'ep', split_axis=0,...]
    unnamed x1 -> x0, blocking collectives: 46.2 us -> none
    pallas_call x0 -> x2, Pallas kernels: none -> 38.4 us  [the longest x1 19.7 us: attend_back(): pl.pallas_call(attend_back_kernel, grid=(pairs,), in_specs=[wide, slim, s...]
    ppermute x2 -> x17, waiting for transfers between devices: 153 us -> 185 us  [the longest x13 165 us: swap(): return lax.ppermute(value, 'es', [(0, 1), (1, 0)])]
    dot_general x8 -> x7, matrix products: 65.6 us -> 53.8 us  [matmul_tn(): lax.dot_general(left, right, (((0,), (0,)), ((), ())), preferred_element_...]
  transfers between devices with their start and end apart: 22 -> 23, of which waited for: 17 -> 16; matrix products, arithmetic and copies ran while one was open for 13% -> 21% of each run, Pallas kernels for 0% -> 5%
where the time goes in v1:
time: 854 us; the launch traced here: 844 us
  waiting for transfers between devices  394 us (46%)
  matrix products  176 us (21%)
  blocking collectives  74.3 us (9%)
  other arithmetic  54.8 us (6%)
  local copies, waits for them, and re-layouts  52.2 us (6%)
  starting transfers between devices  39.4 us (5%)
  Pallas kernels  38.4 us (4%)
  between operations  15.4 us (2%)
    ppermute x13, waiting for transfers between devices, swap(): return lax.ppermute(value, 'es', [(0, 1), (1, 0)])  165 us
    all_to_all x3, waiting for transfers between devices, exchange(): lax.all_to_all(rows.reshape(owners, 2 * room, width), 'ep', split_axis=0,...  118 us
    reduce_scatter x3, waiting for transfers between devices, reduce_rows(): return lax.psum_scatter(value, 'ep', scatter_dimension=0, tiled=True)  90.7 us
    all_to_all x1, blocking collectives, exchange(): lax.all_to_all(rows.reshape(owners, 2 * room, width), 'ep', split_axis=0,...  74.3 us
    dot_general x7, matrix products, matmul_nt(): lax.dot_general(left, right, (((1,), (1,)), ((), ())), preferred_element_...  58.3 us
    dot_general x8, matrix products, matmul(): return jnp.dot(left, right, preferred_element_type=F32)  54.6 us
    dot_general x7, matrix products, matmul_tn(): lax.dot_general(left, right, (((0,), (0,)), ((), ())), preferred_element_...  53.8 us
    all_to_all x3, starting transfers between devices, exchange(): lax.all_to_all(rows.reshape(owners, 2 * room, width), 'ep', split_axis=0,...  20 us
  transfers between devices with their start and end apart: 23, of which 16 were waited for; matrix products, arithmetic and copies ran while one was open for 21% of the time, Pallas kernels for 5%

profile of v1, /device:TPU:18, one launch (start us, length us, event | category | flops | bytes accessed | tf_op | source)
XLA Modules:
  0.0 844.5 jit_solution(3342097321833785408)
XLA Ops:
  11.6 2.1 constant_dynamic-slice_fusion.7
  21.1 2.0 copy.71
  24.4 2.5 pad_maximum_fusion.13
  28.2 2.3 reduce-window.6
  30.5 32.1 %collective-permute-done.1 = bf16[256,1536]{0,1:T(8,128)(2,1)} collective-permute-done((bf16[256,1536]{0,1:T(8,128)(2,1)}, bf16[256,1536]{0,1:T(8,128)(2,1)}, u32[]{:S(2)}, u32[]{:S(2)}) %collective-permute-start.1) | collective-permute-done | bytes 786464 | tf_op jit(solution)/shard_map/ppermute | solution.py:40
  68.9 5.3 convolution_convert_fusion.1.qkv_ref
  74.2 18.7 %attend.1 = (bf16[1024,512]{1,0:T(8,128)(2,1)}, f32[1024,512]{1,0:T(8,128)}) custom-call(bf16[1024,1536]{1,0:T(8,128)(2,1)} %convolution_convert_fusion.1.qkv_ref), custom_call_target="tpu_custom_call" | custom-call | tf_op jit(solution)/shard_map/attend/pallas_call | solution.py:140
  96.1 2.6 fusion.115
  98.7 20.1 %collective-permute-done.3 = bf16[1024,512]{1,0:T(8,128)(2,1)} collective-permute-done((bf16[1024,512]{1,0:T(8,128)(2,1)}, bf16[1024,512]{1,0:T(8,128)(2,1)}, u32[]{:S(2)}, u32[]{:S(2)}) %collective-permute-start.3) | collective-permute-done | bytes 1048608 | tf_op jit(solution)/shard_map/ppermute | solution.py:40
  118.8 2.6 fusion.114
  126.1 1.9 fusion.45
  128.0 2.2 fusion.19
  130.3 6.1 all-to-all-start
  137.8 24.0 %collective-permute-done.10 = bf16[512,1024]{1,0:T(8,128)(2,1)S(1)} collective-permute-done((bf16[512,1024]{1,0:T(8,128)(2,1)}, bf16[512,1024]{1,0:T(8,128)(2,1)S(1)}, u32[]{:S(2)}, u32[]{:S(2)}) %collective-permute-start.10) | collective-permute-done | bytes 1048608 | tf_op jit(solution)/shard_map/ppermute | solution.py:40
  163.3 1.9 fusion.52
  165.3 2.1 copy.86
  167.4 37.3 %all-to-all-done = bf16[16,96,1024]{2,1,0:T(8,128)(2,1)} async-done(((bf16[16,96,1024]{2,1,0:T(8,128)(2,1)}), bf16[16,96,1024]{2,1,0:T(8,128)(2,1)}, u32[]{:S(2)}, u32[]{:S(2)}) %all-to-all-start) | async-done | bytes 3145760 | tf_op jit(solution)/shard_map/all_to_all | solution.py:249
  204.8 7.0 all-to-all-start.2
  213.5 12.1 %fusion.38 = f32[1536,2048]{1,0:T(8,128)} fusion(bf16[1536,1024]{1,0:T(8,128)(2,1)} %bitcast.19, bf16[1,1024,2048]{2,1,0:T(8,128)(2,1)} %param.32), kind=kOutput, calls=%fused_computation.58 | convolution fusion | flops 6442450944 | bytes 19922944 | tf_op jit(solution)/shard_map/dot_general | solution.py:28
  225.6 54.4 %all-to-all-done.2 = bf16[16,96,1024]{2,1,0:T(8,128)(2,1)} async-done(((bf16[16,96,1024]{2,1,0:T(8,128)(2,1)}), bf16[16,96,1024]{2,1,0:T(8,128)(2,1)}, u32[]{:S(2)}, u32[]{:S(2)}) %all-to-all-start.2) | async-done | bytes 3145760 | tf_op jit(solution)/shard_map/all_to_all | solution.py:249
  280.0 2.6 fusion.14
  283.1 17.0 %fusion.6 = bf16[1536,2048]{1,0:T(8,128)(2,1)} fusion(f32[1536,2048]{1,0:T(8,128)} %fusion.38, bf16[1536,1024]{1,0:T(8,128)(2,1)S(1)} %bitcast.188, bf16[1,2048,1024]{2,1,0:T(8,128)(2,1)S(1)} %copy-done.50), kind=kOutput, calls=%fused_computation.8 | convolution fusion | flops 6505365504 | bytes 26214400 | tf_op jit(solution)/shard_map/dot_general | solution.py:32
  300.1 13.6 %fusion.15 = (f32[1536]{0:T(1024)S(1)}, bf16[1536,1024]{1,0:T(8,128)(2,1)}, bf16[1536,1024]{1,0:T(8,128)(2,1)}) fusion(bf16[16,96,1024]{2,1,0:T(8,128)(2,1)} %all-to-all-done.2, f32[1536]{0:T(1024)S(1)} %add.264, bf16[1,2048,1024]{2,1,0:T(8,128)(2,1)S(1)} %copy-done.50, f32[1536,2048]{1,0:T(8,128)} %fusion.38), kind=kOutput, calls=%fused_computation.24 | convolution fusion | flops 6480198144 | bytes 26226688 | tf_op jit(solution)/shard_map/dot_general | solution.py:28
  314.0 10.4 %select_convert_fusion = bf16[16,2,48,1024]{3,2,1,0:T(8,128)(2,1)S(1)} fusion(bf16[16,2,48,2048]{3,2,1,0:T(8,128)(2,1)} %bitcast.227, bf16[1,1024,2048]{2,1,0:T(8,128)(2,1)} %param.32, bf16[16,2,1024]{2,1,0:T(2,128)(2,1)S(1)} %pad.24, bf16[16,2,1024]{2,1,0:T(2,128)(2,1)S(1)} %pad.23, bf16[16,2,1024]{2,1,0:T(2,128)(2,1)S(1)} %pad.22, ...), kind=kOutput, calls=%fused_computation.30 | convolution fusion | flops 6447169536 | bytes 13828240 | tf_op jit(solution)/shard_map/dot_general | solution.py:32
  324.4 74.3 %all_to_all.20 = bf16[16,96,1024]{2,1,0:T(8,128)(2,1)} all-to-all(bf16[16,96,1024]{2,1,0:T(8,128)(2,1)S(1)} %bitcast.185), channel_id=1, replica_groups=mesh['ep'=16,'es'=2] {'ep'}, dimensions={0} | all-to-all | bytes 6291456 | tf_op jit(solution)/shard_map/all_to_all | solution.py:249
  398.7 6.8 all-to-all-start.1
  408.9 23.8 %collective-permute-done.6 = bf16[256,2048]{1,0:T(8,128)(2,1)} collective-permute-done((bf16[256,2048]{1,0:T(8,128)(2,1)S(1)}, bf16[256,2048]{1,0:T(8,128)(2,1)}, u32[]{:S(2)}, u32[]{:S(2)}) %collective-permute-start.6) | collective-permute-done | bytes 1048608 | tf_op jit(solution)/shard_map/ppermute | solution.py:40
  432.8 3.0 collective-permute-done.7
  438.9 6.7 fusion.47
  445.6 2.1 copy.89
  447.8 26.2 %all-to-all-done.1 = bf16[16,96,1024]{2,1,0:T(8,128)(2,1)} async-done(((bf16[16,96,1024]{2,1,0:T(8,128)(2,1)}), bf16[16,96,1024]{2,1,0:T(8,128)(2,1)}, u32[]{:S(2)}, u32[]{:S(2)}) %all-to-all-start.1) | async-done | bytes 3145760 | tf_op jit(solution)/shard_map/all_to_all | solution.py:249
  473.9 2.4 copy.84
  476.3 3.9 fusion.44
  481.0 15.0 %fusion.13 = bf16[1024,2048]{1,0:T(8,128)(2,1)} fusion(f32[1024,2048]{1,0:T(8,128)} %fusion.47, bf16[2048,1024]{1,0:T(8,128)(2,1)} %param.29, f32[1024]{0:T(1024)S(1)} %bitcast.224, bf16[512,1024]{1,0:T(8,128)(2,1)} %copy-done.22, bf16[512,1024]{1,0:T(8,128)(2,1)} %copy-done.19), kind=kOutput, calls=%fused_computation.18 | convolution fusion | flops 4343201792 | bytes 18878464 | tf_op jit(solution)/shard_map/dot_general | solution.py:32
  496.0 11.1 %fusion.27 = (f32[1024]{0:T(1024)S(1)}, f32[1024,1024]{1,0:T(8,128)}) fusion(bf16[512,1024]{1,0:T(8,128)(2,1)S(1)} %copy-done.23, bf16[512,1024]{1,0:T(8,128)(2,1)S(1)} %copy-done.20, f32[2,512,1024]{2,1,0:T(8,128)S(1)} %copy-done.54, f32[1024]{0:T(1024)S(1)} %bitcast.223, f32[1024]{0:T(1024)S(1)} %bitcast.225, bf16[2048,1024]{1,0:T(8,128)(2,1)S(1)} %copy-done.51, ...), kind=kOutput, calls=%fused_computation.46 | convolution fusion | flops 4323277824 | bytes 23080960 | tf_op jit(solution)/shard_map/dot_general | solution.py:28
  507.2 1.8 fusion.42
  511.3 6.7 bitcast_add_fusion
  518.1 1.9 copy-done.16
  522.6 8.3 convolution_convert_fusion.2
  530.9 1.9 dynamic-slice_reduce_fusion
  535.7 11.8 %collective-permute-done.11 = bf16[512,1024]{1,0:T(8,128)(2,1)} collective-permute-done((bf16[512,1024]{1,0:T(8,128)(2,1)}, bf16[512,1024]{1,0:T(8,128)(2,1)}, u32[]{:S(2)}, u32[]{:S(2)}) %collective-permute-start.11) | collective-permute-done | bytes 1048608 | tf_op jit(solution)/shard_map/ppermute | solution.py:40
  547.5 3.0 multiply_reduce_fusion.1
  550.5 17.9 %collective-permute-done.9 = bf16[512,1024]{1,0:T(8,128)(2,1)S(1)} collective-permute-done((bf16[512,1024]{1,0:T(8,128)(2,1)S(1)}, bf16[512,1024]{1,0:T(8,128)(2,1)S(1)}, u32[]{:S(2)}, u32[]{:S(2)}) %collective-permute-start.9) | collective-permute-done | bytes 1048608 | tf_op jit(solution)/shard_map/ppermute | solution.py:40
  568.4 4.0 fusion.109
  575.0 21.6 %collective-permute-done.12 = bf16[512,1024]{1,0:T(8,128)(2,1)S(1)} collective-permute-done((bf16[512,1024]{1,0:T(8,128)(2,1)S(1)}, bf16[512,1024]{1,0:T(8,128)(2,1)S(1)}, u32[]{:S(2)}, u32[]{:S(2)}) %collective-permute-start.12) | collective-permute-done | bytes 1048608 | tf_op jit(solution)/shard_map/ppermute | solution.py:40
  597.7 2.2 convolution_convert_fusion.5.grad_ref
  600.0 19.7 %attend_back.1 = bf16[1024,1536]{1,0:T(8,128)(2,1)} custom-call(bf16[1024,1536]{1,0:T(8,128)(2,1)} %convolution_convert_fusion.1.qkv_ref, bf16[1024,512]{1,0:T(8,128)(2,1)} %get-tuple-element.18.out_ref, f32[1024,512]{1,0:T(8,128)} %get-tuple-element.19.lse_ref, bf16[1024,512]{1,0:T(8,128)(2,1)} %convolution_convert_fusion.5.grad_ref), custom_call_target="tpu_custom_call" | custom-call | tf_op jit(solution)/shard_map/attend_back/pallas_call | solution.py:158
  619.7 6.2 fusion.57
  625.9 1.9 copy-done.13
  632.9 8.1 convolution_convert_fusion
  641.0 11.5 %collective-permute-done.13 = bf16[512,1024]{1,0:T(8,128)(2,1)} collective-permute-done((bf16[512,1024]{1,0:T(8,128)(2,1)}, bf16[512,1024]{1,0:T(8,128)(2,1)}, u32[]{:S(2)}, u32[]{:S(2)}) %collective-permute-start.13) | collective-permute-done | bytes 1048608 | tf_op jit(solution)/shard_map/ppermute | solution.py:40
  652.5 2.2 fusion.56
  656.5 6.8 concatenate.76
  663.7 10.0 %convolution_convert_fusion.3 = bf16[2048,1024]{1,0:T(8,128)(2,1)S(1)} fusion(f32[1024]{0:T(1024)S(1)} %bitcast.226, bf16[512,1024]{1,0:T(8,128)(2,1)} %copy-done.22, bf16[512,1024]{1,0:T(8,128)(2,1)S(1)} %copy-done.21, f32[1024,2048]{1,0:T(8,128)} %fusion.47), kind=kOutput, calls=%fused_computation.65 | convolution fusion | flops 4322230272 | bytes 14684160 | tf_op jit(solution)/shard_map/dot_general | solution.py:36
  675.0 2.9 pad_maximum_fusion
  677.9 12.5 %convolution_bitcast_fusion.1 = f32[1,1024,2048]{2,1,0:T(8,128)} fusion(bf16[1536,1024]{1,0:T(8,128)(2,1)} %bitcast.19, bf16[1536,2048]{1,0:T(8,128)(2,1)} %fusion.6), kind=kOutput, calls=%fused_computation.40 | convolution fusion | flops 6442450944 | bytes 17825792 | tf_op jit(solution)/shard_map/dot_general | solution.py:36
  690.4 13.3 %convolution_bitcast_fusion = f32[1,2048,1024]{2,1,0:T(8,128)} fusion(bf16[1536,1024]{1,0:T(8,128)(2,1)S(1)} %copy-done.55, f32[1536,2048]{1,0:T(8,128)} %fusion.38), kind=kOutput, calls=%fused_computation.39 | convolution fusion | flops 6470762496 | bytes 24117248 | tf_op jit(solution)/shard_map/dot_general | solution.py:36
  703.7 3.5 fusion.108
  709.6 4.0 add_add_fusion.2
  714.4 19.2 %reduce-scatter.4.cloned.1.call-done = bf16[64,1558]{1,0:T(8,128)(2,1)} async-done(((bf16[1024,1558]{1,0:T(8,128)(2,1)}), bf16[64,1558]{1,0:T(8,128)(2,1)}) %reduce-scatter.4.cloned.1.call-update) | async-done | bytes 199440 | tf_op jit(solution)/shard_map/reduce_scatter | solution.py:368
  737.1 2.3 collective-permute-done.14
  743.5 71.5 %reduce-scatter.6.cloned.1.call-done = bf16[160,1024]{1,0:T(8,128)(2,1)} async-done(((bf16[2560,1024]{1,0:T(8,128)(2,1)}), bf16[160,1024]{1,0:T(8,128)(2,1)}) %reduce-scatter.6.cloned.1.call-update) | async-done | bytes 327696 | tf_op jit(solution)/shard_map/reduce_scatter | solution.py:368
  815.1 1.9 collective-permute-start.15
  819.0 17.0 %collective-permute-done.15 = bf16[160,1024]{1,0:T(8,128)(2,1)S(1)} collective-permute-done((bf16[160,1024]{1,0:T(8,128)(2,1)}, bf16[160,1024]{1,0:T(8,128)(2,1)S(1)}, u32[]{:S(2)}, u32[]{:S(2)}) %collective-permute-start.15) | collective-permute-done | bytes 327712 | tf_op jit(solution)/shard_map/ppermute | solution.py:403
  (267 shorter events, 75.1 us)
Async XLA Ops:
  7.2 19.7 %collective-permute-start.8 = (s32[512,1]{0,1:T(1,128)}, s32[512,1]{0,1:T(1,128)S(1)}, u32[]{:S(2)}, u32[]{:S(2)}) collective-permute-start(s32[512,1]{0,1:T(1,128)} %param.19), channel_id=1, source_target_pairs={{0,1},{1,0},{2,3},{3,2},{4,5},{5,4},{6,7},{7,6},{8,9},{9,8},{10,11... | collective-permute-start | bytes 6152 | tf_op jit(solution)/shard_map/ppermute | solution.py:40
  9.6 20.8 %collective-permute-start.4 = (bf16[256,1024]{1,0:T(8,128)(2,1)}, bf16[256,1024]{1,0:T(8,128)(2,1)}, u32[]{:S(2)}, u32[]{:S(2)}) collective-permute-start(bf16[256,1024]{1,0:T(8,128)(2,1)} %constant_dynamic-slice_fusion.3), channel_id=1, source_target_pairs={{0,1},{1,0},{2,3},{3,2},{4,5},{5,4},{6,7},{7,6},{8,9},{9,8},{10,11... | collective-permute-start | bytes 1572872 | tf_op jit(solution)/shard_map/ppermute | solution.py:40
  10.8 51.9 %collective-permute-start = (bf16[512,1024]{1,0:T(8,128)(2,1)}, bf16[512,1024]{1,0:T(8,128)(2,1)}, u32[]{:S(2)}, u32[]{:S(2)}) collective-permute-start(bf16[512,1024]{1,0:T(8,128)(2,1)} %param.17), channel_id=1, source_target_pairs={{0,1},{1,0},{2,3},{3,2},{4,5},{5,4},{6,7},{7,6},{8,9},{9,8},{10,11... | collective-permute-start | bytes 3145736 | tf_op jit(solution)/shard_map/ppermute | solution.py:40
  16.4 4.7 copy-start.40
  17.6 6.8 copy-start.46
  19.0 8.0 copy-start.49
  19.0 43.7 %copy-start.3 = (bf16[512,1024]{1,0:T(8,128)(2,1)S(1)}, bf16[512,1024]{1,0:T(8,128)(2,1)}, u32[]{:S(2)}) copy-start(bf16[512,1024]{1,0:T(8,128)(2,1)} %param.17) | copy-start | bytes 3145732
  19.9 42.7 %collective-permute-start.1 = (bf16[256,1536]{0,1:T(8,128)(2,1)}, bf16[256,1536]{0,1:T(8,128)(2,1)}, u32[]{:S(2)}, u32[]{:S(2)}) collective-permute-start(bf16[256,1536]{0,1:T(8,128)(2,1)} %constant_dynamic-slice_fusion.4), channel_id=1, source_target_pairs={{0,1},{1,0},{2,3},{3,2},{4,5},{5,4},{6,7},{7,6},{8,9},{9,8},{10,11... | collective-permute-start | bytes 2359304 | tf_op jit(solution)/shard_map/ppermute | solution.py:40
  30.5 64.4 %collective-permute-start.5 = (bf16[256,1024]{1,0:T(8,128)(2,1)}, bf16[256,1024]{1,0:T(8,128)(2,1)}, u32[]{:S(2)}, u32[]{:S(2)}) collective-permute-start(bf16[256,1024]{1,0:T(8,128)(2,1)} %collective-permute-done.4), channel_id=1, source_target_pairs={{0,2},{2,0},{4,6},{6,4},{8,10},{10,8},{12,14},{14,12},{16,18},{18,... | collective-permute-start | bytes 1572872 | tf_op jit(solution)/shard_map/ppermute | solution.py:45
  62.6 2.5 collective-permute-start.2
  64.0 3.3 copy-start.8
  64.0 54.8 %copy-start.7 = (bf16[512,1024]{1,0:T(8,128)(2,1)}, bf16[512,1024]{1,0:T(8,128)(2,1)S(1)}, u32[]{:S(2)}) copy-start(bf16[512,1024]{1,0:T(8,128)(2,1)S(1)} %get-tuple-element.112) | copy-start | bytes 3145732
  64.0 2.5 copy-start.18
  64.4 2.9 copy-start.41
  65.1 3.8 copy-start.43
  65.1 3.8 copy-start.52
  92.8 25.9 %collective-permute-start.3 = (bf16[1024,512]{1,0:T(8,128)(2,1)}, bf16[1024,512]{1,0:T(8,128)(2,1)}, u32[]{:S(2)}, u32[]{:S(2)}) collective-permute-start(bf16[1024,512]{1,0:T(8,128)(2,1)} %get-tuple-element.18.out_ref), channel_id=1, source_target_pairs={{0,1},{1,0},{2,3},{3,2},{4,5},{5,4},{6,7},{7,6},{8,9},{9,8},{10,11... | collective-permute-start | bytes 3145736 | tf_op jit(solution)/shard_map/ppermute | solution.py:40
  96.1 22.7 %copy-start.9 = (bf16[512,1024]{1,0:T(8,128)(2,1)S(1)}, bf16[512,1024]{1,0:T(8,128)(2,1)}, u32[]{:S(2)}) copy-start(bf16[512,1024]{1,0:T(8,128)(2,1)} %copy-done.8) | copy-start | bytes 3145732
  130.3 74.5 %all-to-all-start = ((bf16[16,96,1024]{2,1,0:T(8,128)(2,1)}), bf16[16,96,1024]{2,1,0:T(8,128)(2,1)}, u32[]{:S(2)}, u32[]{:S(2)}) async-start(bf16[16,96,1024]{2,1,0:T(8,128)(2,1)} %bitcast.179), calls=%async_computation | async-start | bytes 6291456 | tf_op jit(solution)/shard_map/all_to_all | solution.py:249
  136.4 25.4 %collective-permute-start.10 = (bf16[512,1024]{1,0:T(8,128)(2,1)}, bf16[512,1024]{1,0:T(8,128)(2,1)S(1)}, u32[]{:S(2)}, u32[]{:S(2)}) collective-permute-start(bf16[512,1024]{1,0:T(8,128)(2,1)} %param.18), channel_id=1, source_target_pairs={{0,1},{1,0},{2,3},{3,2},{4,5},{5,4},{6,7},{7,6},{8,9},{9,8},{10,11... | collective-permute-start | bytes 3145736 | tf_op jit(solution)/shard_map/ppermute | solution.py:40
  204.8 75.2 %all-to-all-start.2 = ((bf16[16,96,1024]{2,1,0:T(8,128)(2,1)}), bf16[16,96,1024]{2,1,0:T(8,128)(2,1)}, u32[]{:S(2)}, u32[]{:S(2)}) async-start(bf16[16,96,1024]{2,1,0:T(8,128)(2,1)} %bitcast.180), calls=%async_computation.2 | async-start | bytes 6291456 | tf_op jit(solution)/shard_map/all_to_all | solution.py:249
  280.0 3.1 copy-start.50
  398.7 75.2 %all-to-all-start.1 = ((bf16[16,96,1024]{2,1,0:T(8,128)(2,1)}), bf16[16,96,1024]{2,1,0:T(8,128)(2,1)}, u32[]{:S(2)}, u32[]{:S(2)}) async-start(bf16[16,96,1024]{2,1,0:T(8,128)(2,1)} %bitcast.183), calls=%async_computation.1 | async-start | bytes 6291456 | tf_op jit(solution)/shard_map/all_to_all | solution.py:249
  405.6 301.6 %reduce-scatter.8.cloned.1.call-start = ((), (), s32[]{:S(2)}) async-start(), calls=%async_computation.9 | async-start | bytes 4456448 | tf_op jit(solution)/shard_map/reduce_scatter | solution.py:368
  407.4 25.3 %collective-permute-start.6 = (bf16[256,2048]{1,0:T(8,128)(2,1)S(1)}, bf16[256,2048]{1,0:T(8,128)(2,1)}, u32[]{:S(2)}, u32[]{:S(2)}) collective-permute-start(bf16[256,2048]{1,0:T(8,128)(2,1)S(1)} %dynamic_slice.75), channel_id=1, source_target_pairs={{0,1},{1,0},{2,3},{3,2},{4,5},{5,4},{6,7},{7,6},{8,9},{9,8},{10,11... | collective-permute-start | bytes 3145736 | tf_op jit(solution)/shard_map/ppermute | solution.py:40
  432.8 3.0 collective-permute-start.7
  432.8 4.7 copy-start.25
  438.9 6.8 copy-start.26
  438.9 6.7 copy-start.28
  438.9 6.7 copy-start.10
  481.0 15.0 %copy-start.20 = (bf16[512,1024]{1,0:T(8,128)(2,1)S(1)}, bf16[512,1024]{1,0:T(8,128)(2,1)}, u32[]{:S(2)}) copy-start(bf16[512,1024]{1,0:T(8,128)(2,1)} %copy-done.19) | copy-start | bytes 3145732
  481.0 15.0 %copy-start.23 = (bf16[512,1024]{1,0:T(8,128)(2,1)S(1)}, bf16[512,1024]{1,0:T(8,128)(2,1)}, u32[]{:S(2)}) copy-start(bf16[512,1024]{1,0:T(8,128)(2,1)} %copy-done.22) | copy-start | bytes 3145732
  481.0 15.0 %copy-start.51 = (bf16[2048,1024]{1,0:T(8,128)(2,1)S(1)}, bf16[2048,1024]{1,0:T(8,128)(2,1)}, u32[]{:S(2)}) copy-start(bf16[2048,1024]{1,0:T(8,128)(2,1)} %param.29) | copy-start | bytes 12582916
  481.0 15.0 %copy-start.54 = (f32[2,512,1024]{2,1,0:T(8,128)S(1)}, f32[2,512,1024]{2,1,0:T(8,128)}, u32[]{:S(2)}) copy-start(f32[2,512,1024]{2,1,0:T(8,128)} %fusion.44) | copy-start | bytes 12582916
  496.0 11.2 %copy-start.24 = (bf16[16,2,48,1024]{3,2,0,1:T(8,128)(2,1)S(1)}, bf16[16,2,48,1024]{3,2,0,1:T(8,128)(2,1)}, u32[]{:S(2)}) copy-start(bf16[16,2,48,1024]{3,2,0,1:T(8,128)(2,1)} %copy.89) | copy-start | bytes 9437188
  521.1 26.3 %collective-permute-start.11 = (bf16[512,1024]{1,0:T(8,128)(2,1)}, bf16[512,1024]{1,0:T(8,128)(2,1)}, u32[]{:S(2)}, u32[]{:S(2)}) collective-permute-start(bf16[512,1024]{1,0:T(8,128)(2,1)} %dynamic-slice_convert_fusion.1), channel_id=1, source_target_pairs={{0,1},{1,0},{2,3},{3,2},{4,5},{5,4},{6,7},{7,6},{8,9},{9,8},{10,11... | collective-permute-start | bytes 3145736 | tf_op jit(solution)/shard_map/ppermute | solution.py:40
  530.9 16.6 %copy-start.39 = (f32[1024]{0:T(1024)S(1)}, f32[1024]{0:T(1024)}, u32[]{:S(2)}) copy-start(f32[1024]{0:T(1024)} %param.26) | copy-start | bytes 12292
  530.9 202.8 %reduce-scatter.4.cloned.1.call-start = ((), (), s32[]{:S(2)}) async-start(), calls=%async_computation.7 | async-start | bytes 3620864 | tf_op jit(solution)/shard_map/reduce_scatter | solution.py:368
  530.9 4.4 copy-start.2
  534.6 33.8 %copy-start.17 = (f32[1024,1024]{1,0:T(8,128)S(1)}, f32[1024,1024]{1,0:T(8,128)}, u32[]{:S(2)}) copy-start(f32[1024,1024]{1,0:T(8,128)} %copy-done.16) | copy-start | bytes 12582916
  534.6 33.8 %collective-permute-start.9 = (bf16[512,1024]{1,0:T(8,128)(2,1)S(1)}, bf16[512,1024]{1,0:T(8,128)(2,1)S(1)}, u32[]{:S(2)}, u32[]{:S(2)}) collective-permute-start(bf16[512,1024]{1,0:T(8,128)(2,1)S(1)} %dynamic-slice_convert_fusion.2), channel_id=1, source_target_pairs={{0,1},{1,0},{2,3},{3,2},{4,5},{5,4},{6,7},{7,6},{8,9},{9,8},{10,11... | collective-permute-start | bytes 3145736 | tf_op jit(solution)/shard_map/ppermute | solution.py:40
  550.5 21.9 %copy-start.11 = (bf16[512,1024]{1,0:T(8,128)(2,1)S(1)}, bf16[512,1024]{1,0:T(8,128)(2,1)}, u32[]{:S(2)}) copy-start(bf16[512,1024]{1,0:T(8,128)(2,1)} %param.18) | copy-start | bytes 3145732
  572.4 24.4 %copy-start.6 = (f32[512,1024]{1,0:T(8,128)}, f32[512,1024]{1,0:T(8,128)S(1)}, u32[]{:S(2)}) copy-start(f32[512,1024]{1,0:T(8,128)S(1)} %get-tuple-element.87) | copy-start | bytes 6291460
  572.7 23.9 %collective-permute-start.12 = (bf16[512,1024]{1,0:T(8,128)(2,1)S(1)}, bf16[512,1024]{1,0:T(8,128)(2,1)S(1)}, u32[]{:S(2)}, u32[]{:S(2)}) collective-permute-start(bf16[512,1024]{1,0:T(8,128)(2,1)S(1)} %fusion.62), channel_id=1, source_target_pairs={{0,1},{1,0},{2,3},{3,2},{4,5},{5,4},{6,7},{7,6},{8,9},{9,8},{10,11... | collective-permute-start | bytes 3145736 | tf_op jit(solution)/shard_map/ppermute | solution.py:40
  596.8 3.2 copy-start.35
  627.9 5.0 copy-start.42
  627.9 5.0 copy-start.44
  627.9 5.0 copy-start.48
  627.9 5.0 copy-start.53
  629.0 23.4 %collective-permute-start.13 = (bf16[512,1024]{1,0:T(8,128)(2,1)}, bf16[512,1024]{1,0:T(8,128)(2,1)}, u32[]{:S(2)}, u32[]{:S(2)}) collective-permute-start(bf16[512,1024]{1,0:T(8,128)(2,1)} %dynamic-slice_convert_fusion), channel_id=1, source_target_pairs={{0,1},{1,0},{2,3},{3,2},{4,5},{5,4},{6,7},{7,6},{8,9},{9,8},{10,11... | collective-permute-start | bytes 3145736 | tf_op jit(solution)/shard_map/ppermute | solution.py:40
  632.9 19.6 %copy-start.5 = (bf16[512,1024]{1,0:T(8,128)(2,1)S(1)}, bf16[512,1024]{1,0:T(8,128)(2,1)}, u32[]{:S(2)}) copy-start(bf16[512,1024]{1,0:T(8,128)(2,1)} %param.17) | copy-start | bytes 3145732
  632.9 19.5 %copy-start.14 = (f32[1024,1024]{1,0:T(8,128)S(1)}, f32[1024,1024]{1,0:T(8,128)}, u32[]{:S(2)}) copy-start(f32[1024,1024]{1,0:T(8,128)} %copy-done.13) | copy-start | bytes 12582916
  656.5 7.1 copy-start.21
  663.4 151.7 %reduce-scatter.6.cloned.1.call-start = ((), (), s32[]{:S(2)}) async-start(), calls=%async_computation.8 | async-start | bytes 5570560 | tf_op jit(solution)/shard_map/reduce_scatter | solution.py:368
  663.6 10.0 %copy-start.32 = (bf16[1024,512]{1,0:T(8,128)(2,1)S(1)}, bf16[1024,512]{1,0:T(8,128)(2,1)}, u32[]{:S(2)}) copy-start(bf16[1024,512]{1,0:T(8,128)(2,1)} %get-tuple-element.18.out_ref) | copy-start | bytes 3145732
  663.6 10.0 %copy-start.34 = (bf16[512,1024]{1,0:T(8,128)(2,1)S(1)}, bf16[512,1024]{1,0:T(8,128)(2,1)}, u32[]{:S(2)}) copy-start(bf16[512,1024]{1,0:T(8,128)(2,1)} %copy-done.33) | copy-start | bytes 3145732
  663.6 10.0 %copy-start.36 = (bf16[512,1024]{1,0:T(8,128)(2,1)S(1)}, bf16[512,1024]{1,0:T(8,128)(2,1)}, u32[]{:S(2)}) copy-start(bf16[512,1024]{1,0:T(8,128)(2,1)} %copy-done.35) | copy-start | bytes 3145732
  677.9 12.6 %copy-start.55 = (bf16[1536,1024]{1,0:T(8,128)(2,1)S(1)}, bf16[1536,1024]{1,0:T(8,128)(2,1)}, u32[]{:S(2)}) copy-start(bf16[1536,1024]{1,0:T(8,128)(2,1)} %get-tuple-element.103) | copy-start | bytes 9437188
  690.4 13.3 %copy-start.15 = (f32[1024,1024]{1,0:T(8,128)S(1)}, f32[1024,1024]{1,0:T(8,128)}, u32[]{:S(2)}) copy-start(f32[1024,1024]{1,0:T(8,128)} %copy-done.13) | copy-start | bytes 12582916
  703.7 5.9 copy-start.12
  707.2 6.4 copy-start.37
  708.2 5.4 collective-permute-start.16
  734.6 4.8 collective-permute-start.14
  815.1 21.0 %collective-permute-start.15 = (bf16[160,1024]{1,0:T(8,128)(2,1)}, bf16[160,1024]{1,0:T(8,128)(2,1)S(1)}, u32[]{:S(2)}, u32[]{:S(2)}) collective-permute-start(bf16[160,1024]{1,0:T(8,128)(2,1)} %reduce-scatter.6.cloned.1.call-done), channel_id=1, source_target_pairs={{0,0},{1,16},{2,1},{3,17},{4,2},{5,18},{6,3},{7,19},{8,4},{9,20},{... | collective-permute-start | bytes 983048 | tf_op jit(solution)/shard_map/ppermute | solution.py:403
  (15 other events, 24.9 us)
Sparse Core Ops, SparseCore 0:
  531.0 72.1 reduce-scatter.7
  663.5 70.1 reduce-scatter.3
  737.5 77.4 reduce-scatter.5

commit v2 on v1

--- a/solution.py
+++ b/solution.py
@@ -49,12 +49,25 @@
     return lax.dynamic_slice_in_dim(value, start, count, axis)
 
 
-def fetch(payload, core):
+bar = lax.optimization_barrier
+
+
+def fetch(payload, core, after):
     half = payload.shape[0] // 2
-    got = swap(rows_of(payload, core * half, half))
+    part, after = bar((rows_of(payload, core * half, half), after))
+    got = swap(part)
     other = core_swap(got)
     first = core == 0
-    return jnp.concatenate([jnp.where(first, got, other), jnp.where(first, other, got)], 0)
+    whole = jnp.concatenate([jnp.where(first, got, other), jnp.where(first, other, got)], 0)
+    return whole, got, after
+
+
+def core_sum(blocks):
+    core = lax.axis_index("ep") % 2
+    blocks = blocks.reshape((-1, 2) + blocks.shape[1:])
+    keep = lax.dynamic_index_in_dim(blocks, core, 1, keepdims=False)
+    send = lax.dynamic_index_in_dim(blocks, 1 - core, 1, keepdims=False)
+    return keep.astype(F32) + core_swap(send).astype(F32)
 
 
 def ordered(own, other, side, axis=0):
@@ -173,7 +186,7 @@
     return [high, mid, rest - mid]
 
 
-def body(
+def layer(
     inputs,
     grad_output,
     expert_choice,
@@ -211,24 +224,35 @@
         ]
         return jnp.concatenate(parts, 2).reshape(half, 3 * half)
 
+    chosen = expert_choice[:, 0]
+    onehot = (chosen[:, None] == jnp.arange(experts, dtype=jnp.int32)[None, :]).astype(jnp.int32)
+    own_place = chosen * room + jnp.sum(onehot * jnp.cumsum(onehot, axis=0), axis=1) - 1
+    slots = experts * room
+    number = jnp.arange(slots, dtype=jnp.int32)
+
     inputs_other = swap(inputs)
-    qkv_other = fetch(pair_columns(1 - side), core)
-    grad_other = swap(grad_output)
-    choice_other = swap(expert_choice)
-    output_other = fetch(w_output, core)
-    up_other = fetch(rows_of(w_up, (1 - side) * hidden_half, hidden_half, 1), core)
+    place_other = swap(own_place)
+    qkv_other, qkv_got, grad_output = fetch(pair_columns(1 - side), core, grad_output)
+
+    def exchange(rows):
+        return lax.all_to_all(
+            rows.reshape(owners, -1, width), "ep", split_axis=0, concat_axis=0, tiled=True
+        )
+
+    own_hit = (number[:, None] == own_place[None, :]).astype(BF)
+    grad_arrived = exchange(matmul(own_hit, grad_output).astype(BF))
+
+    output_other, output_got, qkv_got = fetch(w_output, core, qkv_got)
+    up_other, up_got, output_got = fetch(
+        rows_of(w_up, (1 - side) * hidden_half, hidden_half, 1), core, output_got
+    )
 
     source = ordered(inputs, inputs_other, side).astype(F32)
     qkv_w = ordered(pair_columns(side), qkv_other, side)
     up_w = ordered(rows_of(w_up, side * hidden_half, hidden_half, 1), up_other, side)
-    upstream = ordered(grad_output, grad_other, side)
-    chosen = ordered(expert_choice, choice_other, side)[:, 0]
-
-    onehot = (chosen[:, None] == jnp.arange(experts, dtype=jnp.int32)[None, :]).astype(jnp.int32)
-    running = jnp.cumsum(onehot.reshape(2, tokens, experts), axis=1).reshape(2 * tokens, experts)
-    place = chosen * room + jnp.sum(onehot * running, axis=1) - 1
-    slots = experts * room
-    hit = jnp.arange(slots, dtype=jnp.int32)[None, :, None] == place.reshape(2, 1, tokens)
+    place = ordered(own_place, place_other, side)
+    onehot = ((place // room)[:, None] == jnp.arange(experts, dtype=jnp.int32)[None, :])
+    hit = number[None, :, None] == place.reshape(2, 1, tokens)
     placing = hit.astype(BF)
 
     def dispatch(rows):
@@ -245,11 +269,6 @@
             preferred_element_type=F32,
         ).reshape(2 * tokens, width)
 
-    def exchange(rows):
-        return lax.all_to_all(
-            rows.reshape(owners, 2 * room, width), "ep", split_axis=0, concat_axis=0, tiled=True
-        )
-
     pad_row = jnp.arange(room, dtype=jnp.int32)[None, None, :, None] - capacity
 
     def with_scalars(rows, scalars):
@@ -268,12 +287,18 @@
     def to_owner(rows):
         return rows.reshape(2, owners, room, -1).transpose(1, 0, 2, 3)
 
-    grad_slots = exchange(to_owner(dispatch(upstream)).astype(BF))
-
     first = layer_norm(source, pre_gain, pre_shift).astype(BF)
     qkv = matmul(first, qkv_w).astype(BF)
     attended, lse = attend(qkv)
+    attended, up_got = bar((attended, up_got))
     attended_other = swap(attended)
+    grad_output, attended_other = bar((grad_output, attended_other))
+    grad_other = swap(grad_output)
+    grad_arrived, grad_other = bar((grad_arrived, grad_other))
+    grad_slots = ordered(
+        grad_arrived[:, None], swap(grad_arrived)[:, None], side, 1
+    )
+    upstream = ordered(grad_output, grad_other, side)
     resid = source + matmul(attended, w_output) + matmul(attended_other, output_other)
     second = layer_norm(resid, mid_gain, mid_shift).astype(BF)
     small_w = jnp.concatenate([w_router, w_mix], 1)
@@ -292,33 +317,56 @@
     )
     arrived = exchange(sent)
 
+    count = owners * 2 * room
+    grad_there = grad_slots.reshape(count, width)
     up_pre = matmul(second, up_w)
     hidden = gelu_tanh(up_pre).astype(BF)
     dense = matmul(hidden, w_down)
     up32 = upstream.astype(F32)
     d_dense = (mix[:, 0:1] * up32).astype(BF)
     d_up = jax.vjp(gelu_tanh, up_pre)[1](matmul_nt(d_dense, w_down))[0].astype(BF)
-    grad_down = matmul_tn(hidden, d_dense)
-    grad_up = matmul_tn(second, d_up)
-
-    count = owners * 2 * room
+    raw_hidden = matmul_nt(grad_there, expert_down[0])
+    mixed = mix[:, 0:1] * dense
+    mixed_theirs = swap(rows_of(mixed, (1 - side) * tokens, tokens).astype(BF))
+    arrived, dense, d_up, raw_hidden = bar((arrived, dense, d_up, raw_hidden))
+
     coef_there = scalars_of(arrived.reshape(owners, 2, room, width)).reshape(count, 1)
     gathered = arrived.reshape(count, width)
-    grad_there = grad_slots.reshape(count, width)
     expert_pre = matmul(gathered, expert_up[0])
     expert_hidden = gelu_tanh(expert_pre).astype(BF)
-    expert_out = matmul(expert_hidden, expert_down[0])
+    d_expert_pre = jax.vjp(gelu_tanh, expert_pre)[1](coef_there * raw_hidden)[0]
+    d_expert_pre = d_expert_pre.astype(BF)
+    along = jnp.sum(expert_hidden.astype(F32) * raw_hidden, axis=-1)
+    d_slots = matmul_nt(d_expert_pre, expert_up[0])
+    back_sent = with_scalars(
+        d_slots.reshape(owners, 2, room, width), along.reshape(owners, 2, room)
+    )
+    back_sent, d_expert_pre, expert_hidden, d_up, d_dense = bar(
+        (back_sent, d_expert_pre, expert_hidden, d_up, d_dense)
+    )
+    back = exchange(back_sent)
+    expert_out = matmul(expert_hidden, expert_down[0]).reshape(owners, 2, room, width)
+    out_theirs = lax.dynamic_index_in_dim(expert_out, 1 - side, 1, keepdims=False)
+    out_mine = lax.dynamic_index_in_dim(expert_out, side, 1, keepdims=False)
+    out_theirs = swap(out_theirs.astype(BF))
+    expert_out = (out_mine + out_theirs.astype(F32)).astype(BF)
     d_routed = (coef_there * grad_there.astype(F32)).astype(BF)
-    d_expert_pre = jax.vjp(gelu_tanh, expert_pre)[1](matmul_nt(d_routed, expert_down[0]))[0]
-    d_expert_pre = d_expert_pre.astype(BF)
-    along = jnp.sum(grad_there.astype(F32) * expert_out, axis=-1)
-    d_slots = matmul_nt(d_expert_pre, expert_up[0])
-    back = exchange(
-        with_scalars(d_slots.reshape(owners, 2, room, width), along.reshape(owners, 2, room))
-    )
-    out_back = exchange(expert_out.astype(BF))
-    grad_expert_down = matmul_tn(expert_hidden, d_routed)[None]
-    grad_expert_up = matmul_tn(gathered, d_expert_pre)[None]
+    grad_expert_down = matmul_tn(expert_hidden, d_routed)
+    grad_expert_up = matmul_tn(gathered, d_expert_pre)
+    d_second = matmul_nt(d_up, up_w)
+    grad_down = matmul_tn(hidden, d_dense).astype(BF)
+    grad_up = [matmul_tn(second, part).astype(BF) for part in (d_up[:, :width], d_up[:, width:])]
+    grad_ff = jnp.concatenate(
+        [
+            part.reshape(owners, -1, width)
+            for part in grad_up + [grad_down]
+        ],
+        1,
+    ).reshape(-1, width)
+    back, expert_out, grad_expert_down, grad_expert_up, d_second, grad_ff = bar(
+        (back, expert_out, grad_expert_down, grad_expert_up, d_second, grad_ff)
+    )
+    out_back = exchange(expert_out)
 
     back_rows = back.reshape(owners, 2, room, width)
     along_here = jnp.sum(
@@ -335,7 +383,7 @@
     d_small = jnp.concatenate([d_route, d_mix], 1).astype(BF)
     grad_small = matmul_tn(second, d_small)
 
-    d_second = matmul_nt(d_up, up_w) + matmul_nt(d_small, small_w) + collect(back)
+    d_second = d_second + matmul_nt(d_small, small_w) + collect(back)
     theirs = swap(rows_of(d_second, (1 - side) * tokens, tokens).astype(BF))
     d_second = rows_of(d_second, side * tokens, tokens) + theirs.astype(F32)
     d_resid_mid, grad_mid_gain, grad_mid_shift = jax.vjp(
@@ -343,82 +391,93 @@
     )[1](d_second)
     d_resid = grad_output.astype(F32) + d_resid_mid
     d_attn_own = d_resid.astype(BF)
-    d_attn = ordered(d_attn_own, swap(d_attn_own), side)
-    grad_out_w = matmul_tn(attended, d_attn)
+    d_attn_other = swap(d_attn_own)
+    d_attn = ordered(d_attn_own, d_attn_other, side)
+    grad_out_w = matmul_tn(attended, d_attn).astype(BF)
+    out_sums = core_sum(grad_out_w.reshape(owners, -1, width)).astype(BF)
+    groups = [list(range(at, owners, 2)) for at in range(2)]
+    out_rows = lax.all_to_all(out_sums, "ep", 0, 0, axis_index_groups=groups, tiled=True)
+    out_rows = jnp.sum(out_rows.astype(F32), axis=0)
     d_attended = matmul_nt(d_attn, w_output).astype(BF)
     d_qkv = attend_back(qkv, attended, lse, d_attended)
-    grad_qkv = matmul_tn(first, d_qkv)
-    d_first = matmul_nt(d_qkv, qkv_w)
-    theirs = swap(rows_of(d_first, (1 - side) * tokens, tokens).astype(BF))
-    d_first = rows_of(d_first, side * tokens, tokens) + theirs.astype(F32)
-    d_source, grad_pre_gain, grad_pre_shift = jax.vjp(
-        layer_norm, inputs.astype(F32), pre_gain, pre_shift
-    )[1](d_first)
-    grad_inputs = d_resid + d_source
-
-    mixed = mix[:, 0:1] * dense + coef * collect(out_back)
-    theirs = swap(rows_of(mixed, (1 - side) * tokens, tokens).astype(BF))
+    routed = matmul_tn(own_hit, out_back.reshape(slots, width))
     output = (
         rows_of(resid, side * tokens, tokens)
         + rows_of(mixed, side * tokens, tokens)
-        + theirs.astype(F32)
+        + mixed_theirs.astype(F32)
+        + rows_of(coef, side * tokens, tokens) * routed
     ).astype(BF)
-
-    def reduce_rows(value):
-        return lax.psum_scatter(value, "ep", scatter_dimension=0, tiled=True)
-
-    up_rows = reduce_rows(grad_up.astype(BF))
-    down_rows = reduce_rows(
-        jnp.concatenate(
-            [
-                grad_down.astype(BF).reshape(owners, -1, width),
-                grad_out_w.astype(BF).reshape(owners, -1, width),
-            ],
-            1,
-        ).reshape(-1, width)
-    )
+    d_first = matmul_nt(d_qkv, qkv_w)
+    theirs = swap(rows_of(d_first, (1 - side) * tokens, tokens).astype(BF))
+    grad_pre_gain, grad_pre_shift = jax.vjp(
+        lambda gain, shift: layer_norm(source, gain, shift), pre_gain, pre_shift
+    )[1](d_first)
+    grad_qkv = matmul_tn(first, d_qkv).astype(BF)
+    d_first = rows_of(d_first, side * tokens, tokens) + theirs.astype(F32)
+    d_source = jax.vjp(lambda v: layer_norm(v, pre_gain, pre_shift), inputs.astype(F32))[1](
+        d_first
+    )[0]
+    grad_inputs = d_resid + d_source
+
+    ff_rows = lax.psum_scatter(grad_ff, "ep", scatter_dimension=0, tiled=True)
+    mine = width // (2 * owners)
     vectors = jnp.stack([grad_pre_gain, grad_pre_shift, grad_mid_gain, grad_mid_shift], 1)
-    extra = jnp.concatenate([vectors, grad_small], 1)
-    last_rows = reduce_rows(jnp.concatenate([grad_qkv, extra], 1).astype(BF))
-    small_rows = last_rows[:, 3 * half :]
-    mine = last_rows.shape[0] // 2
+    small = jnp.concatenate([vectors, grad_small], 1)
+    count = small.shape[1]
+    spare = [piece.astype(BF) for piece in pieces(core_sum(small.reshape(owners, 2 * mine, -1)))]
+    columns = 3 * half
+    last = jnp.concatenate(
+        [core_sum(grad_qkv.reshape(owners, 2 * mine, -1)).astype(BF)]
+        + spare
+        + [jnp.zeros((owners // 2, 2 * mine, -3 * count % LANES), BF)],
+        2,
+    )
+    groups = [
+        [2 * i + s for i in range(at, owners, 2) for s in range(2)] for at in range(2)
+    ]
+    last = lax.all_to_all(
+        last.reshape(owners, mine, -1),
+        ("ep", "es"),
+        0,
+        0,
+        axis_index_groups=groups,
+        tiled=True,
+    )
+    last = jnp.sum(last.reshape(owners // 2, 2, mine, -1).astype(F32), axis=0)
+    small_out = last[0, :, columns:] + last[1, :, columns:]
+    small_out = jnp.sum(small_out[:, : 3 * count].reshape(mine, 3, count), axis=1)
+    qkv_out = last[:, :, :columns].reshape(2, mine, pairs, 3, LANES)
+    qkv_outs = [
+        qkv_out[:, :, :, at].transpose(1, 0, 2, 3).reshape(mine, 2 * half) for at in range(3)
+    ]
 
     def trade(rows):
         return rows_of(rows, side * mine, mine), swap(rows_of(rows, (1 - side) * mine, mine))
 
+    up_count = 2 * mine
+    up_rows = jnp.concatenate([ff_rows[:up_count], ff_rows[up_count : 2 * up_count]], 1)
     up_own, up_theirs = trade(up_rows)
     grad_up_out = ordered(up_own, up_theirs, side, 1).astype(F32)
-    last_own, last_theirs = trade(last_rows)
-
-    def split_qkv(rows):
-        rows = rows[:, : 3 * half].reshape(mine, pairs, 3, LANES)
-        return [rows[:, :, at].reshape(mine, half) for at in range(3)]
-
-    qkv_outs = [
-        ordered(a, b, side, 1).astype(F32)
-        for a, b in zip(split_qkv(last_own), split_qkv(last_theirs))
-    ]
-    extra_out = last_own[:, 3 * half :].astype(F32) + last_theirs[:, 3 * half :].astype(F32)
     route = [(2 * j + s, owners * s + j) for j in range(owners) for s in range(2)]
-    down_rows = lax.ppermute(down_rows, ("ep", "es"), route).astype(F32)
-    per_down = hidden_half // owners
+    down_out = lax.ppermute(ff_rows[2 * up_count :], ("ep", "es"), route).astype(F32)
+    output_out = lax.ppermute(out_rows.astype(BF), ("ep", "es"), route).astype(F32)
     return (
         output,
         grad_inputs,
-        extra_out[:, 0],
-        extra_out[:, 1],
+        small_out[:, 0],
+        small_out[:, 1],
         qkv_outs[0],
         qkv_outs[1],
         qkv_outs[2],
-        down_rows[per_down:],
-        extra_out[:, 2],
-        extra_out[:, 3],
+        output_out,
+        small_out[:, 2],
+        small_out[:, 3],
         grad_up_out,
-        down_rows[:per_down],
-        extra_out[:, 4 : 4 + experts],
-        extra_out[:, 4 + experts :],
-        grad_expert_up,
-        grad_expert_down,
+        down_out,
+        small_out[:, 4 : 4 + experts],
+        small_out[:, 4 + experts :],
+        grad_expert_up[None],
+        grad_expert_down[None],
     )
 
 
@@ -443,7 +502,7 @@
         P("ep", "es", None),
     )
     return jax.shard_map(
-        body,
+        layer,
         mesh=mesh,
         in_specs=placed,
         out_specs=(

time: 854 us -> 613 us (0.72)
  waiting for transfers between devices: 394 us -> 211 us
  blocking collectives: 74.3 us -> 0 us
  starting transfers between devices: 39.4 us -> 60.5 us
  matrix products: 176 us -> 167 us
    reduce_scatter x3 -> x1, waiting for transfers between devices: 90.7 us -> 0.01 us  [layer(): ff_rows = lax.psum_scatter(grad_ff, 'ep', scatter_dimension=0, tiled=True)]
    all_to_all x3 -> x6, waiting for transfers between devices: 118 us -> 38.7 us  [the longest x4 32.5 us: exchange(): lax.all_to_all(rows.reshape(owners, -1, width), 'ep', split_axis=0, conca...]
    all_to_all x1 -> x0, blocking collectives: 74.3 us -> none  [exchange(): lax.all_to_all(rows.reshape(owners, 2 * room, width), 'ep', split_axis=0,...]
    all_to_all x3 -> x6, starting transfers between devices: 20 us -> 44.2 us  [the longest x4 27.5 us: exchange(): lax.all_to_all(rows.reshape(owners, -1, width), 'ep', split_axis=0, conca...]
    ppermute x13 -> x14, waiting for transfers between devices: 165 us -> 153 us  [swap(): return lax.ppermute(value, 'es', [(0, 1), (1, 0)])]
    dot_general x7, matrix products: 58.3 us -> 47 us  [matmul_nt(): lax.dot_general(left, right, (((1,), (1,)), ((), ())), preferred_element_...]
    unnamed x125 -> x193, local copies, waits for them, and re-layouts: 10.8 us -> 20.6 us
    dot_general x8 -> x9, matrix products: 54.6 us -> 62.3 us  [matmul(): return jnp.dot(left, right, preferred_element_type=F32)]
  transfers between devices with their start and end apart: 23 -> 29, of which waited for: 16 -> 16; matrix products, arithmetic and copies ran while one was open for 21% -> 33% of each run, Pallas kernels for 5% -> 6%
where the time goes in v2:
time: 613 us; the launch traced here: 608 us
  waiting for transfers between devices  211 us (34%)
  matrix products  167 us (27%)
  starting transfers between devices  60.5 us (10%)
  other arithmetic  59.5 us (10%)
  local copies, waits for them, and re-layouts  56.2 us (9%)
  Pallas kernels  38.3 us (6%)
  between operations  15.7 us (3%)
    ppermute x14, waiting for transfers between devices, swap(): return lax.ppermute(value, 'es', [(0, 1), (1, 0)])  153 us
    dot_general x9, matrix products, matmul(): return jnp.dot(left, right, preferred_element_type=F32)  62.3 us
    dot_general x9, matrix products, matmul_tn(): lax.dot_general(left, right, (((0,), (0,)), ((), ())), preferred_element_...  49.8 us
    dot_general x7, matrix products, matmul_nt(): lax.dot_general(left, right, (((1,), (1,)), ((), ())), preferred_element_...  47 us
    all_to_all x4, waiting for transfers between devices, exchange(): lax.all_to_all(rows.reshape(owners, -1, width), 'ep', split_axis=0, conca...  32.5 us
    all_to_all x4, starting transfers between devices, exchange(): lax.all_to_all(rows.reshape(owners, -1, width), 'ep', split_axis=0, conca...  27.5 us
    unnamed x193, local copies, waits for them, and re-layouts  20.6 us
    pallas_call x1, Pallas kernels, attend_back(): pl.pallas_call(attend_back_kernel, grid=(pairs,), in_specs=[wide, slim, s...  19.8 us
  transfers between devices with their start and end apart: 29, of which 16 were waited for; matrix products, arithmetic and copies ran while one was open for 33% of the time, Pallas kernels for 6%

profile of v2, /device:TPU:18, one launch (start us, length us, event | category | flops | bytes accessed | tf_op | source)
XLA Modules:
  0.0 608.1 jit_solution(5887496412479396626)
XLA Ops:
  12.9 2.1 constant_dynamic-slice_fusion.7
  22.6 3.3 convolution_convert_fusion.3
  26.0 6.8 %all-to-all-start.1 = ((bf16[16,48,1024]{2,1,0:T(8,128)(2,1)}), bf16[16,48,1024]{2,1,0:T(8,128)(2,1)}, u32[]{:S(2)}, u32[]{:S(2)}) async-start(bf16[16,48,1024]{2,1,0:T(8,128)(2,1)} %bitcast.220), calls=%async_computation.1 | async-start | bytes 3145728 | tf_op jit(solution)/shard_map/all_to_all | solution.py:238
  33.5 2.8 dynamic_slice.97
  36.7 17.5 %collective-permute-done.1 = bf16[256,1536]{0,1:T(8,128)(2,1)} collective-permute-done((bf16[256,1536]{0,1:T(8,128)(2,1)}, bf16[256,1536]{0,1:T(8,128)(2,1)}, u32[]{:S(2)}, u32[]{:S(2)}) %collective-permute-start.1) | collective-permute-done | bytes 786464 | tf_op jit(solution)/shard_map/ppermute | solution.py:40
  57.2 9.6 %collective-permute-done.3 = bf16[256,1024]{1,0:T(8,128)(2,1)} collective-permute-done((bf16[256,1024]{1,0:T(8,128)(2,1)S(1)}, bf16[256,1024]{1,0:T(8,128)(2,1)}, u32[]{:S(2)}, u32[]{:S(2)}) %collective-permute-start.3) | collective-permute-done | bytes 524320 | tf_op jit(solution)/shard_map/ppermute | solution.py:40
  70.9 5.3 convolution_convert_fusion.1.qkv_ref
  76.2 18.5 %attend.1 = (bf16[1024,512]{1,0:T(8,128)(2,1)}, f32[1024,512]{1,0:T(8,128)}) custom-call(bf16[1024,1536]{1,0:T(8,128)(2,1)} %convolution_convert_fusion.1.qkv_ref), custom_call_target="tpu_custom_call" | custom-call | tf_op jit(solution)/shard_map/attend/pallas_call | solution.py:153
  97.8 2.5 fusion.114
  100.3 20.2 %collective-permute-done.5 = bf16[1024,512]{1,0:T(8,128)(2,1)S(1)} collective-permute-done((bf16[1024,512]{1,0:T(8,128)(2,1)}, bf16[1024,512]{1,0:T(8,128)(2,1)S(1)}, u32[]{:S(2)}, u32[]{:S(2)}) %collective-permute-start.5) | collective-permute-done | bytes 1048608 | tf_op jit(solution)/shard_map/ppermute | solution.py:40
  120.5 1.8 fusion.113
  129.7 1.9 fusion.43
  133.3 2.2 fusion.16
  140.0 6.7 %fusion.45 = f32[1024,2048]{1,0:T(8,128)} fusion(bf16[1024,1024]{1,0:T(8,128)(2,1)S(1)} %add_convert_fusion, bf16[512,2048]{1,0:T(8,128)(2,1)S(1)} %get-tuple-element.87, bf16[512,2048]{1,0:T(8,128)(2,1)S(1)} %get-tuple-element.86), kind=kOutput, calls=%fused_computation.77 | convolution fusion | flops 4303355904 | bytes 14680064 | tf_op jit(solution)/shard_map/dot_general | solution.py:28
  146.7 6.5 %all-to-all-start = ((bf16[16,96,1024]{2,1,0:T(8,128)(2,1)}), bf16[16,96,1024]{2,1,0:T(8,128)(2,1)}, u32[]{:S(2)}, u32[]{:S(2)}) async-start(bf16[16,96,1024]{2,1,0:T(8,128)(2,1)} %bitcast.201), calls=%async_computation | async-start | bytes 6291456 | tf_op jit(solution)/shard_map/all_to_all | solution.py:238
  153.2 1.8 broadcast_select_fusion.7
  156.0 11.4 %fusion.25 = (bf16[1024,1024]{1,0:T(8,128)(2,1)S(1)}, f32[1024,1024]{1,0:T(8,128)}, f32[1024,1024]{1,0:T(8,128)}) fusion(f32[1024]{0:T(1024)S(1)} %bitcast.242, bf16[512,1024]{1,0:T(8,128)(2,1)S(1)} %get-tuple-element.95, bf16[512,1024]{1,0:T(8,128)(2,1)S(1)} %get-tuple-element.94, bf16[2048,1024]{1,0:T(8,128)(2,1)S(1)} %copy-done.78, f32[1024,2048]{1,0:T(8,128)} %fusion.45), kind=kOutput, calls=%fused_computation.41 | convolution fusion | flops 4321181696 | bytes 25169920 | tf_op jit(solution)/shard_map/dot_general | solution.py:28
  167.5 10.6 %fusion.13 = bf16[1024,2048]{1,0:T(8,128)(2,1)} fusion(f32[1024,2048]{1,0:T(8,128)S(1)} %bitcast.251, bf16[1024,1024]{1,0:T(8,128)(2,1)S(1)} %get-tuple-element.59, bf16[2048,1024]{1,0:T(8,128)(2,1)S(1)} %copy-done.78), kind=kOutput, calls=%fused_computation.19 | convolution fusion | flops 4336910336 | bytes 18874368 | tf_op jit(solution)/shard_map/dot_general | solution.py:32
  178.1 13.7 %collective-permute-done.11 = bf16[16,48,1024]{2,1,0:T(8,128)(2,1)S(1)} collective-permute-done((bf16[16,48,1024]{2,1,0:T(8,128)(2,1)}, bf16[16,48,1024]{2,1,0:T(8,128)(2,1)S(1)}, u32[]{:S(2)}, u32[]{:S(2)}) %collective-permute-start.11) | collective-permute-done | bytes 1572896 | tf_op jit(solution)/shard_map/ppermute | solution.py:40
  196.7 9.2 %fusion.34 = f32[1536,2048]{1,0:T(8,128)} fusion(bf16[1536,1024]{1,0:T(8,128)(2,1)S(1)} %bitcast.207, bf16[1,2048,1024]{2,1,0:T(8,128)(2,1)S(1)} %copy-done.79), kind=kOutput, calls=%fused_computation.52 | convolution fusion | flops 6442450944 | bytes 19922944 | tf_op jit(solution)/shard_map/dot_general | solution.py:32
  205.9 15.5 %all-to-all-done = bf16[16,96,1024]{2,1,0:T(8,128)(2,1)} async-done(((bf16[16,96,1024]{2,1,0:T(8,128)(2,1)}), bf16[16,96,1024]{2,1,0:T(8,128)(2,1)}, u32[]{:S(2)}, u32[]{:S(2)}) %all-to-all-start) | async-done | bytes 3145760 | tf_op jit(solution)/shard_map/all_to_all | solution.py:238
  222.4 20.5 %multiply_reduce_fusion = (f32[1536]{0:T(1024)S(1)}, bf16[1536,2048]{1,0:T(8,128)(2,1)}, bf16[1536,2048]{1,0:T(8,128)(2,1)}) fusion(f32[1536,2048]{1,0:T(8,128)} %fusion.34, f32[1536]{0:T(1024)S(1)} %add.283, bf16[1536,1024]{1,0:T(8,128)(2,1)} %bitcast.28, bf16[1,1024,2048]{2,1,0:T(8,128)(2,1)} %param.32), kind=kOutput, calls=%fused_computation.9 | convolution fusion | flops 6524238336 | bytes 32518144 | tf_op jit(solution)/shard_map/dot_general | solution.py:28
  243.2 11.5 %select_convert_fusion = bf16[16,2,48,1024]{3,2,1,0:T(8,128)(2,1)} fusion(bf16[16,2,48,2048]{3,2,1,0:T(8,128)(2,1)} %bitcast.246, bf16[1,1024,2048]{2,1,0:T(8,128)(2,1)} %param.32, bf16[16,2,1024]{2,1,0:T(2,128)(2,1)S(1)} %pad.24, bf16[16,2,1024]{2,1,0:T(2,128)(2,1)S(1)} %pad.23, bf16[16,2,1024]{2,1,0:T(2,128)(2,1)S(1)} %pad.22, ...), kind=kOutput, calls=%fused_computation.27 | convolution fusion | flops 6447169536 | bytes 13828240 | tf_op jit(solution)/shard_map/dot_general | solution.py:32
  254.7 3.8 fusion.59
  258.5 3.8 fusion.56
  262.3 7.0 %convolution_convert_fusion.2 = bf16[2048,1024]{1,0:T(8,128)(2,1)} fusion(bf16[1024,1024]{1,0:T(8,128)(2,1)S(1)} %copy-done.85, f32[1024,2048]{1,0:T(8,128)S(1)} %bitcast.253), kind=kOutput, calls=%fused_computation.58 | convolution fusion | flops 4315938816 | bytes 14680064 | tf_op jit(solution)/shard_map/dot_general | solution.py:36
  269.3 6.4 %all-to-all-start.2 = ((bf16[16,96,1024]{2,1,0:T(8,128)(2,1)}), bf16[16,96,1024]{2,1,0:T(8,128)(2,1)}, u32[]{:S(2)}, u32[]{:S(2)}) async-start(bf16[16,96,1024]{2,1,0:T(8,128)(2,1)} %bitcast.209), calls=%async_computation.2 | async-start | bytes 6291456 | tf_op jit(solution)/shard_map/all_to_all | solution.py:238
  275.8 10.1 %fusion.28 = f32[16,2,48,1024]{3,2,1,0:T(8,128)S(1)} fusion(bf16[16,2,48,2048]{3,2,1,0:T(8,128)(2,1)} %bitcast.249, bf16[1,2048,1024]{2,1,0:T(8,128)(2,1)} %param.33), kind=kOutput, calls=%fused_computation.45 | convolution fusion | flops 6442450944 | bytes 16777216 | tf_op jit(solution)/shard_map/dot_general | solution.py:28
  287.5 4.3 pad_maximum_fusion
  295.9 7.2 %fusion.44 = f32[1024,1024]{1,0:T(8,128)} fusion(bf16[1024,2048]{1,0:T(8,128)(2,1)S(1)} %copy-done.83, bf16[512,2048]{1,0:T(8,128)(2,1)S(1)} %copy-done.29, bf16[512,2048]{1,0:T(8,128)(2,1)S(1)} %copy-done.27), kind=kOutput, calls=%fused_computation.76 | convolution fusion | flops 4303355904 | bytes 12582912 | tf_op jit(solution)/shard_map/dot_general | solution.py:32
  303.1 11.3 %fusion.38 = f32[2048,1024]{1,0:T(8,128)} fusion(bf16[1536,2048]{1,0:T(8,128)(2,1)} %get-tuple-element.56, bf16[1536,1024]{1,0:T(8,128)(2,1)S(1)} %bitcast.208, f32[1536]{0:T(1024)S(1)} %add.283), kind=kOutput, calls=%fused_computation.60 | convolution fusion | flops 6447169536 | bytes 17831936 | tf_op jit(solution)/shard_map/dot_general | solution.py:36
  314.4 11.0 %fusion.116 = f32[1024,2048]{1,0:T(8,128)} fusion(bf16[1536,1024]{1,0:T(8,128)(2,1)} %bitcast.28, bf16[1536,2048]{1,0:T(8,128)(2,1)S(1)} %bitcast.248), kind=kOutput, calls=%fused_computation.275 | convolution fusion | flops 6442450944 | bytes 17825792 | tf_op jit(solution)/shard_map/dot_general | solution.py:36
  325.4 1.7 fusion.40
  327.1 17.0 %all-to-all-done.2 = bf16[16,96,1024]{2,1,0:T(8,128)(2,1)} async-done(((bf16[16,96,1024]{2,1,0:T(8,128)(2,1)}), bf16[16,96,1024]{2,1,0:T(8,128)(2,1)}, u32[]{:S(2)}, u32[]{:S(2)}) %all-to-all-start.2) | async-done | bytes 3145760 | tf_op jit(solution)/shard_map/all_to_all | solution.py:238
  345.0 4.1 copy.71
  350.5 5.7 fusion.42
  357.0 1.9 copy-done.18
  358.9 4.3 bitcast_add_fusion
  364.2 23.6 %collective-permute-done.13 = bf16[512,1024]{1,0:T(8,128)(2,1)S(1)} collective-permute-done((bf16[512,1024]{1,0:T(8,128)(2,1)S(1)}, bf16[512,1024]{1,0:T(8,128)(2,1)S(1)}, u32[]{:S(2)}, u32[]{:S(2)}) %collective-permute-start.13) | collective-permute-done | bytes 1048608 | tf_op jit(solution)/shard_map/ppermute | solution.py:40
  390.9 2.5 fusion.65
  394.1 7.8 %all-to-all-start.3 = ((bf16[16,48,1024]{2,1,0:T(8,128)(2,1)}), bf16[16,48,1024]{2,1,0:T(8,128)(2,1)}, u32[]{:S(2)}, u32[]{:S(2)}) async-start(bf16[16,48,1024]{2,1,0:T(8,128)(2,1)} %fusion.40), calls=%async_computation.3 | async-start | bytes 3145728 | tf_op jit(solution)/shard_map/all_to_all | solution.py:238
  402.6 14.8 %collective-permute-done.14 = bf16[512,1024]{1,0:T(8,128)(2,1)} collective-permute-done((bf16[512,1024]{1,0:T(8,128)(2,1)}, bf16[512,1024]{1,0:T(8,128)(2,1)}, u32[]{:S(2)}, u32[]{:S(2)}) %collective-permute-start.14) | collective-permute-done | bytes 1048608 | tf_op jit(solution)/shard_map/ppermute | solution.py:40
  419.1 2.2 convolution_convert_fusion.5.grad_ref
  421.4 19.8 %attend_back.1 = bf16[1024,1536]{1,0:T(8,128)(2,1)} custom-call(bf16[1024,1536]{1,0:T(8,128)(2,1)} %convolution_convert_fusion.1.qkv_ref, bf16[1024,512]{1,0:T(8,128)(2,1)} %get-tuple-element.46.out_ref, f32[1024,512]{1,0:T(8,128)} %get-tuple-element.64.lse_ref, bf16[1024,512]{1,0:T(8,128)(2,1)} %convolution_convert_fusion.5.grad_ref), custom_call_target="tpu_custom_call" | custom-call | tf_op jit(solution)/shard_map/attend_back/pallas_call | solution.py:171
  441.3 6.0 convolution_convert_fusion
  448.6 2.3 copy-done.24
  450.9 5.6 fusion.106
  460.8 8.8 %all-to-all-start.5 = ((bf16[8,32,1024]{2,1,0:T(8,128)(2,1)}), bf16[8,32,1024]{2,1,0:T(8,128)(2,1)S(1)}, u32[]{:S(2)}, u32[]{:S(2)}) async-start(bf16[8,32,1024]{2,1,0:T(8,128)(2,1)} %fusion.69), calls=%async_computation.5 | async-start | bytes 1048576 | tf_op jit(solution)/shard_map/all_to_all | solution.py:399
  472.7 2.3 fusion.39
  475.7 3.3 concatenate.114
  479.1 6.2 %all-to-all-done.5 = bf16[8,32,1024]{2,1,0:T(8,128)(2,1)S(1)} async-done(((bf16[8,32,1024]{2,1,0:T(8,128)(2,1)}), bf16[8,32,1024]{2,1,0:T(8,128)(2,1)S(1)}, u32[]{:S(2)}, u32[]{:S(2)}) %all-to-all-start.5) | async-done | bytes 524320 | tf_op jit(solution)/shard_map/all_to_all | solution.py:399
  485.2 7.9 %all-to-all-start.4 = ((bf16[16,32,1664]{2,1,0:T(8,128)(2,1)}), bf16[16,32,1664]{2,1,0:T(8,128)(2,1)}, u32[]{:S(2)}, u32[]{:S(2)}) async-start(bf16[16,32,1664]{2,1,0:T(8,128)(2,1)} %bitcast.202), calls=%async_computation.4 | async-start | bytes 3407872 | tf_op jit(solution)/shard_map/all_to_all | solution.py:438
  493.2 2.7 dynamic-slice_convert_fusion.3
  497.4 2.7 dynamic-slice_convert_fusion.1
  500.9 35.2 %collective-permute-done.8 = bf16[512,1024]{1,0:T(8,128)(2,1)} collective-permute-done((bf16[512,1024]{1,0:T(8,128)(2,1)}, bf16[512,1024]{1,0:T(8,128)(2,1)}, u32[]{:S(2)}, u32[]{:S(2)}) %collective-permute-start.8) | collective-permute-done | bytes 1048608 | tf_op jit(solution)/shard_map/ppermute | solution.py:40
  536.1 5.2 add_convert_fusion.1
  541.3 17.0 %collective-permute-done.15 = bf16[512,1024]{1,0:T(8,128)(2,1)S(1)} collective-permute-done((bf16[512,1024]{1,0:T(8,128)(2,1)}, bf16[512,1024]{1,0:T(8,128)(2,1)S(1)}, u32[]{:S(2)}, u32[]{:S(2)}) %collective-permute-start.15) | collective-permute-done | bytes 1048608 | tf_op jit(solution)/shard_map/ppermute | solution.py:40
  559.3 3.5 fusion.107
  564.0 1.9 collective-permute-start.19
  565.9 3.6 add_add_fusion.2
  569.5 3.5 collective-permute-done.19
  573.7 1.7 convert_reduce_fusion.1
  582.2 1.9 collective-permute-start.21
  586.5 13.7 %collective-permute-done.21 = bf16[128,1024]{1,0:T(8,128)(2,1)S(1)} collective-permute-done((bf16[128,1024]{1,0:T(8,128)(2,1)S(1)}, bf16[128,1024]{1,0:T(8,128)(2,1)S(1)}, u32[]{:S(2)}, u32[]{:S(2)}) %collective-permute-start.21) | collective-permute-done | bytes 262176 | tf_op jit(solution)/shard_map/ppermute | solution.py:462
  (364 shorter events, 85.0 us)
Async XLA Ops:
  7.2 29.2 %copy-start = (bf16[512,1024]{1,0:T(8,128)(2,1)S(1)}, bf16[512,1024]{1,0:T(8,128)(2,1)}, u32[]{:S(2)}) copy-start(bf16[512,1024]{1,0:T(8,128)(2,1)} %param.25) | copy-start | bytes 3145732
  10.8 85.3 %copy-start.72 = (s32[512]{0:T(512)}, s32[512]{0:T(512)S(1)}, u32[]{:S(2)}) copy-start(s32[512]{0:T(512)S(1)} %add_add_fusion.4) | copy-start | bytes 6148
  10.8 85.3 %collective-permute-start.9 = (s32[512]{0:T(512)S(1)}, s32[512]{0:T(512)S(1)}, u32[]{:S(2)}, u32[]{:S(2)}) collective-permute-start(s32[512]{0:T(512)S(1)} %add_add_fusion.4), channel_id=1, source_target_pairs={{0,1},{1,0},{2,3},{3,2},{4,5},{5,4},{6,7},{7,6},{8,9},{9,8},{10,11... | collective-permute-start | bytes 6152 | tf_op jit(solution)/shard_map/ppermute | solution.py:40
  12.4 42.3 %collective-permute-start = (bf16[512,1024]{1,0:T(8,128)(2,1)}, bf16[512,1024]{1,0:T(8,128)(2,1)}, u32[]{:S(2)}, u32[]{:S(2)}) collective-permute-start(bf16[512,1024]{1,0:T(8,128)(2,1)} %param.17), channel_id=1, source_target_pairs={{0,1},{1,0},{2,3},{3,2},{4,5},{5,4},{6,7},{7,6},{8,9},{9,8},{10,11... | collective-permute-start | bytes 3145736 | tf_op jit(solution)/shard_map/ppermute | solution.py:40
  21.1 11.7 %copy-start.31 = (bf16[512,512]{1,0:T(8,128)(2,1)S(1)}, bf16[512,512]{1,0:T(8,128)(2,1)}, u32[]{:S(2)}) copy-start(bf16[512,512]{1,0:T(8,128)(2,1)} %get-tuple-element.105) | copy-start | bytes 1572868
  21.1 33.0 %collective-permute-start.1 = (bf16[256,1536]{0,1:T(8,128)(2,1)}, bf16[256,1536]{0,1:T(8,128)(2,1)}, u32[]{:S(2)}, u32[]{:S(2)}) collective-permute-start(bf16[256,1536]{0,1:T(8,128)(2,1)} %constant_dynamic-slice_fusion.4), channel_id=1, source_target_pairs={{0,1},{1,0},{2,3},{3,2},{4,5},{5,4},{6,7},{7,6},{8,9},{9,8},{10,11... | collective-permute-start | bytes 2359304 | tf_op jit(solution)/shard_map/ppermute | solution.py:40
  26.0 120.7 %all-to-all-start.1 = ((bf16[16,48,1024]{2,1,0:T(8,128)(2,1)}), bf16[16,48,1024]{2,1,0:T(8,128)(2,1)}, u32[]{:S(2)}, u32[]{:S(2)}) async-start(bf16[16,48,1024]{2,1,0:T(8,128)(2,1)} %bitcast.220), calls=%async_computation.1 | async-start | bytes 3145728 | tf_op jit(solution)/shard_map/all_to_all | solution.py:238
  33.5 21.2 %copy-start.9 = (bf16[512,1024]{1,0:T(8,128)(2,1)S(1)}, bf16[512,1024]{1,0:T(8,128)(2,1)}, u32[]{:S(2)}) copy-start(bf16[512,1024]{1,0:T(8,128)(2,1)} %param.17) | copy-start | bytes 3145732
  36.4 87.3 %copy-start.45 = (bf16[1024,18]{0,1:T(8,128)(2,1)}, bf16[1024,18]{0,1:T(8,128)(2,1)S(1)}, u32[]{:S(2)}) copy-start(bf16[1024,18]{0,1:T(8,128)(2,1)S(1)} %constant_dynamic-update-slice_fusion) | copy-start | bytes 110596
  54.1 12.6 %collective-permute-start.3 = (bf16[256,1024]{1,0:T(8,128)(2,1)S(1)}, bf16[256,1024]{1,0:T(8,128)(2,1)}, u32[]{:S(2)}, u32[]{:S(2)}) collective-permute-start(bf16[256,1024]{1,0:T(8,128)(2,1)S(1)} %constant_dynamic-slice_fusion.3), channel_id=1, source_target_pairs={{0,1},{1,0},{2,3},{3,2},{4,5},{5,4},{6,7},{7,6},{8,9},{9,8},{10,11... | collective-permute-start | bytes 1572872 | tf_op jit(solution)/shard_map/ppermute | solution.py:40
  54.7 12.7 %collective-permute-start.2 = (bf16[256,1536]{0,1:T(8,128)(2,1)}, bf16[256,1536]{0,1:T(8,128)(2,1)S(1)}, u32[]{:S(2)}, u32[]{:S(2)}) collective-permute-start(bf16[256,1536]{0,1:T(8,128)(2,1)} %collective-permute-done.1), channel_id=1, source_target_pairs={{0,2},{2,0},{4,6},{6,4},{8,10},{10,8},{12,14},{14,12},{16,18},{18,... | collective-permute-start | bytes 2359304 | tf_op jit(solution)/shard_map/ppermute | solution.py:45
  56.1 64.4 %copy-start.5 = (bf16[512,1024]{1,0:T(8,128)(2,1)}, bf16[512,1024]{1,0:T(8,128)(2,1)S(1)}, u32[]{:S(2)}) copy-start(bf16[512,1024]{1,0:T(8,128)(2,1)S(1)} %get-tuple-element.98) | copy-start | bytes 3145732
  56.1 64.4 %copy-start.7 = (bf16[512,1024]{1,0:T(8,128)(2,1)}, bf16[512,1024]{1,0:T(8,128)(2,1)S(1)}, u32[]{:S(2)}) copy-start(bf16[512,1024]{1,0:T(8,128)(2,1)S(1)} %get-tuple-element.99) | copy-start | bytes 3145732
  56.4 12.9 %copy-start.67 = (f32[1024]{0:T(1024)}, f32[1024]{0:T(1024)S(1)}, u32[]{:S(2)}) copy-start(f32[1024]{0:T(1024)S(1)} %broadcast_multiply_fusion.2) | copy-start | bytes 12292
  57.1 12.2 %copy-start.76 = (f32[1024]{0:T(1024)}, f32[1024]{0:T(1024)S(1)}, u32[]{:S(2)}) copy-start(f32[1024]{0:T(1024)S(1)} %add_rsqrt_fusion.1) | copy-start | bytes 12292
  66.8 27.9 %collective-permute-start.4 = (bf16[256,2048]{1,0:T(8,128)(2,1)}, bf16[256,2048]{1,0:T(8,128)(2,1)}, u32[]{:S(2)}, u32[]{:S(2)}) collective-permute-start(bf16[256,2048]{1,0:T(8,128)(2,1)} %dynamic_slice.97), channel_id=1, source_target_pairs={{0,1},{1,0},{2,3},{3,2},{4,5},{5,4},{6,7},{7,6},{8,9},{9,8},{10,11... | collective-permute-start | bytes 3145736 | tf_op jit(solution)/shard_map/ppermute | solution.py:40
  67.3 28.9 %collective-permute-start.6 = (bf16[256,1024]{1,0:T(8,128)(2,1)}, bf16[256,1024]{1,0:T(8,128)(2,1)}, u32[]{:S(2)}, u32[]{:S(2)}) collective-permute-start(bf16[256,1024]{1,0:T(8,128)(2,1)} %collective-permute-done.3), channel_id=1, source_target_pairs={{0,2},{2,0},{4,6},{6,4},{8,10},{10,8},{12,14},{14,12},{16,18},{18,... | collective-permute-start | bytes 1572872 | tf_op jit(solution)/shard_map/ppermute | solution.py:45
  94.7 25.8 %collective-permute-start.5 = (bf16[1024,512]{1,0:T(8,128)(2,1)}, bf16[1024,512]{1,0:T(8,128)(2,1)S(1)}, u32[]{:S(2)}, u32[]{:S(2)}) collective-permute-start(bf16[1024,512]{1,0:T(8,128)(2,1)} %get-tuple-element.46.out_ref), channel_id=1, source_target_pairs={{0,1},{1,0},{2,3},{3,2},{4,5},{5,4},{6,7},{7,6},{8,9},{9,8},{10,11... | collective-permute-start | bytes 3145736 | tf_op jit(solution)/shard_map/ppermute | solution.py:40
  96.2 30.5 %copy-start.64 = (s32[1024]{0:T(1024)}, s32[1024]{0:T(1024)S(1)}, u32[]{:S(2)}) copy-start(s32[1024]{0:T(1024)S(1)} %add_select_fusion) | copy-start | bytes 12292
  96.2 33.4 %copy-start.58 = (s32[2,512]{1,0:T(2,128)}, s32[2,512]{1,0:T(2,128)S(1)}, u32[]{:S(2)}) copy-start(s32[2,512]{1,0:T(2,128)S(1)} %add_bitcast_fusion.1) | copy-start | bytes 12292
  97.5 34.1 %collective-permute-start.7 = (bf16[256,2048]{1,0:T(8,128)(2,1)}, bf16[256,2048]{1,0:T(8,128)(2,1)}, u32[]{:S(2)}, u32[]{:S(2)}) collective-permute-start(bf16[256,2048]{1,0:T(8,128)(2,1)} %collective-permute-done.4), channel_id=1, source_target_pairs={{0,2},{2,0},{4,6},{6,4},{8,10},{10,8},{12,14},{14,12},{16,18},{18,... | collective-permute-start | bytes 3145736 | tf_op jit(solution)/shard_map/ppermute | solution.py:45
  125.0 28.2 %collective-permute-start.10 = (bf16[512,1024]{1,0:T(8,128)(2,1)}, bf16[512,1024]{1,0:T(8,128)(2,1)}, u32[]{:S(2)}, u32[]{:S(2)}) collective-permute-start(bf16[512,1024]{1,0:T(8,128)(2,1)} %param.18), channel_id=1, source_target_pairs={{0,1},{1,0},{2,3},{3,2},{4,5},{5,4},{6,7},{7,6},{8,9},{9,8},{10,11... | collective-permute-start | bytes 3145736 | tf_op jit(solution)/shard_map/ppermute | solution.py:40
  146.7 74.7 %all-to-all-start = ((bf16[16,96,1024]{2,1,0:T(8,128)(2,1)}), bf16[16,96,1024]{2,1,0:T(8,128)(2,1)}, u32[]{:S(2)}, u32[]{:S(2)}) async-start(bf16[16,96,1024]{2,1,0:T(8,128)(2,1)} %bitcast.201), calls=%async_computation | async-start | bytes 6291456 | tf_op jit(solution)/shard_map/all_to_all | solution.py:238
  153.2 14.2 %slice-start.2 = ((s8[8388608]{0:T(1024)(128)(4,1)}), s8[4194304]{0:T(1024)(128)(4,1)S(1)}, s32[]{:S(2)}) async-start(s8[8388608]{0:T(1024)(128)(4,1)} %bitcast.250), calls=%async_computation.10 | async-start | bytes 8388608
  155.1 12.4 %copy-start.14 = (bf16[512,1024]{1,0:T(8,128)(2,1)}, bf16[512,1024]{1,0:T(8,128)(2,1)S(1)}, u32[]{:S(2)}) copy-start(bf16[512,1024]{1,0:T(8,128)(2,1)S(1)} %get-tuple-element.94) | copy-start | bytes 3145732
  155.1 12.4 %copy-start.16 = (bf16[512,1024]{1,0:T(8,128)(2,1)}, bf16[512,1024]{1,0:T(8,128)(2,1)S(1)}, u32[]{:S(2)}) copy-start(bf16[512,1024]{1,0:T(8,128)(2,1)S(1)} %get-tuple-element.95) | copy-start | bytes 3145732
  155.1 36.7 %collective-permute-start.11 = (bf16[16,48,1024]{2,1,0:T(8,128)(2,1)}, bf16[16,48,1024]{2,1,0:T(8,128)(2,1)S(1)}, u32[]{:S(2)}, u32[]{:S(2)}) collective-permute-start(bf16[16,48,1024]{2,1,0:T(8,128)(2,1)} %all-to-all-done.1), channel_id=1, source_target_pairs={{0,1},{1,0},{2,3},{3,2},{4,5},{5,4},{6,7},{7,6},{8,9},{9,8},{10,11... | collective-permute-start | bytes 4718600 | tf_op jit(solution)/shard_map/ppermute | solution.py:40
  156.0 11.4 %slice-start.3 = ((s8[8388608]{0:T(1024)(128)(4,1)}), s8[4194304]{0:T(1024)(128)(4,1)S(1)}, s32[]{:S(2)}) async-start(s8[8388608]{0:T(1024)(128)(4,1)} %bitcast.250), calls=%async_computation.11 | async-start | bytes 8388608
  167.4 10.6 %copy-start.84 = (bf16[1024,1024]{1,0:T(8,128)(2,1)}, bf16[1024,1024]{1,0:T(8,128)(2,1)S(1)}, u32[]{:S(2)}) copy-start(bf16[1024,1024]{1,0:T(8,128)(2,1)S(1)} %get-tuple-element.59) | copy-start | bytes 6291460
  243.2 11.5 %copy-start.82 = (bf16[1024,2048]{1,0:T(8,128)(2,1)S(1)}, bf16[1024,2048]{1,0:T(8,128)(2,1)}, u32[]{:S(2)}) copy-start(bf16[1024,2048]{1,0:T(8,128)(2,1)} %fusion.13) | copy-start | bytes 12582916
  269.3 74.8 %all-to-all-start.2 = ((bf16[16,96,1024]{2,1,0:T(8,128)(2,1)}), bf16[16,96,1024]{2,1,0:T(8,128)(2,1)}, u32[]{:S(2)}, u32[]{:S(2)}) async-start(bf16[16,96,1024]{2,1,0:T(8,128)(2,1)} %bitcast.209), calls=%async_computation.2 | async-start | bytes 6291456 | tf_op jit(solution)/shard_map/all_to_all | solution.py:238
  275.7 303.9 %reduce-scatter.2.cloned.1.call-start = ((), (), s32[]{:S(2)}) async-start(), calls=%async_computation.7 | async-start | bytes 8912896 | tf_op jit(solution)/shard_map/reduce_scatter | solution.py:422
  275.8 11.1 %copy-start.19 = (bf16[2048,1024]{1,0:T(8,128)(2,1)S(1)}, bf16[2048,1024]{1,0:T(8,128)(2,1)}, u32[]{:S(2)}) copy-start(bf16[2048,1024]{1,0:T(8,128)(2,1)} %convolution_convert_fusion.2) | copy-start | bytes 12582916
  275.8 11.0 %copy-start.33 = (bf16[1024,1024]{1,0:T(8,128)(2,1)S(1)}, bf16[1024,1024]{1,0:T(8,128)(2,1)}, u32[]{:S(2)}) copy-start(bf16[1024,1024]{1,0:T(8,128)(2,1)} %fusion.56) | copy-start | bytes 6291460
  286.2 39.2 %collective-permute-start.12 = (bf16[16,48,1024]{2,1,0:T(8,128)(2,1)S(1)}, bf16[16,48,1024]{2,1,0:T(8,128)(2,1)S(1)}, u32[]{:S(2)}, u32[]{:S(2)}) collective-permute-start(bf16[16,48,1024]{2,1,0:T(8,128)(2,1)S(1)} %fusion.62), channel_id=1, source_target_pairs={{0,1},{1,0},{2,3},{3,2},{4,5},{5,4},{6,7},{7,6},{8,9},{9,8},{10,11... | collective-permute-start | bytes 4718600 | tf_op jit(solution)/shard_map/ppermute | solution.py:40
  293.2 21.2 %slice-start = ((s8[6291456]{0:T(1024)(128)(4,1)}), s8[4194304]{0:T(1024)(128)(4,1)S(1)}, s32[]{:S(2)}) async-start(s8[6291456]{0:T(1024)(128)(4,1)} %bitcast.247), calls=%async_computation.8 | async-start | bytes 8388608
  295.9 18.5 %slice-start.1 = ((s8[6291456]{0:T(1024)(128)(4,1)}), s8[2097152]{0:T(1024)(128)(4,1)S(1)}, s32[]{:S(2)}) async-start(s8[6291456]{0:T(1024)(128)(4,1)} %bitcast.247), calls=%async_computation.9 | async-start | bytes 4194304
  363.1 24.6 %copy-start.57 = (f32[1024]{0:T(1024)S(1)}, f32[1024]{0:T(1024)}, u32[]{:S(2)}) copy-start(f32[1024]{0:T(1024)} %param.26) | copy-start | bytes 12292
  363.3 24.4 %collective-permute-start.13 = (bf16[512,1024]{1,0:T(8,128)(2,1)S(1)}, bf16[512,1024]{1,0:T(8,128)(2,1)S(1)}, u32[]{:S(2)}, u32[]{:S(2)}) collective-permute-start(bf16[512,1024]{1,0:T(8,128)(2,1)S(1)} %dynamic-slice_convert_fusion.2), channel_id=1, source_target_pairs={{0,1},{1,0},{2,3},{3,2},{4,5},{5,4},{6,7},{7,6},{8,9},{9,8},{10,11... | collective-permute-start | bytes 3145736 | tf_op jit(solution)/shard_map/ppermute | solution.py:40
  393.4 23.9 %collective-permute-start.14 = (bf16[512,1024]{1,0:T(8,128)(2,1)}, bf16[512,1024]{1,0:T(8,128)(2,1)}, u32[]{:S(2)}, u32[]{:S(2)}) collective-permute-start(bf16[512,1024]{1,0:T(8,128)(2,1)} %fusion.65), channel_id=1, source_target_pairs={{0,1},{1,0},{2,3},{3,2},{4,5},{5,4},{6,7},{7,6},{8,9},{9,8},{10,11... | collective-permute-start | bytes 3145736 | tf_op jit(solution)/shard_map/ppermute | solution.py:40
  394.1 66.7 %all-to-all-start.3 = ((bf16[16,48,1024]{2,1,0:T(8,128)(2,1)}), bf16[16,48,1024]{2,1,0:T(8,128)(2,1)}, u32[]{:S(2)}, u32[]{:S(2)}) async-start(bf16[16,48,1024]{2,1,0:T(8,128)(2,1)} %fusion.40), calls=%async_computation.3 | async-start | bytes 3145728 | tf_op jit(solution)/shard_map/all_to_all | solution.py:238
  421.4 19.9 %copy-start.6 = (bf16[512,1024]{1,0:T(8,128)(2,1)S(1)}, bf16[512,1024]{1,0:T(8,128)(2,1)}, u32[]{:S(2)}) copy-start(bf16[512,1024]{1,0:T(8,128)(2,1)} %copy-done.5) | copy-start | bytes 3145732
  421.4 19.9 %copy-start.8 = (bf16[512,1024]{1,0:T(8,128)(2,1)S(1)}, bf16[512,1024]{1,0:T(8,128)(2,1)}, u32[]{:S(2)}) copy-start(bf16[512,1024]{1,0:T(8,128)(2,1)} %copy-done.7) | copy-start | bytes 3145732
  421.4 19.9 %copy-start.68 = (f32[1024]{0:T(1024)S(1)}, f32[1024]{0:T(1024)}, u32[]{:S(2)}) copy-start(f32[1024]{0:T(1024)} %copy-done.67) | copy-start | bytes 12292
  421.4 19.9 %copy-start.70 = (f32[1024]{0:T(1024)S(1)}, f32[1024]{0:T(1024)}, u32[]{:S(2)}) copy-start(f32[1024]{0:T(1024)} %param.20) | copy-start | bytes 12292
  421.4 19.9 %copy-start.77 = (f32[1024]{0:T(1024)S(1)}, f32[1024]{0:T(1024)}, u32[]{:S(2)}) copy-start(f32[1024]{0:T(1024)} %copy-done.76) | copy-start | bytes 12292
  421.4 19.9 %copy-start.81 = (f32[1024]{0:T(1024)S(1)}, f32[1024]{0:T(1024)}, u32[]{:S(2)}) copy-start(f32[1024]{0:T(1024)} %param.21) | copy-start | bytes 12292
  447.3 9.2 %copy-start.21 = (bf16[1024,1536]{1,0:T(8,128)(2,1)}, bf16[1024,1536]{1,0:T(8,128)(2,1)S(1)}, u32[]{:S(2)}) copy-start(bf16[1024,1536]{1,0:T(8,128)(2,1)S(1)} %convolution_convert_fusion) | copy-start | bytes 9437188
  448.6 7.9 %copy-start.44 = (bf16[512,1024]{1,0:T(8,128)(2,1)S(1)}, bf16[512,1024]{1,0:T(8,128)(2,1)}, u32[]{:S(2)}) copy-start(bf16[512,1024]{1,0:T(8,128)(2,1)} %copy-done.43) | copy-start | bytes 3145732
  448.6 24.1 %collective-permute-start.16 = (bf16[8,64,1536]{2,1,0:T(8,128)(2,1)}, bf16[8,64,1536]{2,1,0:T(8,128)(2,1)}, u32[]{:S(2)}, u32[]{:S(2)}) collective-permute-start(bf16[8,64,1536]{2,1,0:T(8,128)(2,1)} %dynamic-slice_bitcast_fusion), channel_id=1, source_target_pairs={{0,2},{2,0},{4,6},{6,4},{8,10},{10,8},{12,14},{14,12},{16,18},{18,... | collective-permute-start | bytes 4718600 | tf_op jit(solution)/shard_map/ppermute | solution.py:45
  457.8 2.0 collective-permute-start.18
  460.8 24.4 %all-to-all-start.5 = ((bf16[8,32,1024]{2,1,0:T(8,128)(2,1)}), bf16[8,32,1024]{2,1,0:T(8,128)(2,1)S(1)}, u32[]{:S(2)}, u32[]{:S(2)}) async-start(bf16[8,32,1024]{2,1,0:T(8,128)(2,1)} %fusion.69), calls=%async_computation.5 | async-start | bytes 1048576 | tf_op jit(solution)/shard_map/all_to_all | solution.py:399
  471.0 1.6 collective-permute-start.17
  485.2 12.1 %copy-start.30 = (bf16[8,32,1024]{2,1,0:T(8,128)(2,1)}, bf16[8,32,1024]{2,1,0:T(8,128)(2,1)S(1)}, u32[]{:S(2)}) copy-start(bf16[8,32,1024]{2,1,0:T(8,128)(2,1)S(1)} %all-to-all-done.5) | copy-start | bytes 1572868
  485.2 15.4 %copy-start.10 = (bf16[512,1024]{1,0:T(8,128)(2,1)S(1)}, bf16[512,1024]{1,0:T(8,128)(2,1)}, u32[]{:S(2)}) copy-start(bf16[512,1024]{1,0:T(8,128)(2,1)} %param.17) | copy-start | bytes 3145732
  485.2 88.5 %all-to-all-start.4 = ((bf16[16,32,1664]{2,1,0:T(8,128)(2,1)}), bf16[16,32,1664]{2,1,0:T(8,128)(2,1)}, u32[]{:S(2)}, u32[]{:S(2)}) async-start(bf16[16,32,1664]{2,1,0:T(8,128)(2,1)} %bitcast.202), calls=%async_computation.4 | async-start | bytes 3407872 | tf_op jit(solution)/shard_map/all_to_all | solution.py:438
  493.2 42.9 %copy-start.73 = (s32[512]{0:T(512)S(1)}, s32[512]{0:T(512)}, u32[]{:S(2)}) copy-start(s32[512]{0:T(512)} %copy-done.72) | copy-start | bytes 6148
  495.9 40.2 %collective-permute-start.8 = (bf16[512,1024]{1,0:T(8,128)(2,1)}, bf16[512,1024]{1,0:T(8,128)(2,1)}, u32[]{:S(2)}, u32[]{:S(2)}) collective-permute-start(bf16[512,1024]{1,0:T(8,128)(2,1)} %dynamic-slice_convert_fusion.3), channel_id=1, source_target_pairs={{0,1},{1,0},{2,3},{3,2},{4,5},{5,4},{6,7},{7,6},{8,9},{9,8},{10,11... | collective-permute-start | bytes 3145736 | tf_op jit(solution)/shard_map/ppermute | solution.py:40
  500.1 58.2 %collective-permute-start.15 = (bf16[512,1024]{1,0:T(8,128)(2,1)}, bf16[512,1024]{1,0:T(8,128)(2,1)S(1)}, u32[]{:S(2)}, u32[]{:S(2)}) collective-permute-start(bf16[512,1024]{1,0:T(8,128)(2,1)} %dynamic-slice_convert_fusion.1), channel_id=1, source_target_pairs={{0,1},{1,0},{2,3},{3,2},{4,5},{5,4},{6,7},{7,6},{8,9},{9,8},{10,11... | collective-permute-start | bytes 3145736 | tf_op jit(solution)/shard_map/ppermute | solution.py:40
  536.1 22.2 %copy-start.12 = (f32[1024,1024]{1,0:T(8,128)S(1)}, f32[1024,1024]{1,0:T(8,128)}, u32[]{:S(2)}) copy-start(f32[1024,1024]{1,0:T(8,128)} %get-tuple-element.143) | copy-start | bytes 12582916
  541.3 18.0 %copy-start.11 = (bf16[512,1024]{1,0:T(8,128)(2,1)S(1)}, bf16[512,1024]{1,0:T(8,128)(2,1)}, u32[]{:S(2)}) copy-start(bf16[512,1024]{1,0:T(8,128)(2,1)} %param.17) | copy-start | bytes 3145732
  564.0 9.1 %collective-permute-start.19 = (bf16[32,1024]{1,0:T(8,128)(2,1)S(1)}, bf16[32,1024]{1,0:T(8,128)(2,1)S(1)}, u32[]{:S(2)}, u32[]{:S(2)}) collective-permute-start(bf16[32,1024]{1,0:T(8,128)(2,1)S(1)} %reduce_sum.322), channel_id=1, source_target_pairs={{0,0},{1,16},{2,1},{3,17},{4,2},{5,18},{6,3},{7,19},{8,4},{9,20},{... | collective-permute-start | bytes 196616 | tf_op jit(solution)/shard_map/ppermute | solution.py:463
  580.6 5.0 collective-permute-start.20
  582.2 18.1 %collective-permute-start.21 = (bf16[128,1024]{1,0:T(8,128)(2,1)S(1)}, bf16[128,1024]{1,0:T(8,128)(2,1)S(1)}, u32[]{:S(2)}, u32[]{:S(2)}) collective-permute-start(bf16[128,1024]{1,0:T(8,128)(2,1)S(1)} %slice.156), channel_id=1, source_target_pairs={{0,0},{1,16},{2,1},{3,17},{4,2},{5,18},{6,3},{7,19},{8,4},{9,20},{... | collective-permute-start | bytes 786440 | tf_op jit(solution)/shard_map/ppermute | solution.py:462
  (57 other events, 189.7 us)
Sparse Core Ops, SparseCore 0:
  349.2 131.6 reduce-scatter.1

commit v3 on v2

--- a/solution.py
+++ b/solution.py
@@ -145,10 +145,9 @@
     dqkv_ref[:, 2 * LANES :] = dv_ref[...].astype(BF)
 
 
-def attend(qkv):
-    length, columns = qkv.shape
-    pairs = columns // (3 * LANES)
-    wide = pl.BlockSpec((length, 3 * LANES), lambda h: (0, h))
+def attend(qkv, first, pairs):
+    length = qkv.shape[0]
+    wide = pl.BlockSpec((length, 3 * LANES), lambda h: (0, h + first))
     slim = pl.BlockSpec((length, LANES), lambda h: (0, h))
     return pl.pallas_call(
         attend_kernel,
@@ -217,12 +216,18 @@
     pairs = half // LANES
     hidden_half = w_down.shape[0]
 
-    def pair_columns(at):
-        parts = [
-            rows_of(w, at * half, half, 1).reshape(half, pairs, 1, LANES)
-            for w in (w_query, w_key, w_value)
-        ]
-        return jnp.concatenate(parts, 2).reshape(half, 3 * half)
+    def paired(parts):
+        rows = parts[0].shape[0]
+        parts = [part.reshape(rows, pairs, 1, LANES) for part in parts]
+        return jnp.concatenate(parts, 2).reshape(rows, 3 * half)
+
+    def columns_of(rows, at):
+        return [rows_of(rows(w), at * half, half, 1) for w in (w_query, w_key, w_value)]
+
+    quarter = half // 2
+    qkv_got = [
+        swap(part) for part in columns_of(lambda w: rows_of(w, core * quarter, quarter), 1 - side)
+    ]
 
     chosen = expert_choice[:, 0]
     onehot = (chosen[:, None] == jnp.arange(experts, dtype=jnp.int32)[None, :]).astype(jnp.int32)
@@ -232,7 +237,12 @@
 
     inputs_other = swap(inputs)
     place_other = swap(own_place)
-    qkv_other, qkv_got, grad_output = fetch(pair_columns(1 - side), core, grad_output)
+    qkv_got = paired(qkv_got)
+    qkv_swapped = core_swap(qkv_got)
+    lead = core == 0
+    qkv_other = jnp.concatenate(
+        [jnp.where(lead, qkv_got, qkv_swapped), jnp.where(lead, qkv_swapped, qkv_got)], 0
+    )
 
     def exchange(rows):
         return lax.all_to_all(
@@ -242,13 +252,13 @@
     own_hit = (number[:, None] == own_place[None, :]).astype(BF)
     grad_arrived = exchange(matmul(own_hit, grad_output).astype(BF))
 
-    output_other, output_got, qkv_got = fetch(w_output, core, qkv_got)
-    up_other, up_got, output_got = fetch(
-        rows_of(w_up, (1 - side) * hidden_half, hidden_half, 1), core, output_got
+    output_other, _, inputs_other = fetch(w_output, core, inputs_other)
+    up_other, _, inputs_other = fetch(
+        rows_of(w_up, (1 - side) * hidden_half, hidden_half, 1), core, inputs_other
     )
 
     source = ordered(inputs, inputs_other, side).astype(F32)
-    qkv_w = ordered(pair_columns(side), qkv_other, side)
+    qkv_w = ordered(paired(columns_of(lambda w: w, side)), qkv_other, side)
     up_w = ordered(rows_of(w_up, side * hidden_half, hidden_half, 1), up_other, side)
     place = ordered(own_place, place_other, side)
     onehot = ((place // room)[:, None] == jnp.arange(experts, dtype=jnp.int32)[None, :])
@@ -289,17 +299,22 @@
 
     first = layer_norm(source, pre_gain, pre_shift).astype(BF)
     qkv = matmul(first, qkv_w).astype(BF)
-    attended, lse = attend(qkv)
-    attended, up_got = bar((attended, up_got))
-    attended_other = swap(attended)
-    grad_output, attended_other = bar((grad_output, attended_other))
+    attended_a, lse_a = attend(qkv, 0, pairs // 2)
+    other_a = swap(attended_a)
+    attended_b, lse_b = attend(qkv, pairs // 2, pairs - pairs // 2)
+    other_b = swap(attended_b)
+    attended = jnp.concatenate([attended_a, attended_b], 1)
+    lse = jnp.concatenate([lse_a, lse_b], 1)
+    grad_output, other_b = bar((grad_output, other_b))
     grad_other = swap(grad_output)
     grad_arrived, grad_other = bar((grad_arrived, grad_other))
     grad_slots = ordered(
         grad_arrived[:, None], swap(grad_arrived)[:, None], side, 1
     )
     upstream = ordered(grad_output, grad_other, side)
-    resid = source + matmul(attended, w_output) + matmul(attended_other, output_other)
+    early = attended_a.shape[1]
+    resid = source + matmul(attended, w_output) + matmul(other_a, output_other[:early])
+    resid = resid + matmul(other_b, output_other[early:])
     second = layer_norm(resid, mid_gain, mid_shift).astype(BF)
     small_w = jnp.concatenate([w_router, w_mix], 1)
     logits = matmul(second, small_w)

time: 613 us -> 603 us (0.984)
  waiting for transfers between devices: 211 us -> 196 us
  starting transfers between devices: 60.5 us -> 67.9 us
    ppermute x14 -> x17, starting transfers between devices: 11.9 us -> 19.4 us  [swap(): return lax.ppermute(value, 'es', [(0, 1), (1, 0)])]
    ppermute x14 -> x17, waiting for transfers between devices: 153 us -> 147 us  [swap(): return lax.ppermute(value, 'es', [(0, 1), (1, 0)])]
    dot_general x9 -> x10, matrix products: 62.3 us -> 56.3 us  [matmul(): return jnp.dot(left, right, preferred_element_type=F32)]
    unnamed x193 -> x200, local copies, waits for them, and re-layouts: 20.6 us -> 17.4 us
    pallas_call x1 -> x2, Pallas kernels: 18.5 us -> 20.5 us  [attend(): pl.pallas_call(attend_kernel, grid=(pairs,), in_specs=[wide], out_specs=[...]
  transfers between devices with their start and end apart: 29 -> 32, of which waited for: 16 -> 18; matrix products, arithmetic and copies ran while one was open for 33% -> 34% of each run, Pallas kernels for 6% -> 7%
where the time goes in v3:
time: 603 us; the launch traced here: 599 us
  waiting for transfers between devices  196 us (33%)
  matrix products  161 us (27%)
  starting transfers between devices  67.9 us (11%)
  other arithmetic  60.5 us (10%)
  local copies, waits for them, and re-layouts  56.9 us (9%)
  Pallas kernels  40.3 us (7%)
  between operations  15.9 us (3%)
    ppermute x17, waiting for transfers between devices, swap(): return lax.ppermute(value, 'es', [(0, 1), (1, 0)])  147 us
    dot_general x10, matrix products, matmul(): return jnp.dot(left, right, preferred_element_type=F32)  56.3 us
    dot_general x9, matrix products, matmul_tn(): lax.dot_general(left, right, (((0,), (0,)), ((), ())), preferred_element_...  50 us
    dot_general x7, matrix products, matmul_nt(): lax.dot_general(left, right, (((1,), (1,)), ((), ())), preferred_element_...  47 us
    all_to_all x4, waiting for transfers between devices, exchange(): lax.all_to_all(rows.reshape(owners, -1, width), 'ep', split_axis=0, conca...  28 us
    all_to_all x4, starting transfers between devices, exchange(): lax.all_to_all(rows.reshape(owners, -1, width), 'ep', split_axis=0, conca...  27.4 us
    pallas_call x2, Pallas kernels, attend(): pl.pallas_call(attend_kernel, grid=(pairs,), in_specs=[wide], out_specs=[...  20.5 us
    pallas_call x1, Pallas kernels, attend_back(): pl.pallas_call(attend_back_kernel, grid=(pairs,), in_specs=[wide, slim, s...  19.8 us
  transfers between devices with their start and end apart: 32, of which 18 were waited for; matrix products, arithmetic and copies ran while one was open for 34% of the time, Pallas kernels for 7%

profile of v3, /device:TPU:18, one launch (start us, length us, event | category | flops | bytes accessed | tf_op | source)
XLA Modules:
  0.0 598.7 jit_solution(14116358302145197891)
XLA Ops:
  12.4 1.8 dynamic_slice.97
  14.7 1.8 dynamic_slice.96
  18.0 1.8 dynamic_slice.95
  21.9 3.4 convolution_convert_fusion.3
  25.2 6.6 %all-to-all-start.1 = ((bf16[16,48,1024]{2,1,0:T(8,128)(2,1)}), bf16[16,48,1024]{2,1,0:T(8,128)(2,1)}, u32[]{:S(2)}, u32[]{:S(2)}) async-start(bf16[16,48,1024]{2,1,0:T(8,128)(2,1)} %bitcast.22), calls=%async_computation.1 | async-start | bytes 3145728 | tf_op jit(solution)/shard_map/all_to_all | solution.py:248
  37.0 2.8 dynamic_slice.90
  42.5 13.5 %collective-permute-done = bf16[512,1024]{1,0:T(8,128)(2,1)} collective-permute-done((bf16[512,1024]{1,0:T(8,128)(2,1)}, bf16[512,1024]{1,0:T(8,128)(2,1)}, u32[]{:S(2)}, u32[]{:S(2)}) %collective-permute-start) | collective-permute-done | bytes 1048608 | tf_op jit(solution)/shard_map/ppermute | solution.py:40
  62.4 5.3 convolution_convert_fusion.1.qkv_ref
  67.7 10.2 %attend.3 = (bf16[1024,256]{1,0:T(8,128)(2,1)}, f32[1024,256]{1,0:T(8,128)}) custom-call(bf16[1024,1536]{1,0:T(8,128)(2,1)} %convolution_convert_fusion.1.qkv_ref), custom_call_target="tpu_custom_call" | custom-call | tf_op jit(solution)/shard_map/attend/pallas_call | solution.py:152
  77.8 10.3 %attend.2 = (bf16[1024,256]{1,0:T(8,128)(2,1)}, f32[1024,256]{1,0:T(8,128)}) custom-call(bf16[1024,1536]{1,0:T(8,128)(2,1)} %convolution_convert_fusion.1.qkv_ref), custom_call_target="tpu_custom_call" | custom-call | tf_op jit(solution)/shard_map/attend/pallas_call | solution.py:152
  94.2 9.0 %collective-permute-done.8 = bf16[1024,256]{1,0:T(8,128)(2,1)S(1)} collective-permute-done((bf16[1024,256]{1,0:T(8,128)(2,1)}, bf16[1024,256]{1,0:T(8,128)(2,1)S(1)}, u32[]{:S(2)}, u32[]{:S(2)}) %collective-permute-start.8) | collective-permute-done | bytes 524320 | tf_op jit(solution)/shard_map/ppermute | solution.py:40
  104.7 9.7 %collective-permute-done.5 = bf16[1024,256]{1,0:T(8,128)(2,1)S(1)} collective-permute-done((bf16[1024,256]{1,0:T(8,128)(2,1)}, bf16[1024,256]{1,0:T(8,128)(2,1)S(1)}, u32[]{:S(2)}, u32[]{:S(2)}) %collective-permute-start.5) | collective-permute-done | bytes 524320 | tf_op jit(solution)/shard_map/ppermute | solution.py:40
  123.0 14.0 %collective-permute-done.9 = bf16[256,2048]{1,0:T(8,128)(2,1)} collective-permute-done((bf16[256,2048]{1,0:T(8,128)(2,1)}, bf16[256,2048]{1,0:T(8,128)(2,1)}, u32[]{:S(2)}, u32[]{:S(2)}) %collective-permute-start.9) | collective-permute-done | bytes 1048608 | tf_op jit(solution)/shard_map/ppermute | solution.py:40
  137.0 1.9 fusion.44
  139.1 2.2 fusion.16
  141.3 6.8 %all-to-all-start = ((bf16[16,96,1024]{2,1,0:T(8,128)(2,1)}), bf16[16,96,1024]{2,1,0:T(8,128)(2,1)}, u32[]{:S(2)}, u32[]{:S(2)}) async-start(bf16[16,96,1024]{2,1,0:T(8,128)(2,1)} %bitcast.204), calls=%async_computation | async-start | bytes 6291456 | tf_op jit(solution)/shard_map/all_to_all | solution.py:248
  148.1 8.8 %collective-permute-done.13 = bf16[512,1024]{1,0:T(8,128)(2,1)} collective-permute-done((bf16[512,1024]{1,0:T(8,128)(2,1)}, bf16[512,1024]{1,0:T(8,128)(2,1)}, u32[]{:S(2)}, u32[]{:S(2)}) %collective-permute-start.13) | collective-permute-done | bytes 1048608 | tf_op jit(solution)/shard_map/ppermute | solution.py:40
  160.1 2.4 broadcast_select_fusion.3
  163.8 4.5 fusion.46
  168.3 8.2 %fusion.25 = (bf16[1024,1024]{1,0:T(8,128)(2,1)S(1)}, f32[1024,1024]{1,0:T(8,128)}, f32[1024,1024]{1,0:T(8,128)}) fusion(f32[1024]{0:T(1024)S(1)} %bitcast.244, bf16[512,1024]{1,0:T(8,128)(2,1)S(1)} %get-tuple-element.97, bf16[512,1024]{1,0:T(8,128)(2,1)S(1)} %get-tuple-element.96, bf16[2048,1024]{1,0:T(8,128)(2,1)S(1)} %copy-done.82, ...), kind=kOutput, calls=%fused_computation.41 | convolution fusion | flops 4321181696 | bytes 25169920 | tf_op jit(solution)/shard_map/dot_general | solution.py:28
  176.5 10.6 %fusion.13 = bf16[1024,2048]{1,0:T(8,128)(2,1)} fusion(f32[1024,2048]{1,0:T(8,128)S(1)} %fusion.46, bf16[1024,1024]{1,0:T(8,128)(2,1)S(1)} %get-tuple-element.60, bf16[2048,1024]{1,0:T(8,128)(2,1)S(1)} %copy-done.82), kind=kOutput, calls=%fused_computation.19 | convolution fusion | flops 4336910336 | bytes 18874368 | tf_op jit(solution)/shard_map/dot_general | solution.py:32
  187.1 3.9 collective-permute-done.14
  195.9 9.2 %fusion.35 = f32[1536,2048]{1,0:T(8,128)} fusion(bf16[1536,1024]{1,0:T(8,128)(2,1)S(1)} %bitcast.209, bf16[1,2048,1024]{2,1,0:T(8,128)(2,1)S(1)} %copy-done.83), kind=kOutput, calls=%fused_computation.53 | convolution fusion | flops 6442450944 | bytes 19922944 | tf_op jit(solution)/shard_map/dot_general | solution.py:32
  205.1 11.2 %all-to-all-done = bf16[16,96,1024]{2,1,0:T(8,128)(2,1)} async-done(((bf16[16,96,1024]{2,1,0:T(8,128)(2,1)}), bf16[16,96,1024]{2,1,0:T(8,128)(2,1)}, u32[]{:S(2)}, u32[]{:S(2)}) %all-to-all-start) | async-done | bytes 3145760 | tf_op jit(solution)/shard_map/all_to_all | solution.py:248
  217.4 20.3 %multiply_reduce_fusion = (f32[1536]{0:T(1024)S(1)}, bf16[1536,2048]{1,0:T(8,128)(2,1)}, bf16[1536,2048]{1,0:T(8,128)(2,1)}) fusion(f32[1536,2048]{1,0:T(8,128)} %fusion.35, f32[1536]{0:T(1024)S(1)} %add.295, bf16[1536,1024]{1,0:T(8,128)(2,1)} %bitcast.28, bf16[1,1024,2048]{2,1,0:T(8,128)(2,1)} %param.32), kind=kOutput, calls=%fused_computation.9 | convolution fusion | flops 6524238336 | bytes 32518144 | tf_op jit(solution)/shard_map/dot_general | solution.py:28
  237.9 11.5 %select_convert_fusion = bf16[16,2,48,1024]{3,2,1,0:T(8,128)(2,1)} fusion(bf16[16,2,48,2048]{3,2,1,0:T(8,128)(2,1)} %bitcast.248, bf16[1,1024,2048]{2,1,0:T(8,128)(2,1)} %param.32, bf16[16,2,1024]{2,1,0:T(2,128)(2,1)S(1)} %pad.24, bf16[16,2,1024]{2,1,0:T(2,128)(2,1)S(1)} %pad.23, bf16[16,2,1024]{2,1,0:T(2,128)(2,1)S(1)} %pad.22, ...), kind=kOutput, calls=%fused_computation.27 | convolution fusion | flops 6447169536 | bytes 13828240 | tf_op jit(solution)/shard_map/dot_general | solution.py:32
  249.4 3.8 fusion.60
  253.2 3.8 fusion.57
  257.0 7.3 %convolution_convert_fusion.2 = bf16[2048,1024]{1,0:T(8,128)(2,1)} fusion(bf16[1024,1024]{1,0:T(8,128)(2,1)S(1)} %copy-done.90, f32[1024,2048]{1,0:T(8,128)S(1)} %bitcast.253), kind=kOutput, calls=%fused_computation.59 | convolution fusion | flops 4315938816 | bytes 14680064 | tf_op jit(solution)/shard_map/dot_general | solution.py:36
  264.3 6.4 %all-to-all-start.2 = ((bf16[16,96,1024]{2,1,0:T(8,128)(2,1)}), bf16[16,96,1024]{2,1,0:T(8,128)(2,1)}, u32[]{:S(2)}, u32[]{:S(2)}) async-start(bf16[16,96,1024]{2,1,0:T(8,128)(2,1)} %bitcast.211), calls=%async_computation.2 | async-start | bytes 6291456 | tf_op jit(solution)/shard_map/all_to_all | solution.py:248
  270.7 10.1 %fusion.29 = f32[16,2,48,1024]{3,2,1,0:T(8,128)S(1)} fusion(bf16[16,2,48,2048]{3,2,1,0:T(8,128)(2,1)} %bitcast.251, bf16[1,2048,1024]{2,1,0:T(8,128)(2,1)} %param.33), kind=kOutput, calls=%fused_computation.46 | convolution fusion | flops 6442450944 | bytes 16777216 | tf_op jit(solution)/shard_map/dot_general | solution.py:28
  282.7 4.3 pad_maximum_fusion
  291.1 7.2 %fusion.45 = f32[1024,1024]{1,0:T(8,128)} fusion(bf16[1024,2048]{1,0:T(8,128)(2,1)S(1)} %copy-done.88, bf16[512,2048]{1,0:T(8,128)(2,1)S(1)} %copy-done.33, bf16[512,2048]{1,0:T(8,128)(2,1)S(1)} %copy-done.31), kind=kOutput, calls=%fused_computation.77 | convolution fusion | flops 4303355904 | bytes 12582912 | tf_op jit(solution)/shard_map/dot_general | solution.py:32
  298.3 11.3 %fusion.39 = f32[2048,1024]{1,0:T(8,128)} fusion(bf16[1536,2048]{1,0:T(8,128)(2,1)} %get-tuple-element.57, bf16[1536,1024]{1,0:T(8,128)(2,1)S(1)} %bitcast.210, f32[1536]{0:T(1024)S(1)} %add.295), kind=kOutput, calls=%fused_computation.61 | convolution fusion | flops 6447169536 | bytes 17831936 | tf_op jit(solution)/shard_map/dot_general | solution.py:36
  309.6 10.9 %fusion.118 = f32[1024,2048]{1,0:T(8,128)} fusion(bf16[1536,1024]{1,0:T(8,128)(2,1)} %bitcast.28, bf16[1536,2048]{1,0:T(8,128)(2,1)S(1)} %bitcast.250), kind=kOutput, calls=%fused_computation.274 | convolution fusion | flops 6442450944 | bytes 17825792 | tf_op jit(solution)/shard_map/dot_general | solution.py:36
  322.2 16.8 %all-to-all-done.2 = bf16[16,96,1024]{2,1,0:T(8,128)(2,1)} async-done(((bf16[16,96,1024]{2,1,0:T(8,128)(2,1)}), bf16[16,96,1024]{2,1,0:T(8,128)(2,1)}, u32[]{:S(2)}, u32[]{:S(2)}) %all-to-all-start.2) | async-done | bytes 3145760 | tf_op jit(solution)/shard_map/all_to_all | solution.py:248
  339.9 4.1 copy.71
  345.5 5.7 fusion.43
  353.5 4.3 bitcast_add_fusion
  360.1 22.7 %collective-permute-done.16 = bf16[512,1024]{1,0:T(8,128)(2,1)S(1)} collective-permute-done((bf16[512,1024]{1,0:T(8,128)(2,1)S(1)}, bf16[512,1024]{1,0:T(8,128)(2,1)S(1)}, u32[]{:S(2)}, u32[]{:S(2)}) %collective-permute-start.16) | collective-permute-done | bytes 1048608 | tf_op jit(solution)/shard_map/ppermute | solution.py:40
  386.1 2.6 fusion.66
  390.1 3.1 pad_maximum_fusion.9.lse_ref
  393.2 7.7 %all-to-all-start.3 = ((bf16[16,48,1024]{2,1,0:T(8,128)(2,1)}), bf16[16,48,1024]{2,1,0:T(8,128)(2,1)}, u32[]{:S(2)}, u32[]{:S(2)}) async-start(bf16[16,48,1024]{2,1,0:T(8,128)(2,1)} %fusion.41), calls=%async_computation.3 | async-start | bytes 3145728 | tf_op jit(solution)/shard_map/all_to_all | solution.py:248
  401.6 11.4 %collective-permute-done.17 = bf16[512,1024]{1,0:T(8,128)(2,1)} collective-permute-done((bf16[512,1024]{1,0:T(8,128)(2,1)}, bf16[512,1024]{1,0:T(8,128)(2,1)}, u32[]{:S(2)}, u32[]{:S(2)}) %collective-permute-start.17) | collective-permute-done | bytes 1048608 | tf_op jit(solution)/shard_map/ppermute | solution.py:40
  416.0 2.3 convolution_convert_fusion.5.grad_ref
  418.3 19.8 %attend_back.1 = bf16[1024,1536]{1,0:T(8,128)(2,1)} custom-call(bf16[1024,1536]{1,0:T(8,128)(2,1)} %convolution_convert_fusion.1.qkv_ref, bf16[1024,512]{1,0:T(8,128)(2,1)} %copy-done.27, f32[1024,512]{1,0:T(8,128)} %pad_maximum_fusion.9.lse_ref, bf16[1024,512]{1,0:T(8,128)(2,1)} %convolution_convert_fusion.5.grad_ref), custom_call_target="tpu_custom_call" | custom-call | tf_op jit(solution)/shard_map/attend_back/pallas_call | solution.py:170
  438.2 6.0 %convolution_convert_fusion = bf16[1024,1536]{1,0:T(8,128)(2,1)S(1)} fusion(bf16[1024,1536]{1,0:T(8,128)(2,1)} %attend_back.1, f32[1024]{0:T(1024)S(1)} %copy-done.85, f32[1024]{0:T(1024)S(1)} %copy-done.74, f32[1024]{0:T(1024)S(1)} %copy-done.81, f32[1024]{0:T(1024)S(1)} %copy-done.72, bf16[512,1024]{1,0:T(8,128)(2,1)S(1)} %copy-done.12, ...), kind=kOutput, calls=%fused_computation.57 | convolution fusion | flops 3232235520 | bytes 8404992 | tf_op jit(solution)/shard_map/dot_general | solution.py:36
  445.6 5.6 fusion.108
  455.6 8.3 %all-to-all-start.5 = ((bf16[8,32,1024]{2,1,0:T(8,128)(2,1)}), bf16[8,32,1024]{2,1,0:T(8,128)(2,1)S(1)}, u32[]{:S(2)}, u32[]{:S(2)}) async-start(bf16[8,32,1024]{2,1,0:T(8,128)(2,1)} %fusion.67), calls=%async_computation.5 | async-start | bytes 1048576 | tf_op jit(solution)/shard_map/all_to_all | solution.py:414
  467.0 2.3 fusion.40
  470.0 3.3 concatenate.118
  473.3 2.3 all-to-all-done.5
  475.6 8.1 %all-to-all-start.4 = ((bf16[16,32,1664]{2,1,0:T(8,128)(2,1)}), bf16[16,32,1664]{2,1,0:T(8,128)(2,1)}, u32[]{:S(2)}, u32[]{:S(2)}) async-start(bf16[16,32,1664]{2,1,0:T(8,128)(2,1)} %bitcast.205), calls=%async_computation.4 | async-start | bytes 3407872 | tf_op jit(solution)/shard_map/all_to_all | solution.py:453
  483.7 2.7 dynamic-slice_convert_fusion.3
  487.9 2.7 dynamic-slice_convert_fusion.1
  491.4 35.2 %collective-permute-done.11 = bf16[512,1024]{1,0:T(8,128)(2,1)} collective-permute-done((bf16[512,1024]{1,0:T(8,128)(2,1)}, bf16[512,1024]{1,0:T(8,128)(2,1)}, u32[]{:S(2)}, u32[]{:S(2)}) %collective-permute-start.11) | collective-permute-done | bytes 1048608 | tf_op jit(solution)/shard_map/ppermute | solution.py:40
  526.6 5.2 add_convert_fusion.1
  531.9 17.0 %collective-permute-done.18 = bf16[512,1024]{1,0:T(8,128)(2,1)S(1)} collective-permute-done((bf16[512,1024]{1,0:T(8,128)(2,1)}, bf16[512,1024]{1,0:T(8,128)(2,1)S(1)}, u32[]{:S(2)}, u32[]{:S(2)}) %collective-permute-start.18) | collective-permute-done | bytes 1048608 | tf_op jit(solution)/shard_map/ppermute | solution.py:40
  549.9 3.5 fusion.109
  554.5 1.9 collective-permute-start.22
  556.5 3.6 add_add_fusion.2
  560.1 3.5 collective-permute-done.22
  572.7 1.9 collective-permute-start.24
  577.0 13.7 %collective-permute-done.24 = bf16[128,1024]{1,0:T(8,128)(2,1)S(1)} collective-permute-done((bf16[128,1024]{1,0:T(8,128)(2,1)S(1)}, bf16[128,1024]{1,0:T(8,128)(2,1)S(1)}, u32[]{:S(2)}, u32[]{:S(2)}) %collective-permute-start.24) | collective-permute-done | bytes 262176 | tf_op jit(solution)/shard_map/ppermute | solution.py:477
  (382 shorter events, 98.6 us)
Async XLA Ops:
  7.2 27.6 %copy-start = (bf16[512,1024]{1,0:T(8,128)(2,1)S(1)}, bf16[512,1024]{1,0:T(8,128)(2,1)}, u32[]{:S(2)}) copy-start(bf16[512,1024]{1,0:T(8,128)(2,1)} %param.25) | copy-start | bytes 3145732
  10.8 29.0 %copy-start.76 = (s32[512]{0:T(512)}, s32[512]{0:T(512)S(1)}, u32[]{:S(2)}) copy-start(s32[512]{0:T(512)S(1)} %add_add_fusion.4) | copy-start | bytes 6148
  10.8 29.0 %collective-permute-start.12 = (s32[512]{0:T(512)S(1)}, s32[512]{0:T(512)S(1)}, u32[]{:S(2)}, u32[]{:S(2)}) collective-permute-start(s32[512]{0:T(512)S(1)} %add_add_fusion.4), channel_id=1, source_target_pairs={{0,1},{1,0},{2,3},{3,2},{4,5},{5,4},{6,7},{7,6},{8,9},{9,8},{10,11... | collective-permute-start | bytes 6152 | tf_op jit(solution)/shard_map/ppermute | solution.py:40
  14.2 25.7 %collective-permute-start.3 = (bf16[256,512]{1,0:T(8,128)(2,1)}, bf16[256,512]{1,0:T(8,128)(2,1)}, u32[]{:S(2)}, u32[]{:S(2)}) collective-permute-start(bf16[256,512]{1,0:T(8,128)(2,1)} %dynamic_slice.97), channel_id=1, source_target_pairs={{0,1},{1,0},{2,3},{3,2},{4,5},{5,4},{6,7},{7,6},{8,9},{9,8},{10,11... | collective-permute-start | bytes 786440 | tf_op jit(solution)/shard_map/ppermute | solution.py:40
  16.5 24.5 %collective-permute-start.2 = (bf16[256,512]{1,0:T(8,128)(2,1)}, bf16[256,512]{1,0:T(8,128)(2,1)S(1)}, u32[]{:S(2)}, u32[]{:S(2)}) collective-permute-start(bf16[256,512]{1,0:T(8,128)(2,1)} %dynamic_slice.96), channel_id=1, source_target_pairs={{0,1},{1,0},{2,3},{3,2},{4,5},{5,4},{6,7},{7,6},{8,9},{9,8},{10,11... | collective-permute-start | bytes 786440 | tf_op jit(solution)/shard_map/ppermute | solution.py:40
  19.9 12.0 %copy-start.47 = (bf16[512,1024]{1,0:T(8,128)(2,1)S(1)}, bf16[512,1024]{1,0:T(8,128)(2,1)}, u32[]{:S(2)}) copy-start(bf16[512,1024]{1,0:T(8,128)(2,1)} %param.22) | copy-start | bytes 3145732
  19.9 21.3 %collective-permute-start.1 = (bf16[256,512]{1,0:T(8,128)(2,1)}, bf16[256,512]{1,0:T(8,128)(2,1)}, u32[]{:S(2)}, u32[]{:S(2)}) collective-permute-start(bf16[256,512]{1,0:T(8,128)(2,1)} %dynamic_slice.95), channel_id=1, source_target_pairs={{0,1},{1,0},{2,3},{3,2},{4,5},{5,4},{6,7},{7,6},{8,9},{9,8},{10,11... | collective-permute-start | bytes 786440 | tf_op jit(solution)/shard_map/ppermute | solution.py:40
  20.4 35.6 %collective-permute-start = (bf16[512,1024]{1,0:T(8,128)(2,1)}, bf16[512,1024]{1,0:T(8,128)(2,1)}, u32[]{:S(2)}, u32[]{:S(2)}) collective-permute-start(bf16[512,1024]{1,0:T(8,128)(2,1)} %param.17), channel_id=1, source_target_pairs={{0,1},{1,0},{2,3},{3,2},{4,5},{5,4},{6,7},{7,6},{8,9},{9,8},{10,11... | collective-permute-start | bytes 3145736 | tf_op jit(solution)/shard_map/ppermute | solution.py:40
  25.2 8.8 %copy-start.70 = (bf16[1024,16]{0,1:T(8,128)(2,1)S(1)}, bf16[1024,16]{0,1:T(8,128)(2,1)}, u32[]{:S(2)}) copy-start(bf16[1024,16]{0,1:T(8,128)(2,1)} %param.30) | copy-start | bytes 98308
  25.2 116.1 %all-to-all-start.1 = ((bf16[16,48,1024]{2,1,0:T(8,128)(2,1)}), bf16[16,48,1024]{2,1,0:T(8,128)(2,1)}, u32[]{:S(2)}, u32[]{:S(2)}) async-start(bf16[16,48,1024]{2,1,0:T(8,128)(2,1)} %bitcast.22), calls=%async_computation.1 | async-start | bytes 3145728 | tf_op jit(solution)/shard_map/all_to_all | solution.py:248
  34.8 83.9 %copy-start.49 = (bf16[1024,18]{0,1:T(8,128)(2,1)}, bf16[1024,18]{0,1:T(8,128)(2,1)S(1)}, u32[]{:S(2)}) copy-start(bf16[1024,18]{0,1:T(8,128)(2,1)S(1)} %constant_dynamic-update-slice_fusion.2) | copy-start | bytes 110596
  37.0 19.5 %copy-start.5 = (bf16[512,1024]{1,0:T(8,128)(2,1)S(1)}, bf16[512,1024]{1,0:T(8,128)(2,1)}, u32[]{:S(2)}) copy-start(bf16[512,1024]{1,0:T(8,128)(2,1)} %param.17) | copy-start | bytes 3145732
  39.8 80.1 %copy-start.68 = (s32[1024]{0:T(1024)}, s32[1024]{0:T(1024)S(1)}, u32[]{:S(2)}) copy-start(s32[1024]{0:T(1024)S(1)} %add_select_fusion) | copy-start | bytes 12292
  39.9 97.1 %copy-start.62 = (s32[2,512]{1,0:T(2,128)}, s32[2,512]{1,0:T(2,128)S(1)}, u32[]{:S(2)}) copy-start(s32[2,512]{1,0:T(2,128)S(1)} %add_bitcast_fusion.1) | copy-start | bytes 12292
  42.3 16.7 %collective-permute-start.4 = (bf16[256,1536]{0,1:T(8,128)(2,1)S(1)}, bf16[256,1536]{0,1:T(8,128)(2,1)S(1)}, u32[]{:S(2)}, u32[]{:S(2)}) collective-permute-start(bf16[256,1536]{0,1:T(8,128)(2,1)S(1)} %bitcast.214), channel_id=1, source_target_pairs={{0,2},{2,0},{4,6},{6,4},{8,10},{10,8},{12,14},{14,12},{16,18},{18,... | collective-permute-start | bytes 2359304 | tf_op jit(solution)/shard_map/ppermute | solution.py:45
  56.0 34.2 %collective-permute-start.6 = (bf16[256,1024]{1,0:T(8,128)(2,1)}, bf16[256,1024]{1,0:T(8,128)(2,1)}, u32[]{:S(2)}, u32[]{:S(2)}) collective-permute-start(bf16[256,1024]{1,0:T(8,128)(2,1)} %constant_dynamic-slice_fusion.6), channel_id=1, source_target_pairs={{0,1},{1,0},{2,3},{3,2},{4,5},{5,4},{6,7},{7,6},{8,9},{9,8},{10,11... | collective-permute-start | bytes 1572872 | tf_op jit(solution)/shard_map/ppermute | solution.py:40
  57.9 58.3 %copy-start.8 = (bf16[512,1024]{1,0:T(8,128)(2,1)}, bf16[512,1024]{1,0:T(8,128)(2,1)S(1)}, u32[]{:S(2)}) copy-start(bf16[512,1024]{1,0:T(8,128)(2,1)S(1)} %get-tuple-element.100) | copy-start | bytes 3145732
  77.8 15.1 %copy-start.48 = (bf16[1024,256]{1,0:T(8,128)(2,1)S(1)}, bf16[1024,256]{1,0:T(8,128)(2,1)}, u32[]{:S(2)}) copy-start(bf16[1024,256]{1,0:T(8,128)(2,1)} %get-tuple-element.46) | copy-start | bytes 1572868
  88.2 15.0 %collective-permute-start.8 = (bf16[1024,256]{1,0:T(8,128)(2,1)}, bf16[1024,256]{1,0:T(8,128)(2,1)S(1)}, u32[]{:S(2)}, u32[]{:S(2)}) collective-permute-start(bf16[1024,256]{1,0:T(8,128)(2,1)} %get-tuple-element.46), channel_id=1, source_target_pairs={{0,1},{1,0},{2,3},{3,2},{4,5},{5,4},{6,7},{7,6},{8,9},{9,8},{10,11... | collective-permute-start | bytes 1572872 | tf_op jit(solution)/shard_map/ppermute | solution.py:40
  89.7 24.7 %collective-permute-start.5 = (bf16[1024,256]{1,0:T(8,128)(2,1)}, bf16[1024,256]{1,0:T(8,128)(2,1)S(1)}, u32[]{:S(2)}, u32[]{:S(2)}) collective-permute-start(bf16[1024,256]{1,0:T(8,128)(2,1)} %get-tuple-element.45), channel_id=1, source_target_pairs={{0,1},{1,0},{2,3},{3,2},{4,5},{5,4},{6,7},{7,6},{8,9},{9,8},{10,11... | collective-permute-start | bytes 1572872 | tf_op jit(solution)/shard_map/ppermute | solution.py:40
  90.2 24.2 %collective-permute-start.7 = (bf16[256,1024]{1,0:T(8,128)(2,1)}, bf16[256,1024]{1,0:T(8,128)(2,1)S(1)}, u32[]{:S(2)}, u32[]{:S(2)}) collective-permute-start(bf16[256,1024]{1,0:T(8,128)(2,1)} %collective-permute-done.6), channel_id=1, source_target_pairs={{0,2},{2,0},{4,6},{6,4},{8,10},{10,8},{12,14},{14,12},{16,18},{18,... | collective-permute-start | bytes 1572872 | tf_op jit(solution)/shard_map/ppermute | solution.py:45
  91.3 45.7 %collective-permute-start.9 = (bf16[256,2048]{1,0:T(8,128)(2,1)}, bf16[256,2048]{1,0:T(8,128)(2,1)}, u32[]{:S(2)}, u32[]{:S(2)}) collective-permute-start(bf16[256,2048]{1,0:T(8,128)(2,1)} %dynamic_slice.90), channel_id=1, source_target_pairs={{0,1},{1,0},{2,3},{3,2},{4,5},{5,4},{6,7},{7,6},{8,9},{9,8},{10,11... | collective-permute-start | bytes 3145736 | tf_op jit(solution)/shard_map/ppermute | solution.py:40
  94.2 22.0 %copy-start.11 = (bf16[512,1024]{1,0:T(8,128)(2,1)S(1)}, bf16[512,1024]{1,0:T(8,128)(2,1)}, u32[]{:S(2)}) copy-start(bf16[512,1024]{1,0:T(8,128)(2,1)} %copy-done.10) | copy-start | bytes 3145732
  103.2 53.7 %collective-permute-start.13 = (bf16[512,1024]{1,0:T(8,128)(2,1)}, bf16[512,1024]{1,0:T(8,128)(2,1)}, u32[]{:S(2)}, u32[]{:S(2)}) collective-permute-start(bf16[512,1024]{1,0:T(8,128)(2,1)} %param.18), channel_id=1, source_target_pairs={{0,1},{1,0},{2,3},{3,2},{4,5},{5,4},{6,7},{7,6},{8,9},{9,8},{10,11... | collective-permute-start | bytes 3145736 | tf_op jit(solution)/shard_map/ppermute | solution.py:40
  137.0 23.1 %collective-permute-start.10 = (bf16[256,2048]{1,0:T(8,128)(2,1)}, bf16[256,2048]{1,0:T(8,128)(2,1)}, u32[]{:S(2)}, u32[]{:S(2)}) collective-permute-start(bf16[256,2048]{1,0:T(8,128)(2,1)} %collective-permute-done.9), channel_id=1, source_target_pairs={{0,2},{2,0},{4,6},{6,4},{8,10},{10,8},{12,14},{14,12},{16,18},{18,... | collective-permute-start | bytes 3145736 | tf_op jit(solution)/shard_map/ppermute | solution.py:45
  141.3 75.0 %all-to-all-start = ((bf16[16,96,1024]{2,1,0:T(8,128)(2,1)}), bf16[16,96,1024]{2,1,0:T(8,128)(2,1)}, u32[]{:S(2)}, u32[]{:S(2)}) async-start(bf16[16,96,1024]{2,1,0:T(8,128)(2,1)} %bitcast.204), calls=%async_computation | async-start | bytes 6291456 | tf_op jit(solution)/shard_map/all_to_all | solution.py:248
  148.1 14.4 %copy-start.29 = (bf16[512,4096]{1,0:T(8,128)(2,1)S(1)}, bf16[512,4096]{1,0:T(8,128)(2,1)}, u32[]{:S(2)}) copy-start(bf16[512,4096]{1,0:T(8,128)(2,1)} %param.28) | copy-start | bytes 12582916
  156.9 34.1 %collective-permute-start.14 = (bf16[16,48,1024]{2,1,0:T(8,128)(2,1)}, bf16[16,48,1024]{2,1,0:T(8,128)(2,1)S(1)}, u32[]{:S(2)}, u32[]{:S(2)}) collective-permute-start(bf16[16,48,1024]{2,1,0:T(8,128)(2,1)} %all-to-all-done.1), channel_id=1, source_target_pairs={{0,1},{1,0},{2,3},{3,2},{4,5},{5,4},{6,7},{7,6},{8,9},{9,8},{10,11... | collective-permute-start | bytes 4718600 | tf_op jit(solution)/shard_map/ppermute | solution.py:40
  160.1 8.2 %copy-start.16 = (bf16[512,1024]{1,0:T(8,128)(2,1)}, bf16[512,1024]{1,0:T(8,128)(2,1)S(1)}, u32[]{:S(2)}) copy-start(bf16[512,1024]{1,0:T(8,128)(2,1)S(1)} %get-tuple-element.96) | copy-start | bytes 3145732
  168.3 8.2 %copy-start.86 = (f32[1024,2048]{1,0:T(8,128)}, f32[1024,2048]{1,0:T(8,128)S(1)}, u32[]{:S(2)}) copy-start(f32[1024,2048]{1,0:T(8,128)S(1)} %fusion.46) | copy-start | bytes 25165828
  176.5 10.6 %copy-start.89 = (bf16[1024,1024]{1,0:T(8,128)(2,1)}, bf16[1024,1024]{1,0:T(8,128)(2,1)S(1)}, u32[]{:S(2)}) copy-start(bf16[1024,1024]{1,0:T(8,128)(2,1)S(1)} %get-tuple-element.60) | copy-start | bytes 6291460
  237.9 11.5 %copy-start.87 = (bf16[1024,2048]{1,0:T(8,128)(2,1)S(1)}, bf16[1024,2048]{1,0:T(8,128)(2,1)}, u32[]{:S(2)}) copy-start(bf16[1024,2048]{1,0:T(8,128)(2,1)} %fusion.13) | copy-start | bytes 12582916
  264.3 74.8 %all-to-all-start.2 = ((bf16[16,96,1024]{2,1,0:T(8,128)(2,1)}), bf16[16,96,1024]{2,1,0:T(8,128)(2,1)}, u32[]{:S(2)}, u32[]{:S(2)}) async-start(bf16[16,96,1024]{2,1,0:T(8,128)(2,1)} %bitcast.211), calls=%async_computation.2 | async-start | bytes 6291456 | tf_op jit(solution)/shard_map/all_to_all | solution.py:248
  270.7 299.4 %reduce-scatter.2.cloned.1.call-start = ((), (), s32[]{:S(2)}) async-start(), calls=%async_computation.7 | async-start | bytes 8912896 | tf_op jit(solution)/shard_map/reduce_scatter | solution.py:437
  270.7 12.0 %copy-start.21 = (bf16[2048,1024]{1,0:T(8,128)(2,1)S(1)}, bf16[2048,1024]{1,0:T(8,128)(2,1)}, u32[]{:S(2)}) copy-start(bf16[2048,1024]{1,0:T(8,128)(2,1)} %convolution_convert_fusion.2) | copy-start | bytes 12582916
  270.7 12.0 %copy-start.36 = (bf16[1024,1024]{1,0:T(8,128)(2,1)S(1)}, bf16[1024,1024]{1,0:T(8,128)(2,1)}, u32[]{:S(2)}) copy-start(bf16[1024,1024]{1,0:T(8,128)(2,1)} %fusion.57) | copy-start | bytes 6291460
  281.1 39.4 %collective-permute-start.15 = (bf16[16,48,1024]{2,1,0:T(8,128)(2,1)S(1)}, bf16[16,48,1024]{2,1,0:T(8,128)(2,1)S(1)}, u32[]{:S(2)}, u32[]{:S(2)}) collective-permute-start(bf16[16,48,1024]{2,1,0:T(8,128)(2,1)S(1)} %fusion.63), channel_id=1, source_target_pairs={{0,1},{1,0},{2,3},{3,2},{4,5},{5,4},{6,7},{7,6},{8,9},{9,8},{10,11... | collective-permute-start | bytes 4718600 | tf_op jit(solution)/shard_map/ppermute | solution.py:40
  288.4 21.2 %slice-start = ((s8[6291456]{0:T(1024)(128)(4,1)}), s8[4194304]{0:T(1024)(128)(4,1)S(1)}, s32[]{:S(2)}) async-start(s8[6291456]{0:T(1024)(128)(4,1)} %bitcast.249), calls=%async_computation.8 | async-start | bytes 8388608
  291.1 18.5 %slice-start.1 = ((s8[6291456]{0:T(1024)(128)(4,1)}), s8[2097152]{0:T(1024)(128)(4,1)S(1)}, s32[]{:S(2)}) async-start(s8[6291456]{0:T(1024)(128)(4,1)} %bitcast.249), calls=%async_computation.9 | async-start | bytes 4194304
  357.8 25.0 %copy-start.61 = (f32[1024]{0:T(1024)S(1)}, f32[1024]{0:T(1024)}, u32[]{:S(2)}) copy-start(f32[1024]{0:T(1024)} %param.26) | copy-start | bytes 12292
  358.0 24.8 %collective-permute-start.16 = (bf16[512,1024]{1,0:T(8,128)(2,1)S(1)}, bf16[512,1024]{1,0:T(8,128)(2,1)S(1)}, u32[]{:S(2)}, u32[]{:S(2)}) collective-permute-start(bf16[512,1024]{1,0:T(8,128)(2,1)S(1)} %dynamic-slice_convert_fusion.2), channel_id=1, source_target_pairs={{0,1},{1,0},{2,3},{3,2},{4,5},{5,4},{6,7},{7,6},{8,9},{9,8},{10,11... | collective-permute-start | bytes 3145736 | tf_op jit(solution)/shard_map/ppermute | solution.py:40
  388.6 24.3 %collective-permute-start.17 = (bf16[512,1024]{1,0:T(8,128)(2,1)}, bf16[512,1024]{1,0:T(8,128)(2,1)}, u32[]{:S(2)}, u32[]{:S(2)}) collective-permute-start(bf16[512,1024]{1,0:T(8,128)(2,1)} %fusion.66), channel_id=1, source_target_pairs={{0,1},{1,0},{2,3},{3,2},{4,5},{5,4},{6,7},{7,6},{8,9},{9,8},{10,11... | collective-permute-start | bytes 3145736 | tf_op jit(solution)/shard_map/ppermute | solution.py:40
  393.2 62.3 %all-to-all-start.3 = ((bf16[16,48,1024]{2,1,0:T(8,128)(2,1)}), bf16[16,48,1024]{2,1,0:T(8,128)(2,1)}, u32[]{:S(2)}, u32[]{:S(2)}) async-start(bf16[16,48,1024]{2,1,0:T(8,128)(2,1)} %fusion.41), calls=%async_computation.3 | async-start | bytes 3145728 | tf_op jit(solution)/shard_map/all_to_all | solution.py:248
  418.2 19.9 %copy-start.9 = (bf16[512,1024]{1,0:T(8,128)(2,1)S(1)}, bf16[512,1024]{1,0:T(8,128)(2,1)}, u32[]{:S(2)}) copy-start(bf16[512,1024]{1,0:T(8,128)(2,1)} %copy-done.8) | copy-start | bytes 3145732
  418.2 19.9 %copy-start.12 = (bf16[512,1024]{1,0:T(8,128)(2,1)S(1)}, bf16[512,1024]{1,0:T(8,128)(2,1)}, u32[]{:S(2)}) copy-start(bf16[512,1024]{1,0:T(8,128)(2,1)} %copy-done.10) | copy-start | bytes 3145732
  418.2 19.9 %copy-start.72 = (f32[1024]{0:T(1024)S(1)}, f32[1024]{0:T(1024)}, u32[]{:S(2)}) copy-start(f32[1024]{0:T(1024)} %copy-done.71) | copy-start | bytes 12292
  418.2 19.9 %copy-start.74 = (f32[1024]{0:T(1024)S(1)}, f32[1024]{0:T(1024)}, u32[]{:S(2)}) copy-start(f32[1024]{0:T(1024)} %param.20) | copy-start | bytes 12292
  418.2 19.9 %copy-start.81 = (f32[1024]{0:T(1024)S(1)}, f32[1024]{0:T(1024)}, u32[]{:S(2)}) copy-start(f32[1024]{0:T(1024)} %copy-done.80) | copy-start | bytes 12292
  418.3 19.9 %copy-start.85 = (f32[1024]{0:T(1024)S(1)}, f32[1024]{0:T(1024)}, u32[]{:S(2)}) copy-start(f32[1024]{0:T(1024)} %param.21) | copy-start | bytes 12292
  445.5 21.4 %collective-permute-start.19 = (bf16[8,64,1536]{2,1,0:T(8,128)(2,1)}, bf16[8,64,1536]{2,1,0:T(8,128)(2,1)}, u32[]{:S(2)}, u32[]{:S(2)}) collective-permute-start(bf16[8,64,1536]{2,1,0:T(8,128)(2,1)} %dynamic-slice_bitcast_fusion), channel_id=1, source_target_pairs={{0,2},{2,0},{4,6},{6,4},{8,10},{10,8},{12,14},{14,12},{16,18},{18,... | collective-permute-start | bytes 4718600 | tf_op jit(solution)/shard_map/ppermute | solution.py:45
  452.5 2.1 collective-permute-start.21
  455.6 20.0 %all-to-all-start.5 = ((bf16[8,32,1024]{2,1,0:T(8,128)(2,1)}), bf16[8,32,1024]{2,1,0:T(8,128)(2,1)S(1)}, u32[]{:S(2)}, u32[]{:S(2)}) async-start(bf16[8,32,1024]{2,1,0:T(8,128)(2,1)} %fusion.67), calls=%async_computation.5 | async-start | bytes 1048576 | tf_op jit(solution)/shard_map/all_to_all | solution.py:414
  465.3 1.6 collective-permute-start.20
  475.6 12.3 %copy-start.34 = (bf16[8,32,1024]{2,1,0:T(8,128)(2,1)}, bf16[8,32,1024]{2,1,0:T(8,128)(2,1)S(1)}, u32[]{:S(2)}) copy-start(bf16[8,32,1024]{2,1,0:T(8,128)(2,1)S(1)} %all-to-all-done.5) | copy-start | bytes 1572868
  475.6 15.6 %copy-start.6 = (bf16[512,1024]{1,0:T(8,128)(2,1)S(1)}, bf16[512,1024]{1,0:T(8,128)(2,1)}, u32[]{:S(2)}) copy-start(bf16[512,1024]{1,0:T(8,128)(2,1)} %param.17) | copy-start | bytes 3145732
  475.6 88.6 %all-to-all-start.4 = ((bf16[16,32,1664]{2,1,0:T(8,128)(2,1)}), bf16[16,32,1664]{2,1,0:T(8,128)(2,1)}, u32[]{:S(2)}, u32[]{:S(2)}) async-start(bf16[16,32,1664]{2,1,0:T(8,128)(2,1)} %bitcast.205), calls=%async_computation.4 | async-start | bytes 3407872 | tf_op jit(solution)/shard_map/all_to_all | solution.py:453
  483.7 42.9 %copy-start.77 = (s32[512]{0:T(512)S(1)}, s32[512]{0:T(512)}, u32[]{:S(2)}) copy-start(s32[512]{0:T(512)} %copy-done.76) | copy-start | bytes 6148
  486.4 40.2 %collective-permute-start.11 = (bf16[512,1024]{1,0:T(8,128)(2,1)}, bf16[512,1024]{1,0:T(8,128)(2,1)}, u32[]{:S(2)}, u32[]{:S(2)}) collective-permute-start(bf16[512,1024]{1,0:T(8,128)(2,1)} %dynamic-slice_convert_fusion.3), channel_id=1, source_target_pairs={{0,1},{1,0},{2,3},{3,2},{4,5},{5,4},{6,7},{7,6},{8,9},{9,8},{10,11... | collective-permute-start | bytes 3145736 | tf_op jit(solution)/shard_map/ppermute | solution.py:40
  490.6 58.2 %collective-permute-start.18 = (bf16[512,1024]{1,0:T(8,128)(2,1)}, bf16[512,1024]{1,0:T(8,128)(2,1)S(1)}, u32[]{:S(2)}, u32[]{:S(2)}) collective-permute-start(bf16[512,1024]{1,0:T(8,128)(2,1)} %dynamic-slice_convert_fusion.1), channel_id=1, source_target_pairs={{0,1},{1,0},{2,3},{3,2},{4,5},{5,4},{6,7},{7,6},{8,9},{9,8},{10,11... | collective-permute-start | bytes 3145736 | tf_op jit(solution)/shard_map/ppermute | solution.py:40
  526.6 22.2 %copy-start.13 = (f32[1024,1024]{1,0:T(8,128)S(1)}, f32[1024,1024]{1,0:T(8,128)}, u32[]{:S(2)}) copy-start(f32[1024,1024]{1,0:T(8,128)} %get-tuple-element.137) | copy-start | bytes 12582916
  531.9 18.0 %copy-start.7 = (bf16[512,1024]{1,0:T(8,128)(2,1)S(1)}, bf16[512,1024]{1,0:T(8,128)(2,1)}, u32[]{:S(2)}) copy-start(bf16[512,1024]{1,0:T(8,128)(2,1)} %param.17) | copy-start | bytes 3145732
  554.5 9.1 %collective-permute-start.22 = (bf16[32,1024]{1,0:T(8,128)(2,1)S(1)}, bf16[32,1024]{1,0:T(8,128)(2,1)S(1)}, u32[]{:S(2)}, u32[]{:S(2)}) collective-permute-start(bf16[32,1024]{1,0:T(8,128)(2,1)S(1)} %reduce_sum.322), channel_id=1, source_target_pairs={{0,0},{1,16},{2,1},{3,17},{4,2},{5,18},{6,3},{7,19},{8,4},{9,20},{... | collective-permute-start | bytes 196616 | tf_op jit(solution)/shard_map/ppermute | solution.py:478
  571.1 5.0 collective-permute-start.23
  572.7 18.1 %collective-permute-start.24 = (bf16[128,1024]{1,0:T(8,128)(2,1)S(1)}, bf16[128,1024]{1,0:T(8,128)(2,1)S(1)}, u32[]{:S(2)}, u32[]{:S(2)}) collective-permute-start(bf16[128,1024]{1,0:T(8,128)(2,1)S(1)} %slice.156), channel_id=1, source_target_pairs={{0,0},{1,16},{2,1},{3,17},{4,2},{5,18},{6,3},{7,19},{8,4},{9,20},{... | collective-permute-start | bytes 786440 | tf_op jit(solution)/shard_map/ppermute | solution.py:477
  (63 other events, 216.4 us)
Sparse Core Ops, SparseCore 0:
  344.2 122.0 reduce-scatter.1
